TPU v7x, 256 devices: a whole 4x4x8 slice. The times are simulated.
256 devices in a mesh: island: 4 (over x_lo, core), fsdp: 64 (over x_hi, y, z).
Axes of the slice: x: 4 (x_hi: 2, x_lo: 2; x = x_hi * 2 + x_lo), y: 4, z: 8, core: 2. Of those that a mesh axis runs over, the one named last changes fastest.
Arguments:
- local_weights: bfloat16 [4, 512, 8192], P('island', 'fsdp'), may hold values from -6 to 6
- base_master: float32 [512, 8192], P('fsdp'), may hold values from -6 to 6
- momentum: float32 [512, 8192], P('fsdp'), may hold values from -4 to 4
Outputs:
- new_master: float32 [512, 8192], P('fsdp')
- new_momentum: float32 [512, 8192], P('fsdp')
- new_base: bfloat16 [512, 8192], replicated
All inputs are finite; a program needn't handle non-finite values.
Results may differ from a plain program's by a relative error of at most 0.02.
Values may be sent and summed in bfloat16 or wider, within the bound.
No kernel may reach another device: no remote copies, remote signals or barrier semaphores. Data moves between devices by JAX's collectives and lax.ppermute only.
A program may use at most 64 MiB of HBM per device.

v0:
```python
import jax
import jax.numpy as jnp
from jax import lax
from jax.sharding import PartitionSpec as P

BLOCK = 128


epsilon = 1e-06
code_limit = 31.0
momentum_decay = 0.9
outer_rate = 0.7


def copy_for_each(x, axis):
    size = lax.axis_size(axis)
    return lax.all_to_all(jnp.broadcast_to(x[None], (size, *x.shape)), axis, 0, 0, tiled=True)


def taken_together(x, axis):
    everything = copy_for_each(x, axis)
    return jnp.sum(everything.astype(jnp.float32), axis=0)


def encode(outer_grad):
    blocks = outer_grad.reshape(outer_grad.shape[0], outer_grad.shape[1] // BLOCK, BLOCK)
    largest = jnp.max(jnp.abs(blocks), axis=2)
    block_scale = (largest + epsilon) / code_limit
    code_values = (blocks / block_scale[:, :, None]).astype(jnp.bfloat16)
    return (code_values, block_scale)


def decode(code_values, block_scale, target_shape):
    decoded = code_values.astype(jnp.float32) * block_scale[:, :, None]
    return decoded.reshape(target_shape)


def outer_step(summed, base_rows, moment_rows, groups):
    averaged = summed / groups
    fresh_moment = momentum_decay * moment_rows + averaged
    fresh_master = base_rows - outer_rate * (averaged + momentum_decay * fresh_moment)
    return (fresh_master, fresh_moment)


def on_device(local_weights, base_master, momentum):
    groups = lax.axis_size("island")
    outer_grad = base_master - local_weights[0].astype(jnp.float32)
    code_values, block_scale = encode(outer_grad)
    decoded = decode(code_values, block_scale, base_master.shape)
    summed = taken_together(decoded.astype(jnp.bfloat16), "island").astype(jnp.float32)
    new_master, new_momentum = outer_step(summed, base_master, momentum, groups)
    new_base = lax.all_gather(new_master.astype(jnp.bfloat16), "fsdp", axis=0, tiled=True)
    return (new_master, new_momentum, new_base)


def solution(mesh):
    return jax.shard_map(
        on_device,
        mesh=mesh,
        in_specs=(P("island", "fsdp", None), P("fsdp", None), P("fsdp", None)),
        out_specs=(P("fsdp", None), P("fsdp", None), P()),
        check_vma=False,
    )
```

profile of v0, /device:TPU:1, one launch (start us, length us, event | category | flops | bytes accessed | tf_op | source)
XLA Modules:
  0.0 189.6 jit_solution(9935297403109657828)
XLA Ops:
  7.2 0.0 all-gather.2.cloned.1.call-start
  7.2 1.1 bitcast_reduce_fusion
  8.4 1.1 fusion.1
  9.5 13.4 %all_to_all.5 = bf16[4,8,8192]{2,1,0:T(8,128)(2,1)S(1)} all-to-all(bf16[4,8,8192]{2,1,0:T(8,128)(2,1)S(1)} %broadcast_in_dim.2), channel_id=1, replica_groups=mesh['island'=4,'fsdp'=64] {'island'}, dimensions={0} | all-to-all | bytes 1048576 | tf_op jit(solution)/shard_map/all_to_all | solution.py:17
  23.0 0.1 convert_reduce_fusion
  23.1 1.9 %fusion.2 = (bf16[8,8192]{1,0:T(8,128)(2,1)}, f32[8,8192]{1,0:T(8,128)}, f32[8,8192]{1,0:T(8,128)}) fusion(f32[8,8192]{1,0:T(8,128)} %param.4, f32[8,8192]{1,0:T(8,128)S(1)} %convert_reduce_fusion, f32[8,8192]{1,0:T(8,128)} %param.5), kind=kLoop, calls=%fused_computation.10 | loop fusion | flops 524288 | bytes 1441792 | tf_op jit(solution)/shard_map/convert_element_type | solution.py:52
  25.0 0.0 all-gather.2.cloned.1.call-update
  25.0 150.0 %all-gather.2.cloned.1.call-done = bf16[512,8192]{1,0:T(8,128)(2,1)} async-done(((bf16[8,8192]{1,0:T(8,128)(2,1)}), bf16[512,8192]{1,0:T(8,128)(2,1)}) %all-gather.2.cloned.1.call-update) | async-done | bytes 8388624 | tf_op jit(solution)/shard_map/all_gather | solution.py:52
  175.0 7.8 %copy.7 = bf16[512,8192]{1,0:T(8,128)(2,1)} copy(bf16[512,8192]{1,0:T(8,128)(2,1)} %all-gather.2.cloned.1.call-done) | data formatting | bytes 16777216
  (2 shorter events, 0.0 us)
Async XLA Ops:
  7.2 167.8 %all-gather.2.cloned.1.call-start = ((), (), s32[]{:S(2)}) async-start(), calls=%async_computation.1 | async-start | bytes 8519680 | tf_op jit(solution)/shard_map/all_gather | solution.py:52
Sparse Core Ops, SparseCore 0:
  25.1 149.8 all-gather.1
where the time goes:
time: 191 us; the launch traced here: 190 us
  waiting for transfers between devices  150 us (79%)
  between operations  14.1 us (7%)
  blocking collectives  13.4 us (7%)
  local copies, waits for them, and re-layouts  7.81 us (4%)
  other arithmetic  4.26 us (2%)
    all_gather x1, waiting for transfers between devices, on_device(): lax.all_gather(new_master.astype(jnp.bfloat16), 'fsdp', axis=0, tiled=True)  150 us
    all_to_all x1, blocking collectives, copy_for_each(): lax.all_to_all(jnp.broadcast_to(x[None], (size, *x.shape)), axis, 0, 0, t...  13.4 us
    unnamed x1, local copies, waits for them, and re-layouts  7.77 us
  transfers between devices with their start and end apart: 1, of which 1 were waited for; matrix products, arithmetic and copies ran while one was open for 0% of the time, Pallas kernels for 0%

commit v1 on v0

v1 whole, which is shorter than its diff:
```python
import functools

import jax
import jax.numpy as jnp
from jax import lax
from jax.experimental import pallas as pl
from jax.experimental.pallas import tpu as pltpu
from jax.sharding import PartitionSpec as P

BLOCK = 128

epsilon = 1e-06
code_limit = 31.0
momentum_decay = 0.9
outer_rate = 0.7

AXES = ("island", "fsdp")
RING = 8
HALF = 4096
ROWS = 8


def all_places():
    for x_lo in range(2):
        for core in range(2):
            for x_hi in range(2):
                for y in range(4):
                    for z in range(8):
                        yield x_lo, core, x_hi, y, z


def number(place):
    x_lo, core, x_hi, y, z = place
    return (x_lo * 2 + core) * 64 + (x_hi * 4 + y) * 8 + z


def pairs(target):
    return [(number(p), number(target(*p))) for p in all_places()]


def snake_of(x_hi, y):
    return y if x_hi == 0 else 7 - y


def along_snake(x_lo, core, x_hi, y, z, step):
    at = (snake_of(x_hi, y) + step) % RING
    to_hi, to_y = (0, at) if at < 4 else (1, 7 - at)
    return (x_lo if to_hi == x_hi else 1 - x_lo), core, to_hi, to_y, z


def along_z(x_lo, core, x_hi, y, z, step):
    return x_lo, core, x_hi, y, (z + step) % RING


def first_phase(step):
    return pairs(lambda *p: (along_snake if p[1] == 0 else along_z)(*p, step))


def second_phase(step):
    return pairs(lambda *p: (along_z if p[1] == 0 else along_snake)(*p, step))


OTHER_CORE = pairs(lambda x_lo, core, x_hi, y, z: (x_lo, 1 - core, x_hi, y, z))
OTHER_CHIP = pairs(lambda x_lo, core, x_hi, y, z: (1 - x_lo, core, x_hi, y, z))
OTHER_BOTH = pairs(lambda x_lo, core, x_hi, y, z: (1 - x_lo, 1 - core, x_hi, y, z))


def send(x, to):
    return lax.ppermute(x, AXES, to)


def my_core():
    return lax.rem(lax.axis_index("island"), 2)


def my_z():
    return lax.rem(lax.axis_index("fsdp"), RING)


def my_snake():
    at = lax.div(lax.axis_index("fsdp"), RING)
    return jnp.where(at < 4, at, 11 - at)


def row_block(snake):
    at = lax.rem(snake + 2 * RING, RING)
    return jnp.where(at < 4, at, 11 - at)


def encode_kernel(weights, base, keep, give):
    core = my_core()
    for out, half in ((keep, core), (give, 1 - core)):
        for block in range(HALF // BLOCK):
            at = pl.multiple_of(half * HALF + block * BLOCK, BLOCK)
            outer_grad = base[:, pl.ds(at, BLOCK)] - weights[0, :, pl.ds(at, BLOCK)].astype(jnp.float32)
            largest = jnp.max(jnp.abs(outer_grad), axis=1, keepdims=True)
            block_scale = (largest + epsilon) / code_limit
            code_values = (outer_grad / block_scale).astype(jnp.bfloat16)
            decoded = code_values.astype(jnp.float32) * block_scale
            out[:, block * BLOCK:(block + 1) * BLOCK] = decoded.astype(jnp.bfloat16)


def outer_step(summed, base_rows, moment_rows):
    averaged = summed * 0.25
    fresh_moment = momentum_decay * moment_rows + averaged
    fresh_master = base_rows - outer_rate * (averaged + momentum_decay * fresh_moment)
    return fresh_master, fresh_moment


def half_step_kernel(keep, from_core, from_chip, from_both, base, moment, summed, fresh):
    start = pl.multiple_of(my_core() * HALF, HALF)
    f32 = lambda ref: ref[...].astype(jnp.float32)
    total = (f32(keep) + f32(from_core)) + (f32(from_chip) + f32(from_both))
    summed[...] = total
    master, _ = outer_step(total, base[:, pl.ds(start, HALF)], moment[:, pl.ds(start, HALF)])
    fresh[...] = master.astype(jnp.bfloat16)


def whole_step_kernel(mine, theirs, base, moment, master_out, moment_out):
    core = my_core()
    for summed, half in ((mine, core), (theirs, 1 - core)):
        start = pl.multiple_of(half * HALF, HALF)
        master, fresh = outer_step(summed[...], base[:, pl.ds(start, HALF)], moment[:, pl.ds(start, HALF)])
        master_out[:, pl.ds(start, HALF)] = master
        moment_out[:, pl.ds(start, HALF)] = fresh


def bundle_kernel(*refs):
    *pieces, out = refs
    core, snake, z = my_core(), my_snake(), my_z()
    for step, piece in enumerate(pieces):
        at = jnp.where(core == 0, row_block(snake + step), lax.rem(z + step, RING))
        out[pl.ds(at, 1)] = piece[...][None]


def assemble_kernel(steps, *refs):
    *refs, sems = refs
    n = len(steps)
    mine, theirs, out = refs[:n], refs[n:2 * n], refs[-1]
    core, snake, z = my_core(), my_snake(), my_z()

    def copies(low, high):
        for i, step in enumerate(steps):
            to_z = lax.rem(z + step + RING, RING)
            yield pltpu.make_async_copy(low[i], out.at[:, to_z, :, pl.ds(0, HALF)], sems.at[2 * i])
            yield pltpu.make_async_copy(high[i], out.at[row_block(snake + step), :, :, pl.ds(HALF, HALF)], sems.at[2 * i + 1])

    @pl.when(core == 0)
    def _():
        todo = list(copies(mine, theirs))
        for copy in todo:
            copy.start()
        for copy in todo:
            copy.wait()

    @pl.when(core == 1)
    def _():
        todo = list(copies(theirs, mine))
        for copy in todo:
            copy.start()
        for copy in todo:
            copy.wait()


VMEM = pl.BlockSpec(memory_space=pltpu.VMEM)
ANY = pl.BlockSpec(memory_space=pl.ANY)


def shape(dims, kind):
    return jax.ShapeDtypeStruct(dims, kind)


def hints(moved, scratch):
    return {
        "cost_estimate": pl.CostEstimate(flops=moved, bytes_accessed=moved, transcendentals=0),
        "compiler_params": pltpu.CompilerParams(vmem_limit_bytes=scratch),
    }


def assemble(steps, mine, theirs, out=None):
    given = [*mine, *theirs] + ([] if out is None else [out])
    return pl.pallas_call(
        functools.partial(assemble_kernel, steps),
        out_shape=shape((8, 8, ROWS, 2 * HALF), jnp.bfloat16),
        in_specs=[ANY] * len(given),
        out_specs=ANY,
        scratch_shapes=[pltpu.SemaphoreType.DMA((2 * len(steps),))],
        input_output_aliases={} if out is None else {len(given) - 1: 0},
        **hints(len(steps) << 21, 1 << 20),
        name="assemble",
    )(*given)


def on_device(local_weights, base, moment):
    bf16, f32 = jnp.bfloat16, jnp.float32
    keep, give = pl.pallas_call(
        encode_kernel,
        out_shape=(shape((ROWS, HALF), bf16),) * 2,
        in_specs=[VMEM] * 2, out_specs=(VMEM,) * 2, **hints(1 << 20, 4 << 20), name="encode",
    )(local_weights, base)
    peers = send(give, OTHER_BOTH), send(keep, OTHER_CHIP), send(give, OTHER_CORE)
    summed, fresh = pl.pallas_call(
        half_step_kernel,
        out_shape=(shape((ROWS, HALF), f32), shape((ROWS, HALF), bf16)),
        in_specs=[VMEM] * 6, out_specs=(VMEM,) * 2, **hints(1 << 20, 4 << 20), name="half_step",
    )(keep, peers[2], peers[1], peers[0], base, moment)

    pieces = [fresh] + [send(fresh, first_phase(-step)) for step in range(1, RING)]
    bundle = pl.pallas_call(
        bundle_kernel,
        out_shape=shape((8, ROWS, HALF), bf16),
        in_specs=[VMEM] * 8, out_specs=VMEM, **hints(1 << 20, 4 << 20), name="bundle",
    )(*pieces)

    theirs_summed = send(summed, OTHER_CORE)
    master, fresh_moment = pl.pallas_call(
        whole_step_kernel,
        out_shape=(shape((ROWS, 2 * HALF), f32),) * 2,
        in_specs=[VMEM] * 4, out_specs=(VMEM,) * 2, **hints(1 << 20, 4 << 20), name="whole_step",
    )(summed, theirs_summed, base, moment)

    mine = {0: bundle}
    for step in range(1, 5):
        mine[step] = send(mine[step - 1], second_phase(-1))
        if step < 4:
            mine[-step] = send(mine[1 - step], second_phase(1))
    theirs = {step: send(x, OTHER_CORE) for step, x in mine.items()}
    out = None
    for steps in ((0, 1, -1), (2, -2), (3, -3), (4,)):
        out = assemble(steps, [mine[s] for s in steps], [theirs[s] for s in steps], out)
    return master, fresh_moment, out.reshape(512, 2 * HALF)


def solution(mesh):
    return jax.shard_map(
        on_device,
        mesh=mesh,
        in_specs=(P("island", "fsdp", None), P("fsdp", None), P("fsdp", None)),
        out_specs=(P("fsdp", None), P("fsdp", None), P()),
        check_vma=False,
    )
```

time: 191 us -> 84 us (0.44)
  waiting for transfers between devices: 150 us -> 20.7 us
  starting transfers between devices: 0.04 us -> 49.1 us
  blocking collectives: 13.4 us -> 0 us
  between operations: 14.1 us -> 0.91 us
  Pallas kernels: 0 us -> 6.69 us
  other arithmetic: 4.26 us -> 0 us
  local copies, waits for them, and re-layouts: 7.81 us -> 5.65 us
    all_gather x1 -> x0, waiting for transfers between devices: 150 us -> none  [on_device(): lax.all_gather(new_master.astype(jnp.bfloat16), 'fsdp', axis=0, tiled=True)]
    ppermute x0 -> x26, starting transfers between devices: none -> 49.1 us  [send(): return lax.ppermute(x, AXES, to)]
    ppermute x0 -> x26, waiting for transfers between devices: none -> 20.7 us  [send(): return lax.ppermute(x, AXES, to)]
    all_to_all x1 -> x0, blocking collectives: 13.4 us -> none  [copy_for_each(): lax.all_to_all(jnp.broadcast_to(x[None], (size, *x.shape)), axis, 0, 0, t...]
    pallas_call x0 -> x8, Pallas kernels: none -> 6.69 us  [the longest x4 5.48 us: assemble(): pl.pallas_call(functools.partial(assemble_kernel, steps), out_shape=shape...]
    convert_element_type x2 -> x0, other arithmetic: 3.05 us -> none  [the longest x1 1.93 us: on_device(): new_master.astype(jnp.bfloat16)]
    unnamed x1 -> x12, local copies, waits for them, and re-layouts: 7.77 us -> 5.65 us
  transfers between devices with their start and end apart: 1 -> 26, of which waited for: 1 -> 9; matrix products, arithmetic and copies ran while one was open for 0% -> 0% of each run, Pallas kernels for 0% -> 6%
where the time goes in v1:
time: 84 us; the launch traced here: 83.1 us
  starting transfers between devices  49.1 us (58%)
  waiting for transfers between devices  20.7 us (25%)
  Pallas kernels  6.69 us (8%)
  local copies, waits for them, and re-layouts  5.65 us (7%)
  between operations  0.91 us (1%)
    ppermute x26, starting transfers between devices, send(): return lax.ppermute(x, AXES, to)  49.1 us
    ppermute x26, waiting for transfers between devices, send(): return lax.ppermute(x, AXES, to)  20.7 us
    unnamed x12, local copies, waits for them, and re-layouts  5.65 us
    pallas_call x4, Pallas kernels, assemble(): pl.pallas_call(functools.partial(assemble_kernel, steps), out_shape=shape...  5.48 us
  transfers between devices with their start and end apart: 26, of which 9 were waited for; matrix products, arithmetic and copies ran while one was open for 0% of the time, Pallas kernels for 6%

profile of v1, /device:TPU:1, one launch (start us, length us, event | category | flops | bytes accessed | tf_op | source)
XLA Modules:
  0.0 83.1 jit_solution(16031537358228767716)
XLA Ops:
  0.6 0.0 copy-start
  0.6 0.9 %copy-done = f32[8,8192]{1,0:T(8,128)S(1)} copy-done((f32[8,8192]{1,0:T(8,128)S(1)}, f32[8,8192]{1,0:T(8,128)}, u32[]{:S(2)}) %copy-start) | copy-done | bytes 262168
  1.6 0.9 %copy-done.5 = bf16[1,8,8192]{2,1,0:T(8,128)(2,1)S(1)} copy-done((bf16[1,8,8192]{2,1,0:T(8,128)(2,1)S(1)}, bf16[1,8,8192]{2,1,0:T(8,128)(2,1)}, u32[]{:S(2)}) %copy-start.5) | copy-done | bytes 131096
  2.5 0.2 encode.1
  2.7 3.3 %collective-permute-start = (bf16[8,4096]{1,0:T(8,128)(2,1)S(1)}, bf16[8,4096]{1,0:T(8,128)(2,1)S(1)}, u32[]{:S(2)}, u32[]{:S(2)}) collective-permute-start(bf16[8,4096]{1,0:T(8,128)(2,1)S(1)} %get-tuple-element.10), channel_id=1, source_target_pairs={{0,64},{1,65},{2,66},{3,67},{4,68},{5,69},{6,70},{7,71},{8,72},{9,... | collective-permute-start | bytes 196616 | tf_op jit(solution)/shard_map/ppermute | solution.py:69
  6.0 0.0 collective-permute-start.1
  6.0 1.7 %collective-permute-start.2 = (bf16[8,4096]{1,0:T(8,128)(2,1)S(1)}, bf16[8,4096]{1,0:T(8,128)(2,1)S(1)}, u32[]{:S(2)}, u32[]{:S(2)}) collective-permute-start(bf16[8,4096]{1,0:T(8,128)(2,1)S(1)} %get-tuple-element.10), channel_id=1, source_target_pairs={{0,192},{1,193},{2,194},{3,195},{4,196},{5,197},{6,198},{7,199},{8... | collective-permute-start | bytes 196616 | tf_op jit(solution)/shard_map/ppermute | solution.py:69
  7.7 0.0 collective-permute-done.from_core
  7.7 1.9 %collective-permute-done.1.from_chip = bf16[8,4096]{1,0:T(8,128)(2,1)S(1)} collective-permute-done((bf16[8,4096]{1,0:T(8,128)(2,1)S(1)}, bf16[8,4096]{1,0:T(8,128)(2,1)S(1)}, u32[]{:S(2)}, u32[]{:S(2)}) %collective-permute-start.1) | collective-permute-done | bytes 65568 | tf_op jit(solution)/shard_map/ppermute | solution.py:69
  9.7 1.6 %collective-permute-done.2.from_both = bf16[8,4096]{1,0:T(8,128)(2,1)S(1)} collective-permute-done((bf16[8,4096]{1,0:T(8,128)(2,1)S(1)}, bf16[8,4096]{1,0:T(8,128)(2,1)S(1)}, u32[]{:S(2)}, u32[]{:S(2)}) %collective-permute-start.2) | collective-permute-done | bytes 65568 | tf_op jit(solution)/shard_map/ppermute | solution.py:69
  11.3 0.9 %copy-done.1 = f32[8,8192]{1,0:T(8,128)S(1)} copy-done((f32[8,8192]{1,0:T(8,128)S(1)}, f32[8,8192]{1,0:T(8,128)}, u32[]{:S(2)}) %copy-start.1) | copy-done | bytes 262168
  12.2 0.9 %copy-done.3 = f32[8,8192]{1,0:T(8,128)S(1)} copy-done((f32[8,8192]{1,0:T(8,128)S(1)}, f32[8,8192]{1,0:T(8,128)}, u32[]{:S(2)}) %copy-start.3) | copy-done | bytes 262168
  13.2 0.1 half_step.1
  13.2 0.1 collective-permute-start.10
  13.3 4.0 %collective-permute-start.4 = (bf16[8,4096]{1,0:T(8,128)(2,1)S(1)}, bf16[8,4096]{1,0:T(8,128)(2,1)S(1)}, u32[]{:S(2)}, u32[]{:S(2)}) collective-permute-start(bf16[8,4096]{1,0:T(8,128)(2,1)S(1)} %get-tuple-element.14.refs_0_), channel_id=1, source_target_pairs={{0,160},{1,161},{2,162},{3,163},{4,164},{5,165},{6,166},{7,167},{8... | collective-permute-start | bytes 196616 | tf_op jit(solution)/shard_map/ppermute | solution.py:69
  17.3 1.8 %collective-permute-start.5 = (bf16[8,4096]{1,0:T(8,128)(2,1)S(1)}, bf16[8,4096]{1,0:T(8,128)(2,1)S(1)}, u32[]{:S(2)}, u32[]{:S(2)}) collective-permute-start(bf16[8,4096]{1,0:T(8,128)(2,1)S(1)} %get-tuple-element.14.refs_0_), channel_id=1, source_target_pairs={{0,168},{1,169},{2,170},{3,171},{4,172},{5,173},{6,174},{7,175},{8... | collective-permute-start | bytes 196616 | tf_op jit(solution)/shard_map/ppermute | solution.py:69
  19.1 2.1 %collective-permute-start.6 = (bf16[8,4096]{1,0:T(8,128)(2,1)S(1)}, bf16[8,4096]{1,0:T(8,128)(2,1)S(1)}, u32[]{:S(2)}, u32[]{:S(2)}) collective-permute-start(bf16[8,4096]{1,0:T(8,128)(2,1)S(1)} %get-tuple-element.14.refs_0_), channel_id=1, source_target_pairs={{0,176},{1,177},{2,178},{3,179},{4,180},{5,181},{6,182},{7,183},{8... | collective-permute-start | bytes 196616 | tf_op jit(solution)/shard_map/ppermute | solution.py:69
  21.2 2.8 %collective-permute-start.7 = (bf16[8,4096]{1,0:T(8,128)(2,1)S(1)}, bf16[8,4096]{1,0:T(8,128)(2,1)S(1)}, u32[]{:S(2)}, u32[]{:S(2)}) collective-permute-start(bf16[8,4096]{1,0:T(8,128)(2,1)S(1)} %get-tuple-element.14.refs_0_), channel_id=1, source_target_pairs={{0,184},{1,185},{2,186},{3,187},{4,188},{5,189},{6,190},{7,191},{8... | collective-permute-start | bytes 196616 | tf_op jit(solution)/shard_map/ppermute | solution.py:69
  24.0 0.0 collective-permute-done.10.refs_7_
  24.0 0.4 collective-permute-start.8
  24.5 0.0 collective-permute-done.4.refs_1_
  24.5 3.6 %collective-permute-start.9 = (bf16[8,4096]{1,0:T(8,128)(2,1)S(1)}, bf16[8,4096]{1,0:T(8,128)(2,1)S(1)}, u32[]{:S(2)}, u32[]{:S(2)}) collective-permute-start(bf16[8,4096]{1,0:T(8,128)(2,1)S(1)} %get-tuple-element.14.refs_0_), channel_id=1, source_target_pairs={{0,16},{1,17},{2,18},{3,19},{4,20},{5,21},{6,22},{7,23},{8,24},{9,... | collective-permute-start | bytes 196616 | tf_op jit(solution)/shard_map/ppermute | solution.py:69
  28.1 0.0 collective-permute-done.5.refs_2_
  28.1 0.0 collective-permute-done.6.refs_3_
  28.1 0.9 %collective-permute-done.7.refs_4_ = bf16[8,4096]{1,0:T(8,128)(2,1)S(1)} collective-permute-done((bf16[8,4096]{1,0:T(8,128)(2,1)S(1)}, bf16[8,4096]{1,0:T(8,128)(2,1)S(1)}, u32[]{:S(2)}, u32[]{:S(2)}) %collective-permute-start.7) | collective-permute-done | bytes 65568 | tf_op jit(solution)/shard_map/ppermute | solution.py:69
  29.0 1.5 %collective-permute-done.8.refs_5_ = bf16[8,4096]{1,0:T(8,128)(2,1)S(1)} collective-permute-done((bf16[8,4096]{1,0:T(8,128)(2,1)S(1)}, bf16[8,4096]{1,0:T(8,128)(2,1)S(1)}, u32[]{:S(2)}, u32[]{:S(2)}) %collective-permute-start.8) | collective-permute-done | bytes 65568 | tf_op jit(solution)/shard_map/ppermute | solution.py:69
  30.5 1.4 %collective-permute-done.9.refs_6_ = bf16[8,4096]{1,0:T(8,128)(2,1)S(1)} collective-permute-done((bf16[8,4096]{1,0:T(8,128)(2,1)S(1)}, bf16[8,4096]{1,0:T(8,128)(2,1)S(1)}, u32[]{:S(2)}, u32[]{:S(2)}) %collective-permute-start.9) | collective-permute-done | bytes 65568 | tf_op jit(solution)/shard_map/ppermute | solution.py:69
  31.9 0.1 bundle.1.refs_0_
  32.0 2.5 %collective-permute-start.11 = (bf16[8,8,4096]{2,1,0:T(8,128)(2,1)S(1)}, bf16[8,8,4096]{2,1,0:T(8,128)(2,1)S(1)}, u32[]{:S(2)}, u32[]{:S(2)}) collective-permute-start(bf16[8,8,4096]{2,1,0:T(8,128)(2,1)S(1)} %bundle.1.refs_0_), channel_id=1, source_target_pairs={{0,7},{1,0},{2,1},{3,2},{4,3},{5,4},{6,5},{7,6},{8,15},{9,8},{10,9... | collective-permute-start | bytes 1572872 | tf_op jit(solution)/shard_map/ppermute | solution.py:69
  34.5 0.0 collective-permute-start.16
  34.5 6.1 %collective-permute-done.11.refs_1_ = bf16[8,8,4096]{2,1,0:T(8,128)(2,1)S(1)} collective-permute-done((bf16[8,8,4096]{2,1,0:T(8,128)(2,1)S(1)}, bf16[8,8,4096]{2,1,0:T(8,128)(2,1)S(1)}, u32[]{:S(2)}, u32[]{:S(2)}) %collective-permute-start.11) | collective-permute-done | bytes 524320 | tf_op jit(solution)/shard_map/ppermute | solution.py:69
  40.6 3.4 %collective-permute-start.12 = (bf16[8,8,4096]{2,1,0:T(8,128)(2,1)S(1)}, bf16[8,8,4096]{2,1,0:T(8,128)(2,1)S(1)}, u32[]{:S(2)}, u32[]{:S(2)}) collective-permute-start(bf16[8,8,4096]{2,1,0:T(8,128)(2,1)S(1)} %collective-permute-done.11.refs_1_), channel_id=1, source_target_pairs={{0,7},{1,0},{2,1},{3,2},{4,3},{5,4},{6,5},{7,6},{8,15},{9,8},{10,9... | collective-permute-start | bytes 1572872 | tf_op jit(solution)/shard_map/ppermute | solution.py:69
  44.0 0.0 collective-permute-done.16.refs_2_
  44.0 0.0 collective-permute-start.17
  44.0 6.1 %collective-permute-done.12.refs_0_ = bf16[8,8,4096]{2,1,0:T(8,128)(2,1)S(1)} collective-permute-done((bf16[8,8,4096]{2,1,0:T(8,128)(2,1)S(1)}, bf16[8,8,4096]{2,1,0:T(8,128)(2,1)S(1)}, u32[]{:S(2)}, u32[]{:S(2)}) %collective-permute-start.12) | collective-permute-done | bytes 524320 | tf_op jit(solution)/shard_map/ppermute | solution.py:69
  50.2 3.4 %collective-permute-start.13 = (bf16[8,8,4096]{2,1,0:T(8,128)(2,1)S(1)}, bf16[8,8,4096]{2,1,0:T(8,128)(2,1)S(1)}, u32[]{:S(2)}, u32[]{:S(2)}) collective-permute-start(bf16[8,8,4096]{2,1,0:T(8,128)(2,1)S(1)} %collective-permute-done.12.refs_0_), channel_id=1, source_target_pairs={{0,7},{1,0},{2,1},{3,2},{4,3},{5,4},{6,5},{7,6},{8,15},{9,8},{10,9... | collective-permute-start | bytes 1572872 | tf_op jit(solution)/shard_map/ppermute | solution.py:69
  53.6 3.9 %collective-permute-start.3 = (f32[8,4096]{1,0:T(8,128)S(1)}, f32[8,4096]{1,0:T(8,128)S(1)}, u32[]{:S(2)}, u32[]{:S(2)}) collective-permute-start(f32[8,4096]{1,0:T(8,128)S(1)} %get-tuple-element.11.mine), channel_id=1, source_target_pairs={{0,64},{1,65},{2,66},{3,67},{4,68},{5,69},{6,70},{7,71},{8,72},{9,... | collective-permute-start | bytes 393224 | tf_op jit(solution)/shard_map/ppermute | solution.py:69
  57.5 0.0 collective-permute-start.23
  57.5 0.5 collective-permute-start.24
  58.0 0.5 collective-permute-done.3.theirs
  58.5 0.4 collective-permute-start.25
  58.8 0.0 collective-permute-done.17.refs_1_
  58.8 2.8 %collective-permute-start.18 = (bf16[8,8,4096]{2,1,0:T(8,128)(2,1)S(1)}, bf16[8,8,4096]{2,1,0:T(8,128)(2,1)S(1)}, u32[]{:S(2)}, u32[]{:S(2)}) collective-permute-start(bf16[8,8,4096]{2,1,0:T(8,128)(2,1)S(1)} %collective-permute-done.17.refs_1_), channel_id=1, source_target_pairs={{0,1},{1,2},{2,3},{3,4},{4,5},{5,6},{6,7},{7,0},{8,9},{9,10},{10,1... | collective-permute-start | bytes 1572872 | tf_op jit(solution)/shard_map/ppermute | solution.py:69
  61.6 0.0 collective-permute-done.13.refs_0_
  61.6 1.2 %collective-permute-start.14 = (bf16[8,8,4096]{2,1,0:T(8,128)(2,1)S(1)}, bf16[8,8,4096]{2,1,0:T(8,128)(2,1)S(1)}, u32[]{:S(2)}, u32[]{:S(2)}) collective-permute-start(bf16[8,8,4096]{2,1,0:T(8,128)(2,1)S(1)} %collective-permute-done.13.refs_0_), channel_id=1, source_target_pairs={{0,7},{1,0},{2,1},{3,2},{4,3},{5,4},{6,5},{7,6},{8,15},{9,8},{10,9... | collective-permute-start | bytes 1572872 | tf_op jit(solution)/shard_map/ppermute | solution.py:69
  62.8 0.0 collective-permute-done.23.refs_3_
  62.8 5.1 %collective-permute-start.21 = (bf16[8,8,4096]{2,1,0:T(8,128)(2,1)S(1)}, bf16[8,8,4096]{2,1,0:T(8,128)(2,1)S(1)}, u32[]{:S(2)}, u32[]{:S(2)}) collective-permute-start(bf16[8,8,4096]{2,1,0:T(8,128)(2,1)S(1)} %collective-permute-done.12.refs_0_), channel_id=1, source_target_pairs={{0,64},{1,65},{2,66},{3,67},{4,68},{5,69},{6,70},{7,71},{8,72},{9,... | collective-permute-start | bytes 1572872 | tf_op jit(solution)/shard_map/ppermute | solution.py:69
  67.9 0.0 collective-permute-done.24.refs_4_
  67.9 0.1 collective-permute-start.22
  68.0 0.0 collective-permute-done.25.refs_5_
  68.0 0.4 collective-permute-start.19
  68.4 1.0 %collective-permute-start.20 = (bf16[8,8,4096]{2,1,0:T(8,128)(2,1)S(1)}, bf16[8,8,4096]{2,1,0:T(8,128)(2,1)S(1)}, u32[]{:S(2)}, u32[]{:S(2)}) collective-permute-start(bf16[8,8,4096]{2,1,0:T(8,128)(2,1)S(1)} %collective-permute-done.18.refs_1_), channel_id=1, source_target_pairs={{0,64},{1,65},{2,66},{3,67},{4,68},{5,69},{6,70},{7,71},{8,72},{9,... | collective-permute-start | bytes 1572872 | tf_op jit(solution)/shard_map/ppermute | solution.py:69
  69.4 0.6 collective-permute-done.14.refs_0_
  70.0 4.6 %collective-permute-start.15 = (bf16[8,8,4096]{2,1,0:T(8,128)(2,1)S(1)}, bf16[8,8,4096]{2,1,0:T(8,128)(2,1)S(1)}, u32[]{:S(2)}, u32[]{:S(2)}) collective-permute-start(bf16[8,8,4096]{2,1,0:T(8,128)(2,1)S(1)} %collective-permute-done.14.refs_0_), channel_id=1, source_target_pairs={{0,64},{1,65},{2,66},{3,67},{4,68},{5,69},{6,70},{7,71},{8,72},{9,... | collective-permute-start | bytes 1572872 | tf_op jit(solution)/shard_map/ppermute | solution.py:69
  74.6 0.9 %copy-done.2 = f32[8,8192]{1,0:T(8,128)S(1)} copy-done((f32[8,8192]{1,0:T(8,128)S(1)}, f32[8,8192]{1,0:T(8,128)}, u32[]{:S(2)}) %copy-start.2) | copy-done | bytes 262168
  75.5 0.9 %copy-done.4 = f32[8,8192]{1,0:T(8,128)S(1)} copy-done((f32[8,8192]{1,0:T(8,128)S(1)}, f32[8,8192]{1,0:T(8,128)}, u32[]{:S(2)}) %copy-start.4) | copy-done | bytes 262168
  76.5 0.9 %whole_step.1 = (f32[8,8192]{1,0:T(8,128)}, f32[8,8192]{1,0:T(8,128)}) custom-call(f32[8,4096]{1,0:T(8,128)S(1)} %get-tuple-element.11.mine, f32[8,4096]{1,0:T(8,128)S(1)} %collective-permute-done.3.theirs, f32[8,8192]{1,0:T(8,128)S(1)} %copy-done.2, f32[8,8192]{1,0:T(8,128)S(1)} %copy-done.4), custom_call_target="tpu_custom_call" | custom-call | flops 1048576 | bytes 1048576 | tf_op jit(solution)/shard_map/whole_step/pallas_call | solution.py:216
  77.4 1.7 %assemble.4.refs_4_ = bf16[8,8,8,8192]{3,2,1,0:T(8,128)(2,1)} custom-call(bf16[8,8,4096]{2,1,0:T(8,128)(2,1)S(1)} %bundle.1.refs_0_, bf16[8,8,4096]{2,1,0:T(8,128)(2,1)S(1)} %collective-permute-done.11.refs_1_, bf16[8,8,4096]{2,1,0:T(8,128)(2,1)S(1)} %collective-permute-done.16.refs_2_, bf16[8,8,4096]{2,1,0:T(8,128)(2,1)S(1)} %collective-permute-done.23.refs_3_, ...), custom_call_target="tpu_custom_call" | custom-call | flops 6291456 | bytes 6291456 | tf_op jit(solution)/shard_map/assemble/pallas_call | solution.py:182
  79.1 0.0 collective-permute-done.21.refs_2_
  79.1 1.4 %assemble.5.refs_4_ = bf16[8,8,8,8192]{3,2,1,0:T(8,128)(2,1)} custom-call(bf16[8,8,4096]{2,1,0:T(8,128)(2,1)S(1)} %collective-permute-done.12.refs_0_, bf16[8,8,4096]{2,1,0:T(8,128)(2,1)S(1)} %collective-permute-done.17.refs_1_, bf16[8,8,4096]{2,1,0:T(8,128)(2,1)S(1)} %collective-permute-done.21.refs_2_, ...), custom_call_target="tpu_custom_call", output_to_operand_aliasing={{}: (4, {})} | custom-call | flops 4194304 | bytes 4194304 | tf_op jit(solution)/shard_map/assemble/pallas_call | solution.py:182
  80.5 0.0 collective-permute-done.19.refs_2_
  80.5 0.0 collective-permute-done.20.refs_3_
  80.5 1.4 %assemble.6.refs_2_ = bf16[8,8,8,8192]{3,2,1,0:T(8,128)(2,1)} custom-call(bf16[8,8,4096]{2,1,0:T(8,128)(2,1)S(1)} %collective-permute-done.13.refs_0_, bf16[8,8,4096]{2,1,0:T(8,128)(2,1)S(1)} %collective-permute-done.18.refs_1_, bf16[8,8,4096]{2,1,0:T(8,128)(2,1)S(1)} %collective-permute-done.19.refs_2_, ...), custom_call_target="tpu_custom_call", output_to_operand_aliasing={{}: (4, {})} | custom-call | flops 4194304 | bytes 4194304 | tf_op jit(solution)/shard_map/assemble/pallas_call | solution.py:182
  81.9 1.0 %assemble.7 = bf16[8,8,8,8192]{3,2,1,0:T(8,128)(2,1)} custom-call(bf16[8,8,4096]{2,1,0:T(8,128)(2,1)S(1)} %collective-permute-done.14.refs_0_, bf16[8,8,4096]{2,1,0:T(8,128)(2,1)S(1)} %collective-permute-done.15.refs_1_, bf16[8,8,8,8192]{3,2,1,0:T(8,128)(2,1)} %assemble.6.refs_2_), custom_call_target="tpu_custom_call", output_to_operand_aliasing={{}: (2, {})} | custom-call | flops 2097152 | bytes 2097152 | tf_op jit(solution)/shard_map/assemble/pallas_call | solution.py:182
  (8 shorter events, 0.0 us)
Async XLA Ops:
  0.6 1.0 %copy-start = (f32[8,8192]{1,0:T(8,128)S(1)}, f32[8,8192]{1,0:T(8,128)}, u32[]{:S(2)}) copy-start(f32[8,8192]{1,0:T(8,128)} %base.5) | copy-start | bytes 786436
  1.6 0.9 %copy-start.5 = (bf16[1,8,8192]{2,1,0:T(8,128)(2,1)S(1)}, bf16[1,8,8192]{2,1,0:T(8,128)(2,1)}, u32[]{:S(2)}) copy-start(bf16[1,8,8192]{2,1,0:T(8,128)(2,1)} %weights.1) | copy-start | bytes 393220
  2.7 5.1 %collective-permute-start = (bf16[8,4096]{1,0:T(8,128)(2,1)S(1)}, bf16[8,4096]{1,0:T(8,128)(2,1)S(1)}, u32[]{:S(2)}, u32[]{:S(2)}) collective-permute-start(bf16[8,4096]{1,0:T(8,128)(2,1)S(1)} %get-tuple-element.10), channel_id=1, source_target_pairs={{0,64},{1,65},{2,66},{3,67},{4,68},{5,69},{6,70},{7,71},{8,72},{9,... | collective-permute-start | bytes 196616 | tf_op jit(solution)/shard_map/ppermute | solution.py:69
  6.0 3.7 %collective-permute-start.1 = (bf16[8,4096]{1,0:T(8,128)(2,1)S(1)}, bf16[8,4096]{1,0:T(8,128)(2,1)S(1)}, u32[]{:S(2)}, u32[]{:S(2)}) collective-permute-start(bf16[8,4096]{1,0:T(8,128)(2,1)S(1)} %get-tuple-element.9.keep), channel_id=1, source_target_pairs={{0,128},{1,129},{2,130},{3,131},{4,132},{5,133},{6,134},{7,135},{8... | collective-permute-start | bytes 196616 | tf_op jit(solution)/shard_map/ppermute | solution.py:69
  6.0 5.2 %collective-permute-start.2 = (bf16[8,4096]{1,0:T(8,128)(2,1)S(1)}, bf16[8,4096]{1,0:T(8,128)(2,1)S(1)}, u32[]{:S(2)}, u32[]{:S(2)}) collective-permute-start(bf16[8,4096]{1,0:T(8,128)(2,1)S(1)} %get-tuple-element.10), channel_id=1, source_target_pairs={{0,192},{1,193},{2,194},{3,195},{4,196},{5,197},{6,198},{7,199},{8... | collective-permute-start | bytes 196616 | tf_op jit(solution)/shard_map/ppermute | solution.py:69
  11.3 1.0 %copy-start.1 = (f32[8,8192]{1,0:T(8,128)S(1)}, f32[8,8192]{1,0:T(8,128)}, u32[]{:S(2)}) copy-start(f32[8,8192]{1,0:T(8,128)} %base.5) | copy-start | bytes 786436
  12.2 0.9 %copy-start.3 = (f32[8,8192]{1,0:T(8,128)S(1)}, f32[8,8192]{1,0:T(8,128)}, u32[]{:S(2)}) copy-start(f32[8,8192]{1,0:T(8,128)} %moment.3) | copy-start | bytes 786436
  13.2 10.8 %collective-permute-start.10 = (bf16[8,4096]{1,0:T(8,128)(2,1)S(1)}, bf16[8,4096]{1,0:T(8,128)(2,1)S(1)}, u32[]{:S(2)}, u32[]{:S(2)}) collective-permute-start(bf16[8,4096]{1,0:T(8,128)(2,1)S(1)} %get-tuple-element.14.refs_0_), channel_id=1, source_target_pairs={{0,8},{1,9},{2,10},{3,11},{4,12},{5,13},{6,14},{7,15},{8,16},{9,17... | collective-permute-start | bytes 196616 | tf_op jit(solution)/shard_map/ppermute | solution.py:69
  13.3 11.2 %collective-permute-start.4 = (bf16[8,4096]{1,0:T(8,128)(2,1)S(1)}, bf16[8,4096]{1,0:T(8,128)(2,1)S(1)}, u32[]{:S(2)}, u32[]{:S(2)}) collective-permute-start(bf16[8,4096]{1,0:T(8,128)(2,1)S(1)} %get-tuple-element.14.refs_0_), channel_id=1, source_target_pairs={{0,160},{1,161},{2,162},{3,163},{4,164},{5,165},{6,166},{7,167},{8... | collective-permute-start | bytes 196616 | tf_op jit(solution)/shard_map/ppermute | solution.py:69
  17.3 10.8 %collective-permute-start.5 = (bf16[8,4096]{1,0:T(8,128)(2,1)S(1)}, bf16[8,4096]{1,0:T(8,128)(2,1)S(1)}, u32[]{:S(2)}, u32[]{:S(2)}) collective-permute-start(bf16[8,4096]{1,0:T(8,128)(2,1)S(1)} %get-tuple-element.14.refs_0_), channel_id=1, source_target_pairs={{0,168},{1,169},{2,170},{3,171},{4,172},{5,173},{6,174},{7,175},{8... | collective-permute-start | bytes 196616 | tf_op jit(solution)/shard_map/ppermute | solution.py:69
  19.1 9.0 %collective-permute-start.6 = (bf16[8,4096]{1,0:T(8,128)(2,1)S(1)}, bf16[8,4096]{1,0:T(8,128)(2,1)S(1)}, u32[]{:S(2)}, u32[]{:S(2)}) collective-permute-start(bf16[8,4096]{1,0:T(8,128)(2,1)S(1)} %get-tuple-element.14.refs_0_), channel_id=1, source_target_pairs={{0,176},{1,177},{2,178},{3,179},{4,180},{5,181},{6,182},{7,183},{8... | collective-permute-start | bytes 196616 | tf_op jit(solution)/shard_map/ppermute | solution.py:69
  21.2 7.8 %collective-permute-start.7 = (bf16[8,4096]{1,0:T(8,128)(2,1)S(1)}, bf16[8,4096]{1,0:T(8,128)(2,1)S(1)}, u32[]{:S(2)}, u32[]{:S(2)}) collective-permute-start(bf16[8,4096]{1,0:T(8,128)(2,1)S(1)} %get-tuple-element.14.refs_0_), channel_id=1, source_target_pairs={{0,184},{1,185},{2,186},{3,187},{4,188},{5,189},{6,190},{7,191},{8... | collective-permute-start | bytes 196616 | tf_op jit(solution)/shard_map/ppermute | solution.py:69
  24.0 6.4 %collective-permute-start.8 = (bf16[8,4096]{1,0:T(8,128)(2,1)S(1)}, bf16[8,4096]{1,0:T(8,128)(2,1)S(1)}, u32[]{:S(2)}, u32[]{:S(2)}) collective-permute-start(bf16[8,4096]{1,0:T(8,128)(2,1)S(1)} %get-tuple-element.14.refs_0_), channel_id=1, source_target_pairs={{0,24},{1,25},{2,26},{3,27},{4,28},{5,29},{6,30},{7,31},{8,184},{9... | collective-permute-start | bytes 196616 | tf_op jit(solution)/shard_map/ppermute | solution.py:69
  24.5 7.4 %collective-permute-start.9 = (bf16[8,4096]{1,0:T(8,128)(2,1)S(1)}, bf16[8,4096]{1,0:T(8,128)(2,1)S(1)}, u32[]{:S(2)}, u32[]{:S(2)}) collective-permute-start(bf16[8,4096]{1,0:T(8,128)(2,1)S(1)} %get-tuple-element.14.refs_0_), channel_id=1, source_target_pairs={{0,16},{1,17},{2,18},{3,19},{4,20},{5,21},{6,22},{7,23},{8,24},{9,... | collective-permute-start | bytes 196616 | tf_op jit(solution)/shard_map/ppermute | solution.py:69
  32.0 8.6 %collective-permute-start.11 = (bf16[8,8,4096]{2,1,0:T(8,128)(2,1)S(1)}, bf16[8,8,4096]{2,1,0:T(8,128)(2,1)S(1)}, u32[]{:S(2)}, u32[]{:S(2)}) collective-permute-start(bf16[8,8,4096]{2,1,0:T(8,128)(2,1)S(1)} %bundle.1.refs_0_), channel_id=1, source_target_pairs={{0,7},{1,0},{2,1},{3,2},{4,3},{5,4},{6,5},{7,6},{8,15},{9,8},{10,9... | collective-permute-start | bytes 1572872 | tf_op jit(solution)/shard_map/ppermute | solution.py:69
  34.5 9.5 %collective-permute-start.16 = (bf16[8,8,4096]{2,1,0:T(8,128)(2,1)S(1)}, bf16[8,8,4096]{2,1,0:T(8,128)(2,1)S(1)}, u32[]{:S(2)}, u32[]{:S(2)}) collective-permute-start(bf16[8,8,4096]{2,1,0:T(8,128)(2,1)S(1)} %bundle.1.refs_0_), channel_id=1, source_target_pairs={{0,1},{1,2},{2,3},{3,4},{4,5},{5,6},{6,7},{7,0},{8,9},{9,10},{10,1... | collective-permute-start | bytes 1572872 | tf_op jit(solution)/shard_map/ppermute | solution.py:69
  40.6 9.5 %collective-permute-start.12 = (bf16[8,8,4096]{2,1,0:T(8,128)(2,1)S(1)}, bf16[8,8,4096]{2,1,0:T(8,128)(2,1)S(1)}, u32[]{:S(2)}, u32[]{:S(2)}) collective-permute-start(bf16[8,8,4096]{2,1,0:T(8,128)(2,1)S(1)} %collective-permute-done.11.refs_1_), channel_id=1, source_target_pairs={{0,7},{1,0},{2,1},{3,2},{4,3},{5,4},{6,5},{7,6},{8,15},{9,8},{10,9... | collective-permute-start | bytes 1572872 | tf_op jit(solution)/shard_map/ppermute | solution.py:69
  44.0 14.8 %collective-permute-start.17 = (bf16[8,8,4096]{2,1,0:T(8,128)(2,1)S(1)}, bf16[8,8,4096]{2,1,0:T(8,128)(2,1)S(1)}, u32[]{:S(2)}, u32[]{:S(2)}) collective-permute-start(bf16[8,8,4096]{2,1,0:T(8,128)(2,1)S(1)} %collective-permute-done.16.refs_2_), channel_id=1, source_target_pairs={{0,1},{1,2},{2,3},{3,4},{4,5},{5,6},{6,7},{7,0},{8,9},{9,10},{10,1... | collective-permute-start | bytes 1572872 | tf_op jit(solution)/shard_map/ppermute | solution.py:69
  50.2 11.5 %collective-permute-start.13 = (bf16[8,8,4096]{2,1,0:T(8,128)(2,1)S(1)}, bf16[8,8,4096]{2,1,0:T(8,128)(2,1)S(1)}, u32[]{:S(2)}, u32[]{:S(2)}) collective-permute-start(bf16[8,8,4096]{2,1,0:T(8,128)(2,1)S(1)} %collective-permute-done.12.refs_0_), channel_id=1, source_target_pairs={{0,7},{1,0},{2,1},{3,2},{4,3},{5,4},{6,5},{7,6},{8,15},{9,8},{10,9... | collective-permute-start | bytes 1572872 | tf_op jit(solution)/shard_map/ppermute | solution.py:69
  53.6 4.9 %collective-permute-start.3 = (f32[8,4096]{1,0:T(8,128)S(1)}, f32[8,4096]{1,0:T(8,128)S(1)}, u32[]{:S(2)}, u32[]{:S(2)}) collective-permute-start(f32[8,4096]{1,0:T(8,128)S(1)} %get-tuple-element.11.mine), channel_id=1, source_target_pairs={{0,64},{1,65},{2,66},{3,67},{4,68},{5,69},{6,70},{7,71},{8,72},{9,... | collective-permute-start | bytes 393224 | tf_op jit(solution)/shard_map/ppermute | solution.py:69
  57.5 5.3 %collective-permute-start.23 = (bf16[8,8,4096]{2,1,0:T(8,128)(2,1)S(1)}, bf16[8,8,4096]{2,1,0:T(8,128)(2,1)S(1)}, u32[]{:S(2)}, u32[]{:S(2)}) collective-permute-start(bf16[8,8,4096]{2,1,0:T(8,128)(2,1)S(1)} %bundle.1.refs_0_), channel_id=1, source_target_pairs={{0,64},{1,65},{2,66},{3,67},{4,68},{5,69},{6,70},{7,71},{8,72},{9,... | collective-permute-start | bytes 1572872 | tf_op jit(solution)/shard_map/ppermute | solution.py:69
  57.5 10.4 %collective-permute-start.24 = (bf16[8,8,4096]{2,1,0:T(8,128)(2,1)S(1)}, bf16[8,8,4096]{2,1,0:T(8,128)(2,1)S(1)}, u32[]{:S(2)}, u32[]{:S(2)}) collective-permute-start(bf16[8,8,4096]{2,1,0:T(8,128)(2,1)S(1)} %collective-permute-done.11.refs_1_), channel_id=1, source_target_pairs={{0,64},{1,65},{2,66},{3,67},{4,68},{5,69},{6,70},{7,71},{8,72},{9,... | collective-permute-start | bytes 1572872 | tf_op jit(solution)/shard_map/ppermute | solution.py:69
  58.5 9.5 %collective-permute-start.25 = (bf16[8,8,4096]{2,1,0:T(8,128)(2,1)S(1)}, bf16[8,8,4096]{2,1,0:T(8,128)(2,1)S(1)}, u32[]{:S(2)}, u32[]{:S(2)}) collective-permute-start(bf16[8,8,4096]{2,1,0:T(8,128)(2,1)S(1)} %collective-permute-done.16.refs_2_), channel_id=1, source_target_pairs={{0,64},{1,65},{2,66},{3,67},{4,68},{5,69},{6,70},{7,71},{8,72},{9,... | collective-permute-start | bytes 1572872 | tf_op jit(solution)/shard_map/ppermute | solution.py:69
  58.8 9.6 %collective-permute-start.18 = (bf16[8,8,4096]{2,1,0:T(8,128)(2,1)S(1)}, bf16[8,8,4096]{2,1,0:T(8,128)(2,1)S(1)}, u32[]{:S(2)}, u32[]{:S(2)}) collective-permute-start(bf16[8,8,4096]{2,1,0:T(8,128)(2,1)S(1)} %collective-permute-done.17.refs_1_), channel_id=1, source_target_pairs={{0,1},{1,2},{2,3},{3,4},{4,5},{5,6},{6,7},{7,0},{8,9},{9,10},{10,1... | collective-permute-start | bytes 1572872 | tf_op jit(solution)/shard_map/ppermute | solution.py:69
  61.6 8.3 %collective-permute-start.14 = (bf16[8,8,4096]{2,1,0:T(8,128)(2,1)S(1)}, bf16[8,8,4096]{2,1,0:T(8,128)(2,1)S(1)}, u32[]{:S(2)}, u32[]{:S(2)}) collective-permute-start(bf16[8,8,4096]{2,1,0:T(8,128)(2,1)S(1)} %collective-permute-done.13.refs_0_), channel_id=1, source_target_pairs={{0,7},{1,0},{2,1},{3,2},{4,3},{5,4},{6,5},{7,6},{8,15},{9,8},{10,9... | collective-permute-start | bytes 1572872 | tf_op jit(solution)/shard_map/ppermute | solution.py:69
  62.8 16.3 %collective-permute-start.21 = (bf16[8,8,4096]{2,1,0:T(8,128)(2,1)S(1)}, bf16[8,8,4096]{2,1,0:T(8,128)(2,1)S(1)}, u32[]{:S(2)}, u32[]{:S(2)}) collective-permute-start(bf16[8,8,4096]{2,1,0:T(8,128)(2,1)S(1)} %collective-permute-done.12.refs_0_), channel_id=1, source_target_pairs={{0,64},{1,65},{2,66},{3,67},{4,68},{5,69},{6,70},{7,71},{8,72},{9,... | collective-permute-start | bytes 1572872 | tf_op jit(solution)/shard_map/ppermute | solution.py:69
  67.9 11.2 %collective-permute-start.22 = (bf16[8,8,4096]{2,1,0:T(8,128)(2,1)S(1)}, bf16[8,8,4096]{2,1,0:T(8,128)(2,1)S(1)}, u32[]{:S(2)}, u32[]{:S(2)}) collective-permute-start(bf16[8,8,4096]{2,1,0:T(8,128)(2,1)S(1)} %collective-permute-done.17.refs_1_), channel_id=1, source_target_pairs={{0,64},{1,65},{2,66},{3,67},{4,68},{5,69},{6,70},{7,71},{8,72},{9,... | collective-permute-start | bytes 1572872 | tf_op jit(solution)/shard_map/ppermute | solution.py:69
  68.0 12.5 %collective-permute-start.19 = (bf16[8,8,4096]{2,1,0:T(8,128)(2,1)S(1)}, bf16[8,8,4096]{2,1,0:T(8,128)(2,1)S(1)}, u32[]{:S(2)}, u32[]{:S(2)}) collective-permute-start(bf16[8,8,4096]{2,1,0:T(8,128)(2,1)S(1)} %collective-permute-done.13.refs_0_), channel_id=1, source_target_pairs={{0,64},{1,65},{2,66},{3,67},{4,68},{5,69},{6,70},{7,71},{8,72},{9,... | collective-permute-start | bytes 1572872 | tf_op jit(solution)/shard_map/ppermute | solution.py:69
  68.4 12.1 %collective-permute-start.20 = (bf16[8,8,4096]{2,1,0:T(8,128)(2,1)S(1)}, bf16[8,8,4096]{2,1,0:T(8,128)(2,1)S(1)}, u32[]{:S(2)}, u32[]{:S(2)}) collective-permute-start(bf16[8,8,4096]{2,1,0:T(8,128)(2,1)S(1)} %collective-permute-done.18.refs_1_), channel_id=1, source_target_pairs={{0,64},{1,65},{2,66},{3,67},{4,68},{5,69},{6,70},{7,71},{8,72},{9,... | collective-permute-start | bytes 1572872 | tf_op jit(solution)/shard_map/ppermute | solution.py:69
  70.0 11.9 %collective-permute-start.15 = (bf16[8,8,4096]{2,1,0:T(8,128)(2,1)S(1)}, bf16[8,8,4096]{2,1,0:T(8,128)(2,1)S(1)}, u32[]{:S(2)}, u32[]{:S(2)}) collective-permute-start(bf16[8,8,4096]{2,1,0:T(8,128)(2,1)S(1)} %collective-permute-done.14.refs_0_), channel_id=1, source_target_pairs={{0,64},{1,65},{2,66},{3,67},{4,68},{5,69},{6,70},{7,71},{8,72},{9,... | collective-permute-start | bytes 1572872 | tf_op jit(solution)/shard_map/ppermute | solution.py:69
  74.6 0.9 %copy-start.2 = (f32[8,8192]{1,0:T(8,128)S(1)}, f32[8,8192]{1,0:T(8,128)}, u32[]{:S(2)}) copy-start(f32[8,8192]{1,0:T(8,128)} %base.5) | copy-start | bytes 786436
  75.5 0.9 %copy-start.4 = (f32[8,8192]{1,0:T(8,128)S(1)}, f32[8,8192]{1,0:T(8,128)}, u32[]{:S(2)}) copy-start(f32[8,8192]{1,0:T(8,128)} %moment.3) | copy-start | bytes 786436

commit v2 on v1

v2 whole, which is shorter than its diff:
```python
import functools

import jax
import jax.numpy as jnp
from jax import lax
from jax.experimental import pallas as pl
from jax.experimental.pallas import tpu as pltpu
from jax.sharding import PartitionSpec as P

BLOCK = 128

epsilon = 1e-06
code_limit = 31.0
momentum_decay = 0.9
outer_rate = 0.7

AXES = ("island", "fsdp")
RING = 8
HALF = 4096
ROWS = 8


def all_places():
    for x_lo in range(2):
        for core in range(2):
            for x_hi in range(2):
                for y in range(4):
                    for z in range(8):
                        yield x_lo, core, x_hi, y, z


def number(place):
    x_lo, core, x_hi, y, z = place
    return (x_lo * 2 + core) * 64 + (x_hi * 4 + y) * 8 + z


def pairs(target):
    return [(number(p), number(target(*p))) for p in all_places()]


def snake_of(x_hi, y):
    return y if x_hi == 0 else 7 - y


def along_snake(x_lo, core, x_hi, y, z, step):
    at = (snake_of(x_hi, y) + step) % RING
    to_hi, to_y = (0, at) if at < 4 else (1, 7 - at)
    return (x_lo if to_hi == x_hi else 1 - x_lo), core, to_hi, to_y, z


def along_z(x_lo, core, x_hi, y, z, step):
    return x_lo, core, x_hi, y, (z + step) % RING


def first_phase(step):
    return pairs(lambda *p: (along_snake if p[1] == 0 else along_z)(*p, step))


def second_phase(step):
    return pairs(lambda *p: (along_z if p[1] == 0 else along_snake)(*p, step))


OTHER_CORE = pairs(lambda x_lo, core, x_hi, y, z: (x_lo, 1 - core, x_hi, y, z))
OTHER_CHIP = pairs(lambda x_lo, core, x_hi, y, z: (1 - x_lo, core, x_hi, y, z))
OTHER_BOTH = pairs(lambda x_lo, core, x_hi, y, z: (1 - x_lo, 1 - core, x_hi, y, z))


def send(x, to):
    return lax.ppermute(x, AXES, to)


def my_core():
    return lax.rem(lax.axis_index("island"), 2)


def my_z():
    return lax.rem(lax.axis_index("fsdp"), RING)


def my_snake():
    at = lax.div(lax.axis_index("fsdp"), RING)
    return jnp.where(at < 4, at, 11 - at)


def row_block(snake):
    at = lax.rem(snake + 2 * RING, RING)
    return jnp.where(at < 4, at, 11 - at)


def encode_kernel(weights, base, keep, give, base_near):
    core = my_core()
    for out, half in ((keep, core), (give, 1 - core)):
        for block in range(HALF // BLOCK):
            at = pl.multiple_of(half * HALF + block * BLOCK, BLOCK)
            outer_grad = base[:, pl.ds(at, BLOCK)] - weights[0, :, pl.ds(at, BLOCK)].astype(jnp.float32)
            largest = jnp.max(jnp.abs(outer_grad), axis=1, keepdims=True)
            block_scale = (largest + epsilon) / code_limit
            code_values = (outer_grad / block_scale).astype(jnp.bfloat16)
            decoded = code_values.astype(jnp.float32) * block_scale
            out[:, block * BLOCK:(block + 1) * BLOCK] = decoded.astype(jnp.bfloat16)
    base_near[...] = base[...]


def outer_step(summed, base_rows, decayed_rows):
    averaged = summed * 0.25
    fresh_moment = decayed_rows + averaged
    fresh_master = base_rows - outer_rate * (averaged + momentum_decay * fresh_moment)
    return fresh_master, fresh_moment


def half_step_kernel(keep, from_core, from_chip, from_both, base, decayed, summed, fresh):
    start = pl.multiple_of(my_core() * HALF, HALF)
    f32 = lambda ref: ref[...].astype(jnp.float32)
    total = (f32(keep) + f32(from_core)) + (f32(from_chip) + f32(from_both))
    summed[...] = total
    master, _ = outer_step(total, base[:, pl.ds(start, HALF)], decayed[:, pl.ds(start, HALF)])
    fresh[...] = master.astype(jnp.bfloat16)


def whole_step_kernel(mine, theirs, base, decayed, master_out, moment_out, written):
    written[...] = jnp.zeros_like(written)
    core = my_core()
    for summed, half in ((mine, core), (theirs, 1 - core)):
        start = pl.multiple_of(half * HALF, HALF)
        master, fresh = outer_step(summed[...], base[:, pl.ds(start, HALF)], decayed[:, pl.ds(start, HALF)])
        master_out[:, pl.ds(start, HALF)] = master
        moment_out[:, pl.ds(start, HALF)] = fresh


def trio_kernel(before, own, after, trio, duo):
    trio[0], trio[1], trio[2] = before[...], own[...], after[...]
    duo[0], duo[1] = own[...], after[...]


def chunk_kernel(trio, ahead, behind, low, high):
    core, snake, z = my_core(), my_snake(), my_z()
    for pieces, first in ((trio, -1), (ahead, 2), (behind, -3)):
        for i in range(pieces.shape[0]):
            step = first + i
            at = jnp.where(core == 0, row_block(snake + step), lax.rem(z + step + RING, RING))

            @pl.when(at < 4)
            def _():
                low[pl.ds(at, 1)] = pieces[i][None]

            @pl.when(at >= 4)
            def _():
                high[pl.ds(at - 4, 1)] = pieces[i][None]


def pack_kernel(count, *refs):
    for i in range(count):
        refs[-1][i] = refs[i][...]


def assemble_kernel(own, other, *refs):
    *refs, out, written, sems = refs
    core, snake, z = my_core(), my_snake(), my_z()

    def along_z(step, part):
        return out.at[pl.ds(4 * part, 4), lax.rem(z + step + RING, RING), :, pl.ds(0, HALF)]

    def along_snake(step, part):
        return out.at[row_block(snake + step), pl.ds(4 * part, 4), :, pl.ds(HALF, HALF)]

    def copies(at_own, at_other):
        for i, (where, array, place) in enumerate(own + other):
            source = refs[array] if place is None else refs[array].at[place]
            yield pltpu.make_async_copy(source, (at_own if i < len(own) else at_other)(*where), sems.at[i])

    for core_is, places in ((0, (along_z, along_snake)), (1, (along_snake, along_z))):
        @pl.when(core == core_is)
        def _():
            todo = list(copies(*places))
            for copy in todo:
                copy.start()
            for copy in todo:
                copy.wait()

    written[...] = jnp.zeros_like(written)


VMEM = pl.BlockSpec(memory_space=pltpu.VMEM)
ANY = pl.BlockSpec(memory_space=pl.ANY)


def shape(dims, kind):
    return jax.ShapeDtypeStruct(dims, kind)


def hints(moved, scratch):
    return {
        "cost_estimate": pl.CostEstimate(flops=moved, bytes_accessed=moved, transcendentals=0),
        "compiler_params": pltpu.CompilerParams(vmem_limit_bytes=scratch),
    }


def local(kernel, outs, given, scratch=(), grant=4 << 20, name=None, **more):
    return pl.pallas_call(
        kernel,
        out_shape=tuple(shape(*out) for out in outs),
        in_specs=more.pop("in_specs", [VMEM] * len(given)),
        out_specs=(VMEM,) * len(outs),
        scratch_shapes=scratch,
        name=name,
        **hints(1 << 20, grant),
    )(*given)


def assemble(own, other, out=None):
    arrays, placed = [], ([], [])
    for found, given in zip(placed, (own, other)):
        for array, where in given:
            if isinstance(where, list):
                found.extend((place, len(arrays), i) for i, place in enumerate(where))
            else:
                found.append((where, len(arrays), None))
            arrays.append(array)
    chunks = len(placed[0]) + len(placed[1])
    given = arrays + ([] if out is None else [out])
    return pl.pallas_call(
        functools.partial(assemble_kernel, *placed),
        out_shape=(shape((8, 8, ROWS, 2 * HALF), jnp.bfloat16), shape((8, 128), jnp.float32)),
        in_specs=[ANY] * len(given),
        out_specs=(ANY, VMEM),
        scratch_shapes=[pltpu.SemaphoreType.DMA((chunks,))],
        input_output_aliases={} if out is None else {len(given) - 1: 0},
        name="assemble",
        **hints(chunks << 20, 1 << 20),
    )(*given)


def on_device(local_weights, base_in, moment_in):
    bf16, f32 = jnp.bfloat16, jnp.float32
    half, whole = (ROWS, HALF), (ROWS, 2 * HALF)
    keep, give, base = local(
        encode_kernel, [(half, bf16), (half, bf16), (whole, f32)], (local_weights, base_in), name="encode",
    )
    decayed = momentum_decay * moment_in
    from_both, from_chip, from_core = send(give, OTHER_BOTH), send(keep, OTHER_CHIP), send(give, OTHER_CORE)
    summed, fresh = local(
        half_step_kernel, [(half, f32), (half, bf16)],
        (keep, from_core, from_chip, from_both, base, decayed), name="half_step",
    )

    after, before = send(fresh, first_phase(-1)), send(fresh, first_phase(1))
    trio, duo = local(trio_kernel, [((3, *half), bf16), ((2, *half), bf16)], (before, fresh, after), name="trio")
    ahead, behind = send(trio, first_phase(-3)), send(duo, first_phase(3))
    chunks = local(chunk_kernel, [((4, *half), bf16)] * 2, (trio, ahead, behind), name="chunks")

    theirs_summed = send(summed, OTHER_CORE)
    master, fresh_moment, stepped = local(
        whole_step_kernel, [(whole, f32)] * 2 + [((8, 128), f32)], (summed, theirs_summed, base, decayed), name="whole_step",
    )

    mine = {(0, part): chunks[part] for part in range(2)}
    for step in range(1, 5):
        for part in range(2):
            if step < 4 or part == 0:
                mine[step, part] = send(mine[step - 1, part], second_phase(-1))
            if step < 4 or part == 1:
                mine[-step, part] = send(mine[1 - step, part], second_phase(1))
    out, arrived, done = None, [], []
    for step in range(4):
        keys = [k for k in mine if abs(k[0]) == step]
        pack, = local(
            functools.partial(pack_kernel, len(keys)), [((len(keys), 4, *half), bf16)], [mine[k] for k in keys] + done,
            name="pack", grant=1 << 20, in_specs=[VMEM] * len(keys) + [ANY] * len(done),
        )
        out, written = assemble([(pack, keys)], arrived, out)
        done = [written] + ([stepped] if step == 0 else [])
        arrived = [(send(pack, OTHER_CORE), keys)]
    keys = [(4, 0), (-4, 1)]
    *last, _ = lax.optimization_barrier((*(mine[k] for k in keys), written))
    swapped = [(send(x, OTHER_CORE), k) for x, k in zip(last, keys)]
    out, _ = assemble([(mine[k], k) for k in keys], arrived, out)
    out, _ = assemble([], swapped, out)
    return master, fresh_moment, out.reshape(512, 2 * HALF)


def solution(mesh):
    return jax.shard_map(
        on_device,
        mesh=mesh,
        in_specs=(P("island", "fsdp", None), P("fsdp", None), P("fsdp", None)),
        out_specs=(P("fsdp", None), P("fsdp", None), P()),
        check_vma=False,
    )
```

time: 84 us -> 81.1 us (0.965)
  starting transfers between devices: 49.1 us -> 42.4 us
  waiting for transfers between devices: 20.7 us -> 24.6 us
  local copies, waits for them, and re-layouts: 5.65 us -> 1.85 us
  Pallas kernels: 6.69 us -> 10.1 us
  other arithmetic: 0 us -> 0.97 us
    ppermute x26 -> x28, starting transfers between devices: 49.1 us -> 42.4 us  [send(): return lax.ppermute(x, AXES, to)]
    ppermute x26 -> x28, waiting for transfers between devices: 20.7 us -> 24.6 us  [send(): return lax.ppermute(x, AXES, to)]
    unnamed x12 -> x4, local copies, waits for them, and re-layouts: 5.65 us -> 1.85 us
    pallas_call x8 -> x15, Pallas kernels: 6.69 us -> 10.1 us  [the longest x6 8.61 us: assemble(): pl.pallas_call(functools.partial(assemble_kernel, *placed), out_shape=(sh...]
    mul x0 -> x1, other arithmetic: none -> 0.97 us  [on_device(): decayed = momentum_decay * moment_in]
  transfers between devices with their start and end apart: 26 -> 28, of which waited for: 9 -> 10; matrix products, arithmetic and copies ran while one was open for 0% -> 1% of each run, Pallas kernels for 6% -> 10%
where the time goes in v2:
time: 81.1 us; the launch traced here: 80.9 us
  starting transfers between devices  42.4 us (52%)
  waiting for transfers between devices  24.6 us (30%)
  Pallas kernels  10.1 us (12%)
  local copies, waits for them, and re-layouts  1.85 us (2%)
  between operations  1.02 us (1%)
  other arithmetic  0.97 us (1%)
    ppermute x28, starting transfers between devices, send(): return lax.ppermute(x, AXES, to)  42.4 us
    ppermute x28, waiting for transfers between devices, send(): return lax.ppermute(x, AXES, to)  24.6 us
    pallas_call x6, Pallas kernels, assemble(): pl.pallas_call(functools.partial(assemble_kernel, *placed), out_shape=(sh...  8.61 us
    unnamed x4, local copies, waits for them, and re-layouts  1.85 us
  transfers between devices with their start and end apart: 28, of which 10 were waited for; matrix products, arithmetic and copies ran while one was open for 1% of the time, Pallas kernels for 10%

profile of v2, /device:TPU:1, one launch (start us, length us, event | category | flops | bytes accessed | tf_op | source)
XLA Modules:
  0.0 80.9 jit_solution(16789931347787315176)
XLA Ops:
  0.6 0.9 %copy-done = f32[8,8192]{1,0:T(8,128)S(1)} copy-done((f32[8,8192]{1,0:T(8,128)S(1)}, f32[8,8192]{1,0:T(8,128)}, u32[]{:S(2)}) %copy-start) | copy-done | bytes 262168
  1.6 0.9 %copy-done.1 = bf16[1,8,8192]{2,1,0:T(8,128)(2,1)S(1)} copy-done((bf16[1,8,8192]{2,1,0:T(8,128)(2,1)S(1)}, bf16[1,8,8192]{2,1,0:T(8,128)(2,1)}, u32[]{:S(2)}) %copy-start.1) | copy-done | bytes 131096
  2.5 0.2 encode.1
  2.7 3.3 %collective-permute-start = (bf16[8,4096]{1,0:T(8,128)(2,1)S(1)}, bf16[8,4096]{1,0:T(8,128)(2,1)S(1)}, u32[]{:S(2)}, u32[]{:S(2)}) collective-permute-start(bf16[8,4096]{1,0:T(8,128)(2,1)S(1)} %get-tuple-element.27), channel_id=1, source_target_pairs={{0,64},{1,65},{2,66},{3,67},{4,68},{5,69},{6,70},{7,71},{8,72},{9,... | collective-permute-start | bytes 196616 | tf_op jit(solution)/shard_map/ppermute | solution.py:69
  6.0 0.0 collective-permute-start.2
  6.0 1.4 %collective-permute-start.1 = (bf16[8,4096]{1,0:T(8,128)(2,1)S(1)}, bf16[8,4096]{1,0:T(8,128)(2,1)S(1)}, u32[]{:S(2)}, u32[]{:S(2)}) collective-permute-start(bf16[8,4096]{1,0:T(8,128)(2,1)S(1)} %get-tuple-element.26.keep), channel_id=1, source_target_pairs={{0,128},{1,129},{2,130},{3,131},{4,132},{5,133},{6,134},{7,135},{8... | collective-permute-start | bytes 196616 | tf_op jit(solution)/shard_map/ppermute | solution.py:69
  7.5 1.0 %broadcast_multiply_fusion.decayed = f32[8,8192]{1,0:T(8,128)S(1)} fusion(f32[8,8192]{1,0:T(8,128)} %param.5), kind=kLoop, calls=%fused_computation | loop fusion | flops 65536 | bytes 524288 | tf_op jit(solution)/shard_map/mul | solution.py:239
  8.4 0.0 collective-permute-done.from_core
  8.4 2.5 %collective-permute-done.1.from_chip = bf16[8,4096]{1,0:T(8,128)(2,1)S(1)} collective-permute-done((bf16[8,4096]{1,0:T(8,128)(2,1)S(1)}, bf16[8,4096]{1,0:T(8,128)(2,1)S(1)}, u32[]{:S(2)}, u32[]{:S(2)}) %collective-permute-start.1) | collective-permute-done | bytes 65568 | tf_op jit(solution)/shard_map/ppermute | solution.py:69
  11.0 0.1 half_step.1
  11.0 0.1 collective-permute-start.4
  11.1 3.8 %collective-permute-start.5 = (bf16[8,4096]{1,0:T(8,128)(2,1)S(1)}, bf16[8,4096]{1,0:T(8,128)(2,1)S(1)}, u32[]{:S(2)}, u32[]{:S(2)}) collective-permute-start(bf16[8,4096]{1,0:T(8,128)(2,1)S(1)} %get-tuple-element.32.own), channel_id=1, source_target_pairs={{0,160},{1,161},{2,162},{3,163},{4,164},{5,165},{6,166},{7,167},{8... | collective-permute-start | bytes 196616 | tf_op jit(solution)/shard_map/ppermute | solution.py:69
  14.9 1.9 %collective-permute-done.4.before = bf16[8,4096]{1,0:T(8,128)(2,1)S(1)} collective-permute-done((bf16[8,4096]{1,0:T(8,128)(2,1)S(1)}, bf16[8,4096]{1,0:T(8,128)(2,1)S(1)}, u32[]{:S(2)}, u32[]{:S(2)}) %collective-permute-start.4) | collective-permute-done | bytes 65568 | tf_op jit(solution)/shard_map/ppermute | solution.py:69
  16.8 0.0 collective-permute-done.5.after
  16.8 2.9 %collective-permute-start.6 = (bf16[3,8,4096]{2,1,0:T(8,128)(2,1)S(1)}, bf16[3,8,4096]{2,1,0:T(8,128)(2,1)S(1)}, u32[]{:S(2)}, u32[]{:S(2)}) collective-permute-start(bf16[3,8,4096]{2,1,0:T(8,128)(2,1)S(1)} %get-tuple-element.33.trio), channel_id=1, source_target_pairs={{0,176},{1,177},{2,178},{3,179},{4,180},{5,181},{6,182},{7,183},{8... | collective-permute-start | bytes 589832 | tf_op jit(solution)/shard_map/ppermute | solution.py:69
  19.7 1.3 %collective-permute-start.7 = (bf16[2,8,4096]{2,1,0:T(8,128)(2,1)S(1)}, bf16[2,8,4096]{2,1,0:T(8,128)(2,1)S(1)}, u32[]{:S(2)}, u32[]{:S(2)}) collective-permute-start(bf16[2,8,4096]{2,1,0:T(8,128)(2,1)S(1)} %get-tuple-element.34), channel_id=1, source_target_pairs={{0,24},{1,25},{2,26},{3,27},{4,28},{5,29},{6,30},{7,31},{8,184},{9... | collective-permute-start | bytes 393224 | tf_op jit(solution)/shard_map/ppermute | solution.py:69
  21.0 7.0 %collective-permute-done.7.behind = bf16[2,8,4096]{2,1,0:T(8,128)(2,1)S(1)} collective-permute-done((bf16[2,8,4096]{2,1,0:T(8,128)(2,1)S(1)}, bf16[2,8,4096]{2,1,0:T(8,128)(2,1)S(1)}, u32[]{:S(2)}, u32[]{:S(2)}) %collective-permute-start.7) | collective-permute-done | bytes 131104 | tf_op jit(solution)/shard_map/ppermute | solution.py:69
  27.9 0.0 collective-permute-done.6.ahead
  28.0 0.1 chunks.1
  28.1 1.1 %collective-permute-start.12 = (bf16[4,8,4096]{2,1,0:T(8,128)(2,1)S(1)}, bf16[4,8,4096]{2,1,0:T(8,128)(2,1)S(1)}, u32[]{:S(2)}, u32[]{:S(2)}) collective-permute-start(bf16[4,8,4096]{2,1,0:T(8,128)(2,1)S(1)} %get-tuple-element.36.refs_1_), channel_id=1, source_target_pairs={{0,1},{1,2},{2,3},{3,4},{4,5},{5,6},{6,7},{7,0},{8,9},{9,10},{10,1... | collective-permute-start | bytes 786440 | tf_op jit(solution)/shard_map/ppermute | solution.py:69
  29.2 1.5 %collective-permute-start.18 = (bf16[4,8,4096]{2,1,0:T(8,128)(2,1)S(1)}, bf16[4,8,4096]{2,1,0:T(8,128)(2,1)S(1)}, u32[]{:S(2)}, u32[]{:S(2)}) collective-permute-start(bf16[4,8,4096]{2,1,0:T(8,128)(2,1)S(1)} %get-tuple-element.35.refs_0_), channel_id=1, source_target_pairs={{0,1},{1,2},{2,3},{3,4},{4,5},{5,6},{6,7},{7,0},{8,9},{9,10},{10,1... | collective-permute-start | bytes 786440 | tf_op jit(solution)/shard_map/ppermute | solution.py:69
  30.8 1.1 %collective-permute-start.21 = (bf16[4,8,4096]{2,1,0:T(8,128)(2,1)S(1)}, bf16[4,8,4096]{2,1,0:T(8,128)(2,1)S(1)}, u32[]{:S(2)}, u32[]{:S(2)}) collective-permute-start(bf16[4,8,4096]{2,1,0:T(8,128)(2,1)S(1)} %get-tuple-element.36.refs_1_), channel_id=1, source_target_pairs={{0,7},{1,0},{2,1},{3,2},{4,3},{5,4},{6,5},{7,6},{8,15},{9,8},{10,9... | collective-permute-start | bytes 786440 | tf_op jit(solution)/shard_map/ppermute | solution.py:69
  31.9 0.4 collective-permute-start.8
  32.3 5.0 %collective-permute-start.3 = (f32[8,4096]{1,0:T(8,128)S(1)}, f32[8,4096]{1,0:T(8,128)S(1)}, u32[]{:S(2)}, u32[]{:S(2)}) collective-permute-start(f32[8,4096]{1,0:T(8,128)S(1)} %get-tuple-element.29.mine), channel_id=1, source_target_pairs={{0,64},{1,65},{2,66},{3,67},{4,68},{5,69},{6,70},{7,71},{8,72},{9,... | collective-permute-start | bytes 393224 | tf_op jit(solution)/shard_map/ppermute | solution.py:69
  37.3 1.0 %collective-permute-done.3.theirs = f32[8,4096]{1,0:T(8,128)S(1)} collective-permute-done((f32[8,4096]{1,0:T(8,128)S(1)}, f32[8,4096]{1,0:T(8,128)S(1)}, u32[]{:S(2)}, u32[]{:S(2)}) %collective-permute-start.3) | collective-permute-done | bytes 131104 | tf_op jit(solution)/shard_map/ppermute | solution.py:69
  38.3 0.9 %whole_step.1 = (f32[8,8192]{1,0:T(8,128)}, f32[8,8192]{1,0:T(8,128)}, f32[8,128]{1,0:T(8,128)S(1)}) custom-call(f32[8,4096]{1,0:T(8,128)S(1)} %get-tuple-element.29.mine, f32[8,4096]{1,0:T(8,128)S(1)} %collective-permute-done.3.theirs, f32[8,8192]{1,0:T(8,128)S(1)} %get-tuple-element.28.base, f32[8,8192]{1,0:T(8,128)S(1)} %broadcast_multiply_fusion.decayed), custom_call_target="tpu_custom_call" | custom-call | flops 1048576 | bytes 1048576 | tf_op jit(solution)/shard_map/whole_step/pallas_call | solution.py:199
  39.2 0.8 %assemble.6 = (bf16[8,8,8,8192]{3,2,1,0:T(8,128)(2,1)}, f32[8,128]{1,0:T(8,128)S(1)}) custom-call(bf16[2,4,8,4096]{3,2,1,0:T(8,128)(2,1)S(1)} %pack.4.refs_0_), custom_call_target="tpu_custom_call" | custom-call | flops 2097152 | bytes 2097152 | tf_op jit(solution)/shard_map/assemble/pallas_call | solution.py:221
  40.0 0.0 collective-permute-done.12.refs_3_
  40.0 0.0 collective-permute-done.18.refs_1_
  40.1 0.0 collective-permute-done.8.refs_0_
  40.1 0.1 pack.5.refs_0_
  40.1 2.4 %collective-permute-start.25 = (bf16[4,4,8,4096]{3,2,1,0:T(8,128)(2,1)S(1)}, bf16[4,4,8,4096]{3,2,1,0:T(8,128)(2,1)S(1)}, u32[]{:S(2)}, u32[]{:S(2)}) collective-permute-start(bf16[4,4,8,4096]{3,2,1,0:T(8,128)(2,1)S(1)} %pack.5.refs_0_), channel_id=1, source_target_pairs={{0,64},{1,65},{2,66},{3,67},{4,68},{5,69},{6,70},{7,71},{8,72},{9,... | collective-permute-start | bytes 3145736 | tf_op jit(solution)/shard_map/ppermute | solution.py:69
  42.5 0.1 collective-permute-start.24
  42.6 0.4 collective-permute-start.9
  43.0 1.0 %collective-permute-start.13 = (bf16[4,8,4096]{2,1,0:T(8,128)(2,1)S(1)}, bf16[4,8,4096]{2,1,0:T(8,128)(2,1)S(1)}, u32[]{:S(2)}, u32[]{:S(2)}) collective-permute-start(bf16[4,8,4096]{2,1,0:T(8,128)(2,1)S(1)} %collective-permute-done.12.refs_3_), channel_id=1, source_target_pairs={{0,1},{1,2},{2,3},{3,4},{4,5},{5,6},{6,7},{7,0},{8,9},{9,10},{10,1... | collective-permute-start | bytes 786440 | tf_op jit(solution)/shard_map/ppermute | solution.py:69
  44.1 0.9 %collective-permute-start.19 = (bf16[4,8,4096]{2,1,0:T(8,128)(2,1)S(1)}, bf16[4,8,4096]{2,1,0:T(8,128)(2,1)S(1)}, u32[]{:S(2)}, u32[]{:S(2)}) collective-permute-start(bf16[4,8,4096]{2,1,0:T(8,128)(2,1)S(1)} %collective-permute-done.18.refs_1_), channel_id=1, source_target_pairs={{0,1},{1,2},{2,3},{3,4},{4,5},{5,6},{6,7},{7,0},{8,9},{9,10},{10,1... | collective-permute-start | bytes 786440 | tf_op jit(solution)/shard_map/ppermute | solution.py:69
  44.9 0.6 collective-permute-done.24.refs_1_
  45.5 1.4 %collective-permute-start.22 = (bf16[4,8,4096]{2,1,0:T(8,128)(2,1)S(1)}, bf16[4,8,4096]{2,1,0:T(8,128)(2,1)S(1)}, u32[]{:S(2)}, u32[]{:S(2)}) collective-permute-start(bf16[4,8,4096]{2,1,0:T(8,128)(2,1)S(1)} %collective-permute-done.21.refs_2_), channel_id=1, source_target_pairs={{0,7},{1,0},{2,1},{3,2},{4,3},{5,4},{6,5},{7,6},{8,15},{9,8},{10,9... | collective-permute-start | bytes 786440 | tf_op jit(solution)/shard_map/ppermute | solution.py:69
  46.9 1.2 %collective-permute-done.9.refs_0_ = bf16[4,8,4096]{2,1,0:T(8,128)(2,1)S(1)} collective-permute-done((bf16[4,8,4096]{2,1,0:T(8,128)(2,1)S(1)}, bf16[4,8,4096]{2,1,0:T(8,128)(2,1)S(1)}, u32[]{:S(2)}, u32[]{:S(2)}) %collective-permute-start.9) | collective-permute-done | bytes 262176 | tf_op jit(solution)/shard_map/ppermute | solution.py:69
  48.1 2.0 %collective-permute-start.10 = (bf16[4,8,4096]{2,1,0:T(8,128)(2,1)S(1)}, bf16[4,8,4096]{2,1,0:T(8,128)(2,1)S(1)}, u32[]{:S(2)}, u32[]{:S(2)}) collective-permute-start(bf16[4,8,4096]{2,1,0:T(8,128)(2,1)S(1)} %collective-permute-done.9.refs_0_), channel_id=1, source_target_pairs={{0,7},{1,0},{2,1},{3,2},{4,3},{5,4},{6,5},{7,6},{8,15},{9,8},{10,9... | collective-permute-start | bytes 786440 | tf_op jit(solution)/shard_map/ppermute | solution.py:69
  50.1 0.7 collective-permute-done.13.refs_3_
  50.9 2.8 %collective-permute-done.19.refs_1_ = bf16[4,8,4096]{2,1,0:T(8,128)(2,1)S(1)} collective-permute-done((bf16[4,8,4096]{2,1,0:T(8,128)(2,1)S(1)}, bf16[4,8,4096]{2,1,0:T(8,128)(2,1)S(1)}, u32[]{:S(2)}, u32[]{:S(2)}) %collective-permute-start.19) | collective-permute-done | bytes 262176 | tf_op jit(solution)/shard_map/ppermute | solution.py:69
  53.7 0.0 collective-permute-start.20
  53.7 0.0 collective-permute-done.22.refs_2_
  53.7 2.7 %collective-permute-start.23 = (bf16[4,8,4096]{2,1,0:T(8,128)(2,1)S(1)}, bf16[4,8,4096]{2,1,0:T(8,128)(2,1)S(1)}, u32[]{:S(2)}, u32[]{:S(2)}) collective-permute-start(bf16[4,8,4096]{2,1,0:T(8,128)(2,1)S(1)} %collective-permute-done.22.refs_2_), channel_id=1, source_target_pairs={{0,7},{1,0},{2,1},{3,2},{4,3},{5,4},{6,5},{7,6},{8,15},{9,8},{10,9... | collective-permute-start | bytes 786440 | tf_op jit(solution)/shard_map/ppermute | solution.py:69
  56.4 1.2 %assemble.7 = (bf16[8,8,8,8192]{3,2,1,0:T(8,128)(2,1)}, f32[8,128]{1,0:T(8,128)S(1)}) custom-call(bf16[4,4,8,4096]{3,2,1,0:T(8,128)(2,1)S(1)} %pack.5.refs_0_, bf16[2,4,8,4096]{3,2,1,0:T(8,128)(2,1)S(1)} %collective-permute-done.24.refs_1_, bf16[8,8,8,8192]{3,2,1,0:T(8,128)(2,1)} %get-tuple-element.41.refs_2_), custom_call_target="tpu_custom_call", output_to_operand_aliasing={{0}: (2, {})} | custom-call | flops 6291456 | bytes 6291456 | tf_op jit(solution)/shard_map/assemble/pallas_call | solution.py:221
  57.6 0.1 pack.6.refs_0_
  57.6 3.8 %collective-permute-start.27 = (bf16[4,4,8,4096]{3,2,1,0:T(8,128)(2,1)S(1)}, bf16[4,4,8,4096]{3,2,1,0:T(8,128)(2,1)S(1)}, u32[]{:S(2)}, u32[]{:S(2)}) collective-permute-start(bf16[4,4,8,4096]{3,2,1,0:T(8,128)(2,1)S(1)} %pack.6.refs_0_), channel_id=1, source_target_pairs={{0,64},{1,65},{2,66},{3,67},{4,68},{5,69},{6,70},{7,71},{8,72},{9,... | collective-permute-start | bytes 3145736 | tf_op jit(solution)/shard_map/ppermute | solution.py:69
  61.4 1.4 %assemble.8 = (bf16[8,8,8,8192]{3,2,1,0:T(8,128)(2,1)}, f32[8,128]{1,0:T(8,128)S(1)}) custom-call(bf16[4,4,8,4096]{3,2,1,0:T(8,128)(2,1)S(1)} %pack.6.refs_0_, bf16[4,4,8,4096]{3,2,1,0:T(8,128)(2,1)S(1)} %collective-permute-done.25.refs_1_, bf16[8,8,8,8192]{3,2,1,0:T(8,128)(2,1)} %get-tuple-element.43.refs_2_), custom_call_target="tpu_custom_call", output_to_operand_aliasing={{0}: (2, {})} | custom-call | flops 8388608 | bytes 8388608 | tf_op jit(solution)/shard_map/assemble/pallas_call | solution.py:221
  62.8 0.0 collective-permute-done.10.refs_0_
  62.8 0.0 collective-permute-done.14.refs_3_
  62.8 0.0 collective-permute-done.23.refs_2_
  62.8 0.1 pack.7.refs_0_
  62.9 1.6 %collective-permute-start.26 = (bf16[4,4,8,4096]{3,2,1,0:T(8,128)(2,1)S(1)}, bf16[4,4,8,4096]{3,2,1,0:T(8,128)(2,1)S(1)}, u32[]{:S(2)}, u32[]{:S(2)}) collective-permute-start(bf16[4,4,8,4096]{3,2,1,0:T(8,128)(2,1)S(1)} %pack.7.refs_0_), channel_id=1, source_target_pairs={{0,64},{1,65},{2,66},{3,67},{4,68},{5,69},{6,70},{7,71},{8,72},{9,... | collective-permute-start | bytes 3145736 | tf_op jit(solution)/shard_map/ppermute | solution.py:69
  64.6 0.4 collective-permute-start.11
  65.0 1.0 %collective-permute-start.15 = (bf16[4,8,4096]{2,1,0:T(8,128)(2,1)S(1)}, bf16[4,8,4096]{2,1,0:T(8,128)(2,1)S(1)}, u32[]{:S(2)}, u32[]{:S(2)}) collective-permute-start(bf16[4,8,4096]{2,1,0:T(8,128)(2,1)S(1)} %collective-permute-done.14.refs_3_), channel_id=1, source_target_pairs={{0,1},{1,2},{2,3},{3,4},{4,5},{5,6},{6,7},{7,0},{8,9},{9,10},{10,1... | collective-permute-start | bytes 786440 | tf_op jit(solution)/shard_map/ppermute | solution.py:69
  66.0 4.1 %collective-permute-done.11.refs_0_ = bf16[4,8,4096]{2,1,0:T(8,128)(2,1)S(1)} collective-permute-done((bf16[4,8,4096]{2,1,0:T(8,128)(2,1)S(1)}, bf16[4,8,4096]{2,1,0:T(8,128)(2,1)S(1)}, u32[]{:S(2)}, u32[]{:S(2)}) %collective-permute-start.11) | collective-permute-done | bytes 262176 | tf_op jit(solution)/shard_map/ppermute | solution.py:69
  70.1 2.8 %collective-permute-done.15.refs_1_ = bf16[4,8,4096]{2,1,0:T(8,128)(2,1)S(1)} collective-permute-done((bf16[4,8,4096]{2,1,0:T(8,128)(2,1)S(1)}, bf16[4,8,4096]{2,1,0:T(8,128)(2,1)S(1)}, u32[]{:S(2)}, u32[]{:S(2)}) %collective-permute-start.15) | collective-permute-done | bytes 262176 | tf_op jit(solution)/shard_map/ppermute | solution.py:69
  72.8 2.6 %collective-permute-start.16 = (bf16[4,8,4096]{2,1,0:T(8,128)(2,1)S(1)}, bf16[4,8,4096]{2,1,0:T(8,128)(2,1)S(1)}, u32[]{:S(2)}, u32[]{:S(2)}) collective-permute-start(bf16[4,8,4096]{2,1,0:T(8,128)(2,1)S(1)} %collective-permute-done.11.refs_0_), channel_id=1, source_target_pairs={{0,64},{1,65},{2,66},{3,67},{4,68},{5,69},{6,70},{7,71},{8,72},{9,... | collective-permute-start | bytes 786440 | tf_op jit(solution)/shard_map/ppermute | solution.py:69
  75.5 0.0 collective-permute-start.17
  75.5 2.0 %assemble.9 = (bf16[8,8,8,8192]{3,2,1,0:T(8,128)(2,1)}, f32[8,128]{1,0:T(8,128)}) custom-call(bf16[4,4,8,4096]{3,2,1,0:T(8,128)(2,1)S(1)} %pack.7.refs_0_, bf16[4,4,8,4096]{3,2,1,0:T(8,128)(2,1)S(1)} %collective-permute-done.27.refs_1_, bf16[8,8,8,8192]{3,2,1,0:T(8,128)(2,1)} %get-tuple-element.45.refs_2_), custom_call_target="tpu_custom_call", output_to_operand_aliasing={{0}: (2, {})} | custom-call | flops 8388608 | bytes 8388608 | tf_op jit(solution)/shard_map/assemble/pallas_call | solution.py:221
  77.5 1.8 %assemble.10 = (bf16[8,8,8,8192]{3,2,1,0:T(8,128)(2,1)}, f32[8,128]{1,0:T(8,128)}) custom-call(bf16[4,8,4096]{2,1,0:T(8,128)(2,1)S(1)} %collective-permute-done.11.refs_0_, bf16[4,8,4096]{2,1,0:T(8,128)(2,1)S(1)} %collective-permute-done.15.refs_1_, bf16[4,4,8,4096]{3,2,1,0:T(8,128)(2,1)S(1)} %collective-permute-done.26.refs_2_, ...), custom_call_target="tpu_custom_call", output_to_operand_aliasing={{0}: (3, {})} | custom-call | flops 6291456 | bytes 6291456 | tf_op jit(solution)/shard_map/assemble/pallas_call | solution.py:221
  79.3 0.0 collective-permute-done.16.refs_0_
  79.3 1.4 %assemble.11 = (bf16[8,8,8,8192]{3,2,1,0:T(8,128)(2,1)}, f32[8,128]{1,0:T(8,128)}) custom-call(bf16[4,8,4096]{2,1,0:T(8,128)(2,1)S(1)} %collective-permute-done.16.refs_0_, bf16[4,8,4096]{2,1,0:T(8,128)(2,1)S(1)} %collective-permute-done.17.refs_1_, bf16[8,8,8,8192]{3,2,1,0:T(8,128)(2,1)} %get-tuple-element.47.refs_2_), custom_call_target="tpu_custom_call", output_to_operand_aliasing={{0}: (2, {})} | custom-call | flops 2097152 | bytes 2097152 | tf_op jit(solution)/shard_map/assemble/pallas_call | solution.py:221
  (12 shorter events, 0.1 us)
Async XLA Ops:
  0.6 1.0 %copy-start = (f32[8,8192]{1,0:T(8,128)S(1)}, f32[8,8192]{1,0:T(8,128)}, u32[]{:S(2)}) copy-start(f32[8,8192]{1,0:T(8,128)} %base.1) | copy-start | bytes 786436
  1.6 0.9 %copy-start.1 = (bf16[1,8,8192]{2,1,0:T(8,128)(2,1)S(1)}, bf16[1,8,8192]{2,1,0:T(8,128)(2,1)}, u32[]{:S(2)}) copy-start(bf16[1,8,8192]{2,1,0:T(8,128)(2,1)} %weights.1) | copy-start | bytes 393220
  2.7 5.8 %collective-permute-start = (bf16[8,4096]{1,0:T(8,128)(2,1)S(1)}, bf16[8,4096]{1,0:T(8,128)(2,1)S(1)}, u32[]{:S(2)}, u32[]{:S(2)}) collective-permute-start(bf16[8,4096]{1,0:T(8,128)(2,1)S(1)} %get-tuple-element.27), channel_id=1, source_target_pairs={{0,64},{1,65},{2,66},{3,67},{4,68},{5,69},{6,70},{7,71},{8,72},{9,... | collective-permute-start | bytes 196616 | tf_op jit(solution)/shard_map/ppermute | solution.py:69
  6.0 5.0 %collective-permute-start.2 = (bf16[8,4096]{1,0:T(8,128)(2,1)S(1)}, bf16[8,4096]{1,0:T(8,128)(2,1)S(1)}, u32[]{:S(2)}, u32[]{:S(2)}) collective-permute-start(bf16[8,4096]{1,0:T(8,128)(2,1)S(1)} %get-tuple-element.27), channel_id=1, source_target_pairs={{0,192},{1,193},{2,194},{3,195},{4,196},{5,197},{6,198},{7,199},{8... | collective-permute-start | bytes 196616 | tf_op jit(solution)/shard_map/ppermute | solution.py:69
  6.0 4.9 %collective-permute-start.1 = (bf16[8,4096]{1,0:T(8,128)(2,1)S(1)}, bf16[8,4096]{1,0:T(8,128)(2,1)S(1)}, u32[]{:S(2)}, u32[]{:S(2)}) collective-permute-start(bf16[8,4096]{1,0:T(8,128)(2,1)S(1)} %get-tuple-element.26.keep), channel_id=1, source_target_pairs={{0,128},{1,129},{2,130},{3,131},{4,132},{5,133},{6,134},{7,135},{8... | collective-permute-start | bytes 196616 | tf_op jit(solution)/shard_map/ppermute | solution.py:69
  11.0 5.7 %collective-permute-start.4 = (bf16[8,4096]{1,0:T(8,128)(2,1)S(1)}, bf16[8,4096]{1,0:T(8,128)(2,1)S(1)}, u32[]{:S(2)}, u32[]{:S(2)}) collective-permute-start(bf16[8,4096]{1,0:T(8,128)(2,1)S(1)} %get-tuple-element.32.own), channel_id=1, source_target_pairs={{0,8},{1,9},{2,10},{3,11},{4,12},{5,13},{6,14},{7,15},{8,16},{9,17... | collective-permute-start | bytes 196616 | tf_op jit(solution)/shard_map/ppermute | solution.py:69
  11.1 5.7 %collective-permute-start.5 = (bf16[8,4096]{1,0:T(8,128)(2,1)S(1)}, bf16[8,4096]{1,0:T(8,128)(2,1)S(1)}, u32[]{:S(2)}, u32[]{:S(2)}) collective-permute-start(bf16[8,4096]{1,0:T(8,128)(2,1)S(1)} %get-tuple-element.32.own), channel_id=1, source_target_pairs={{0,160},{1,161},{2,162},{3,163},{4,164},{5,165},{6,166},{7,167},{8... | collective-permute-start | bytes 196616 | tf_op jit(solution)/shard_map/ppermute | solution.py:69
  16.8 11.2 %collective-permute-start.6 = (bf16[3,8,4096]{2,1,0:T(8,128)(2,1)S(1)}, bf16[3,8,4096]{2,1,0:T(8,128)(2,1)S(1)}, u32[]{:S(2)}, u32[]{:S(2)}) collective-permute-start(bf16[3,8,4096]{2,1,0:T(8,128)(2,1)S(1)} %get-tuple-element.33.trio), channel_id=1, source_target_pairs={{0,176},{1,177},{2,178},{3,179},{4,180},{5,181},{6,182},{7,183},{8... | collective-permute-start | bytes 589832 | tf_op jit(solution)/shard_map/ppermute | solution.py:69
  19.7 8.3 %collective-permute-start.7 = (bf16[2,8,4096]{2,1,0:T(8,128)(2,1)S(1)}, bf16[2,8,4096]{2,1,0:T(8,128)(2,1)S(1)}, u32[]{:S(2)}, u32[]{:S(2)}) collective-permute-start(bf16[2,8,4096]{2,1,0:T(8,128)(2,1)S(1)} %get-tuple-element.34), channel_id=1, source_target_pairs={{0,24},{1,25},{2,26},{3,27},{4,28},{5,29},{6,30},{7,31},{8,184},{9... | collective-permute-start | bytes 393224 | tf_op jit(solution)/shard_map/ppermute | solution.py:69
  28.1 11.9 %collective-permute-start.12 = (bf16[4,8,4096]{2,1,0:T(8,128)(2,1)S(1)}, bf16[4,8,4096]{2,1,0:T(8,128)(2,1)S(1)}, u32[]{:S(2)}, u32[]{:S(2)}) collective-permute-start(bf16[4,8,4096]{2,1,0:T(8,128)(2,1)S(1)} %get-tuple-element.36.refs_1_), channel_id=1, source_target_pairs={{0,1},{1,2},{2,3},{3,4},{4,5},{5,6},{6,7},{7,0},{8,9},{9,10},{10,1... | collective-permute-start | bytes 786440 | tf_op jit(solution)/shard_map/ppermute | solution.py:69
  29.2 10.8 %collective-permute-start.18 = (bf16[4,8,4096]{2,1,0:T(8,128)(2,1)S(1)}, bf16[4,8,4096]{2,1,0:T(8,128)(2,1)S(1)}, u32[]{:S(2)}, u32[]{:S(2)}) collective-permute-start(bf16[4,8,4096]{2,1,0:T(8,128)(2,1)S(1)} %get-tuple-element.35.refs_0_), channel_id=1, source_target_pairs={{0,1},{1,2},{2,3},{3,4},{4,5},{5,6},{6,7},{7,0},{8,9},{9,10},{10,1... | collective-permute-start | bytes 786440 | tf_op jit(solution)/shard_map/ppermute | solution.py:69
  30.8 9.3 %collective-permute-start.21 = (bf16[4,8,4096]{2,1,0:T(8,128)(2,1)S(1)}, bf16[4,8,4096]{2,1,0:T(8,128)(2,1)S(1)}, u32[]{:S(2)}, u32[]{:S(2)}) collective-permute-start(bf16[4,8,4096]{2,1,0:T(8,128)(2,1)S(1)} %get-tuple-element.36.refs_1_), channel_id=1, source_target_pairs={{0,7},{1,0},{2,1},{3,2},{4,3},{5,4},{6,5},{7,6},{8,15},{9,8},{10,9... | collective-permute-start | bytes 786440 | tf_op jit(solution)/shard_map/ppermute | solution.py:69
  31.9 8.2 %collective-permute-start.8 = (bf16[4,8,4096]{2,1,0:T(8,128)(2,1)S(1)}, bf16[4,8,4096]{2,1,0:T(8,128)(2,1)S(1)}, u32[]{:S(2)}, u32[]{:S(2)}) collective-permute-start(bf16[4,8,4096]{2,1,0:T(8,128)(2,1)S(1)} %get-tuple-element.35.refs_0_), channel_id=1, source_target_pairs={{0,7},{1,0},{2,1},{3,2},{4,3},{5,4},{6,5},{7,6},{8,15},{9,8},{10,9... | collective-permute-start | bytes 786440 | tf_op jit(solution)/shard_map/ppermute | solution.py:69
  32.3 6.0 %collective-permute-start.3 = (f32[8,4096]{1,0:T(8,128)S(1)}, f32[8,4096]{1,0:T(8,128)S(1)}, u32[]{:S(2)}, u32[]{:S(2)}) collective-permute-start(f32[8,4096]{1,0:T(8,128)S(1)} %get-tuple-element.29.mine), channel_id=1, source_target_pairs={{0,64},{1,65},{2,66},{3,67},{4,68},{5,69},{6,70},{7,71},{8,72},{9,... | collective-permute-start | bytes 393224 | tf_op jit(solution)/shard_map/ppermute | solution.py:69
  40.1 17.5 %collective-permute-start.25 = (bf16[4,4,8,4096]{3,2,1,0:T(8,128)(2,1)S(1)}, bf16[4,4,8,4096]{3,2,1,0:T(8,128)(2,1)S(1)}, u32[]{:S(2)}, u32[]{:S(2)}) collective-permute-start(bf16[4,4,8,4096]{3,2,1,0:T(8,128)(2,1)S(1)} %pack.5.refs_0_), channel_id=1, source_target_pairs={{0,64},{1,65},{2,66},{3,67},{4,68},{5,69},{6,70},{7,71},{8,72},{9,... | collective-permute-start | bytes 3145736 | tf_op jit(solution)/shard_map/ppermute | solution.py:69
  42.5 3.0 %collective-permute-start.24 = (bf16[2,4,8,4096]{3,2,1,0:T(8,128)(2,1)S(1)}, bf16[2,4,8,4096]{3,2,1,0:T(8,128)(2,1)S(1)}, u32[]{:S(2)}, u32[]{:S(2)}) collective-permute-start(bf16[2,4,8,4096]{3,2,1,0:T(8,128)(2,1)S(1)} %pack.4.refs_0_), channel_id=1, source_target_pairs={{0,64},{1,65},{2,66},{3,67},{4,68},{5,69},{6,70},{7,71},{8,72},{9,... | collective-permute-start | bytes 1572872 | tf_op jit(solution)/shard_map/ppermute | solution.py:69
  42.6 5.5 %collective-permute-start.9 = (bf16[4,8,4096]{2,1,0:T(8,128)(2,1)S(1)}, bf16[4,8,4096]{2,1,0:T(8,128)(2,1)S(1)}, u32[]{:S(2)}, u32[]{:S(2)}) collective-permute-start(bf16[4,8,4096]{2,1,0:T(8,128)(2,1)S(1)} %collective-permute-done.8.refs_0_), channel_id=1, source_target_pairs={{0,7},{1,0},{2,1},{3,2},{4,3},{5,4},{6,5},{7,6},{8,15},{9,8},{10,9... | collective-permute-start | bytes 786440 | tf_op jit(solution)/shard_map/ppermute | solution.py:69
  43.0 7.8 %collective-permute-start.13 = (bf16[4,8,4096]{2,1,0:T(8,128)(2,1)S(1)}, bf16[4,8,4096]{2,1,0:T(8,128)(2,1)S(1)}, u32[]{:S(2)}, u32[]{:S(2)}) collective-permute-start(bf16[4,8,4096]{2,1,0:T(8,128)(2,1)S(1)} %collective-permute-done.12.refs_3_), channel_id=1, source_target_pairs={{0,1},{1,2},{2,3},{3,4},{4,5},{5,6},{6,7},{7,0},{8,9},{9,10},{10,1... | collective-permute-start | bytes 786440 | tf_op jit(solution)/shard_map/ppermute | solution.py:69
  44.1 9.6 %collective-permute-start.19 = (bf16[4,8,4096]{2,1,0:T(8,128)(2,1)S(1)}, bf16[4,8,4096]{2,1,0:T(8,128)(2,1)S(1)}, u32[]{:S(2)}, u32[]{:S(2)}) collective-permute-start(bf16[4,8,4096]{2,1,0:T(8,128)(2,1)S(1)} %collective-permute-done.18.refs_1_), channel_id=1, source_target_pairs={{0,1},{1,2},{2,3},{3,4},{4,5},{5,6},{6,7},{7,0},{8,9},{9,10},{10,1... | collective-permute-start | bytes 786440 | tf_op jit(solution)/shard_map/ppermute | solution.py:69
  45.5 8.2 %collective-permute-start.22 = (bf16[4,8,4096]{2,1,0:T(8,128)(2,1)S(1)}, bf16[4,8,4096]{2,1,0:T(8,128)(2,1)S(1)}, u32[]{:S(2)}, u32[]{:S(2)}) collective-permute-start(bf16[4,8,4096]{2,1,0:T(8,128)(2,1)S(1)} %collective-permute-done.21.refs_2_), channel_id=1, source_target_pairs={{0,7},{1,0},{2,1},{3,2},{4,3},{5,4},{6,5},{7,6},{8,15},{9,8},{10,9... | collective-permute-start | bytes 786440 | tf_op jit(solution)/shard_map/ppermute | solution.py:69
  48.1 14.7 %collective-permute-start.10 = (bf16[4,8,4096]{2,1,0:T(8,128)(2,1)S(1)}, bf16[4,8,4096]{2,1,0:T(8,128)(2,1)S(1)}, u32[]{:S(2)}, u32[]{:S(2)}) collective-permute-start(bf16[4,8,4096]{2,1,0:T(8,128)(2,1)S(1)} %collective-permute-done.9.refs_0_), channel_id=1, source_target_pairs={{0,7},{1,0},{2,1},{3,2},{4,3},{5,4},{6,5},{7,6},{8,15},{9,8},{10,9... | collective-permute-start | bytes 786440 | tf_op jit(solution)/shard_map/ppermute | solution.py:69
  50.9 11.9 %collective-permute-start.14 = (bf16[4,8,4096]{2,1,0:T(8,128)(2,1)S(1)}, bf16[4,8,4096]{2,1,0:T(8,128)(2,1)S(1)}, u32[]{:S(2)}, u32[]{:S(2)}) collective-permute-start(bf16[4,8,4096]{2,1,0:T(8,128)(2,1)S(1)} %collective-permute-done.13.refs_3_), channel_id=1, source_target_pairs={{0,1},{1,2},{2,3},{3,4},{4,5},{5,6},{6,7},{7,0},{8,9},{9,10},{10,1... | collective-permute-start | bytes 786440 | tf_op jit(solution)/shard_map/ppermute | solution.py:69
  53.7 9.1 %collective-permute-start.20 = (bf16[4,8,4096]{2,1,0:T(8,128)(2,1)S(1)}, bf16[4,8,4096]{2,1,0:T(8,128)(2,1)S(1)}, u32[]{:S(2)}, u32[]{:S(2)}) collective-permute-start(bf16[4,8,4096]{2,1,0:T(8,128)(2,1)S(1)} %collective-permute-done.19.refs_1_), channel_id=1, source_target_pairs={{0,1},{1,2},{2,3},{3,4},{4,5},{5,6},{6,7},{7,0},{8,9},{9,10},{10,1... | collective-permute-start | bytes 786440 | tf_op jit(solution)/shard_map/ppermute | solution.py:69
  53.7 9.1 %collective-permute-start.23 = (bf16[4,8,4096]{2,1,0:T(8,128)(2,1)S(1)}, bf16[4,8,4096]{2,1,0:T(8,128)(2,1)S(1)}, u32[]{:S(2)}, u32[]{:S(2)}) collective-permute-start(bf16[4,8,4096]{2,1,0:T(8,128)(2,1)S(1)} %collective-permute-done.22.refs_2_), channel_id=1, source_target_pairs={{0,7},{1,0},{2,1},{3,2},{4,3},{5,4},{6,5},{7,6},{8,15},{9,8},{10,9... | collective-permute-start | bytes 786440 | tf_op jit(solution)/shard_map/ppermute | solution.py:69
  57.6 17.8 %collective-permute-start.27 = (bf16[4,4,8,4096]{3,2,1,0:T(8,128)(2,1)S(1)}, bf16[4,4,8,4096]{3,2,1,0:T(8,128)(2,1)S(1)}, u32[]{:S(2)}, u32[]{:S(2)}) collective-permute-start(bf16[4,4,8,4096]{3,2,1,0:T(8,128)(2,1)S(1)} %pack.6.refs_0_), channel_id=1, source_target_pairs={{0,64},{1,65},{2,66},{3,67},{4,68},{5,69},{6,70},{7,71},{8,72},{9,... | collective-permute-start | bytes 3145736 | tf_op jit(solution)/shard_map/ppermute | solution.py:69
  62.9 14.5 %collective-permute-start.26 = (bf16[4,4,8,4096]{3,2,1,0:T(8,128)(2,1)S(1)}, bf16[4,4,8,4096]{3,2,1,0:T(8,128)(2,1)S(1)}, u32[]{:S(2)}, u32[]{:S(2)}) collective-permute-start(bf16[4,4,8,4096]{3,2,1,0:T(8,128)(2,1)S(1)} %pack.7.refs_0_), channel_id=1, source_target_pairs={{0,64},{1,65},{2,66},{3,67},{4,68},{5,69},{6,70},{7,71},{8,72},{9,... | collective-permute-start | bytes 3145736 | tf_op jit(solution)/shard_map/ppermute | solution.py:69
  64.6 5.5 %collective-permute-start.11 = (bf16[4,8,4096]{2,1,0:T(8,128)(2,1)S(1)}, bf16[4,8,4096]{2,1,0:T(8,128)(2,1)S(1)}, u32[]{:S(2)}, u32[]{:S(2)}) collective-permute-start(bf16[4,8,4096]{2,1,0:T(8,128)(2,1)S(1)} %collective-permute-done.10.refs_0_), channel_id=1, source_target_pairs={{0,7},{1,0},{2,1},{3,2},{4,3},{5,4},{6,5},{7,6},{8,15},{9,8},{10,9... | collective-permute-start | bytes 786440 | tf_op jit(solution)/shard_map/ppermute | solution.py:69
  65.0 7.8 %collective-permute-start.15 = (bf16[4,8,4096]{2,1,0:T(8,128)(2,1)S(1)}, bf16[4,8,4096]{2,1,0:T(8,128)(2,1)S(1)}, u32[]{:S(2)}, u32[]{:S(2)}) collective-permute-start(bf16[4,8,4096]{2,1,0:T(8,128)(2,1)S(1)} %collective-permute-done.14.refs_3_), channel_id=1, source_target_pairs={{0,1},{1,2},{2,3},{3,4},{4,5},{5,6},{6,7},{7,0},{8,9},{9,10},{10,1... | collective-permute-start | bytes 786440 | tf_op jit(solution)/shard_map/ppermute | solution.py:69
  72.8 6.5 %collective-permute-start.16 = (bf16[4,8,4096]{2,1,0:T(8,128)(2,1)S(1)}, bf16[4,8,4096]{2,1,0:T(8,128)(2,1)S(1)}, u32[]{:S(2)}, u32[]{:S(2)}) collective-permute-start(bf16[4,8,4096]{2,1,0:T(8,128)(2,1)S(1)} %collective-permute-done.11.refs_0_), channel_id=1, source_target_pairs={{0,64},{1,65},{2,66},{3,67},{4,68},{5,69},{6,70},{7,71},{8,72},{9,... | collective-permute-start | bytes 786440 | tf_op jit(solution)/shard_map/ppermute | solution.py:69
  75.5 3.8 %collective-permute-start.17 = (bf16[4,8,4096]{2,1,0:T(8,128)(2,1)S(1)}, bf16[4,8,4096]{2,1,0:T(8,128)(2,1)S(1)}, u32[]{:S(2)}, u32[]{:S(2)}) collective-permute-start(bf16[4,8,4096]{2,1,0:T(8,128)(2,1)S(1)} %collective-permute-done.15.refs_1_), channel_id=1, source_target_pairs={{0,64},{1,65},{2,66},{3,67},{4,68},{5,69},{6,70},{7,71},{8,72},{9,... | collective-permute-start | bytes 786440 | tf_op jit(solution)/shard_map/ppermute | solution.py:69

commit v3 on v2

v3 whole, which is shorter than its diff:
```python
import functools

import jax
import jax.numpy as jnp
from jax import lax
from jax.experimental import pallas as pl
from jax.experimental.pallas import tpu as pltpu
from jax.sharding import PartitionSpec as P

BLOCK = 128

epsilon = 1e-06
code_limit = 31.0
momentum_decay = 0.9
outer_rate = 0.7

AXES = ("island", "fsdp")
HALF = 4096
ROWS = 8


def all_places():
    for x_lo in range(2):
        for core in range(2):
            for x_hi in range(2):
                for y in range(4):
                    for z in range(8):
                        yield x_lo, core, x_hi, y, z


def number(place):
    x_lo, core, x_hi, y, z = place
    return (x_lo * 2 + core) * 64 + (x_hi * 4 + y % 4) * 8 + z


def pairs(target):
    return [(number(p), number(target(*p))) for p in all_places()]


OTHER_CORE = pairs(lambda x_lo, core, x_hi, y, z: (x_lo, 1 - core, x_hi, y, z))
OTHER_CHIP = pairs(lambda x_lo, core, x_hi, y, z: (1 - x_lo, core, x_hi, y, z))
OTHER_BOTH = pairs(lambda x_lo, core, x_hi, y, z: (1 - x_lo, 1 - core, x_hi, y, z))


def z_flipped(bits):
    return pairs(lambda x_lo, core, x_hi, y, z: (x_lo, core, x_hi, y, z ^ bits))


def along_y(sign):
    return pairs(lambda x_lo, core, x_hi, y, z: (x_lo, core, x_hi, y - sign if core == 0 else y + sign, z))


def across(sign):
    return pairs(lambda x_lo, core, x_hi, y, z: (1 - x_lo, core, 1 - x_hi, y if core == 0 else y + sign, z))


def send(x, to):
    return lax.ppermute(x, AXES, to)


def my_core():
    return lax.rem(lax.axis_index("island"), 2)


def my_z():
    return lax.rem(lax.axis_index("fsdp"), 8)


def my_y():
    return lax.rem(lax.div(lax.axis_index("fsdp"), 8), 4)


def my_x_hi():
    return lax.div(lax.axis_index("fsdp"), 32)


def encode_kernel(weights, base, keep, give, base_near):
    core = my_core()
    for out, half in ((keep, core), (give, 1 - core)):
        for block in range(HALF // BLOCK):
            at = pl.multiple_of(half * HALF + block * BLOCK, BLOCK)
            outer_grad = base[:, pl.ds(at, BLOCK)] - weights[0, :, pl.ds(at, BLOCK)].astype(jnp.float32)
            largest = jnp.max(jnp.abs(outer_grad), axis=1, keepdims=True)
            block_scale = (largest + epsilon) / code_limit
            code_values = (outer_grad / block_scale).astype(jnp.bfloat16)
            decoded = code_values.astype(jnp.float32) * block_scale
            out[:, block * BLOCK:(block + 1) * BLOCK] = decoded.astype(jnp.bfloat16)
    base_near[...] = base[...]


def outer_step(summed, base_rows, decayed_rows):
    averaged = summed * 0.25
    fresh_moment = decayed_rows + averaged
    fresh_master = base_rows - outer_rate * (averaged + momentum_decay * fresh_moment)
    return fresh_master, fresh_moment


def half_step_kernel(keep, from_core, from_chip, from_both, base, decayed, summed, fresh):
    start = pl.multiple_of(my_core() * HALF, HALF)
    f32 = lambda ref: ref[...].astype(jnp.float32)
    total = (f32(keep) + f32(from_core)) + (f32(from_chip) + f32(from_both))
    summed[...] = total
    master, _ = outer_step(total, base[:, pl.ds(start, HALF)], decayed[:, pl.ds(start, HALF)])
    fresh[...] = master.astype(jnp.bfloat16)


def whole_step_kernel(mine, theirs, base, decayed, master_out, moment_out, written):
    written[...] = jnp.zeros_like(written)
    core = my_core()
    for summed, half in ((mine, core), (theirs, 1 - core)):
        start = pl.multiple_of(half * HALF, HALF)
        master, fresh = outer_step(summed[...], base[:, pl.ds(start, HALF)], decayed[:, pl.ds(start, HALF)])
        master_out[:, pl.ds(start, HALF)] = master
        moment_out[:, pl.ds(start, HALF)] = fresh


def z_kernel(*refs):
    at, out = lax.rem(my_z(), 4), refs[-1]
    for bits, piece in enumerate(refs[:4]):
        out[pl.ds(at ^ bits, 1)] = piece[...][None]


def join_kernel(mine, theirs, out):
    core = my_core()
    out[:, :, pl.ds(pl.multiple_of(core * HALF, HALF), HALF)] = mine[...]
    out[:, :, pl.ds(pl.multiple_of((1 - core) * HALF, HALF), HALF)] = theirs[...]


def pack_kernel(first, second, *refs):
    refs[-1][0], refs[-1][1] = first[...], second[...]


def append_kernel(first, second, *refs):
    refs[-1][:4], refs[-1][4:] = first[...], second[...]


def cut_kernel(array, *refs):
    refs[-1][...] = array[pl.ds(2 * my_core(), 2)]


def place_of(what, lane, sign):
    x_hi, y = my_x_hi(), my_y()
    to_x, (low, high) = {
        "own": (x_hi, (0, 0)),
        "a": (x_hi, (sign, -sign)),
        "b": (1 - x_hi, (0, -sign)),
        "c": (1 - x_hi, (sign, 2)),
        "cut": (x_hi, (2, 2)),
    }[what]
    return to_x * 4 + lax.rem(y + 4 + jnp.where(lane == 0, low, high), 4)


def assemble_kernel(where, *refs):
    *refs, out, written, sems = refs
    core, half = my_core(), lax.div(my_z(), 4)
    todo = []
    for i, (what, wave, theirs, array, place) in enumerate(where):
        lane = 1 - core if theirs else core
        start = 4 * (half if wave == 0 else 1 - half)
        z = pl.ds(start + 2 * lane, 2) if what == "cut" else pl.ds(start, 4)
        source = refs[array] if place is None else refs[array].at[place if isinstance(place, int) else pl.ds(*place)]
        target = out.at[place_of(what, lane, SIGNS[wave]), z]
        todo.append(pltpu.make_async_copy(source, target, sems.at[i]))
    for copy in todo:
        copy.start()
    for copy in todo:
        copy.wait()
    written[...] = jnp.zeros_like(written)


SIGNS = (1, -1)
VMEM = pl.BlockSpec(memory_space=pltpu.VMEM)
ANY = pl.BlockSpec(memory_space=pl.ANY)


def shape(dims, kind):
    return jax.ShapeDtypeStruct(dims, kind)


def hints(moved, scratch):
    return {
        "cost_estimate": pl.CostEstimate(flops=moved, bytes_accessed=moved, transcendentals=0),
        "compiler_params": pltpu.CompilerParams(vmem_limit_bytes=scratch),
    }


def local(kernel, outs, given, scratch=(), grant=4 << 20, name=None, **more):
    return pl.pallas_call(
        kernel,
        out_shape=tuple(shape(*out) for out in outs),
        in_specs=more.pop("in_specs", [VMEM] * len(given)),
        out_specs=(VMEM,) * len(outs),
        scratch_shapes=scratch,
        name=name,
        **hints(1 << 20, grant),
    )(*given)


def assemble(given, out=None):
    where, size = [], 0
    for number_of, (array, what) in enumerate(given):
        if isinstance(what, tuple):
            what = [(*what, None)]
        where.extend((*item, number_of, place) for *item, place in what)
        size += array.size * 2
    given = [array for array, _ in given] + ([] if out is None else [out])
    return pl.pallas_call(
        functools.partial(assemble_kernel, where),
        out_shape=(shape((8, 8, ROWS, 2 * HALF), jnp.bfloat16), shape((8, 128), jnp.float32)),
        in_specs=[ANY] * len(given),
        out_specs=(ANY, VMEM),
        scratch_shapes=[pltpu.SemaphoreType.DMA((len(where),))],
        input_output_aliases={} if out is None else {len(given) - 1: 0},
        name="assemble",
        **hints(2 * size, 1 << 20),
    )(*given)


def on_device(local_weights, base_in, moment_in):
    bf16, f32 = jnp.bfloat16, jnp.float32
    half, whole = (ROWS, HALF), (ROWS, 2 * HALF)
    keep, give, base = local(
        encode_kernel, [(half, bf16), (half, bf16), (whole, f32)], (local_weights, base_in), name="encode",
    )
    decayed = momentum_decay * moment_in
    from_both, from_chip, from_core = send(give, OTHER_BOTH), send(keep, OTHER_CHIP), send(give, OTHER_CORE)
    summed, fresh = local(
        half_step_kernel, [(half, f32), (half, bf16)],
        (keep, from_core, from_chip, from_both, base, decayed), name="half_step",
    )

    theirs_summed = send(summed, OTHER_CORE)
    master, fresh_moment, stepped = local(
        whole_step_kernel, [(whole, f32)] * 2 + [((8, 128), f32)], (summed, theirs_summed, base, decayed), name="whole_step",
    )

    def small(kernel, dims, given, name, after=()):
        specs = [VMEM] * len(given) + [ANY] * len(after)
        return local(kernel, [(dims, bf16)], [*given, *after], name=name, grant=1 << 20, in_specs=specs)[0]

    far = send(fresh, z_flipped(4))
    bundles = []
    for first, after in ((fresh, (far,)), (far, ())):
        pieces = [first] + [send(first, z_flipped(bits)) for bits in (1, 2, 3)]
        mine = small(z_kernel, (4, *half), pieces, "z_pieces", after)
        bundles.append(small(join_kernel, (4, *whole), (mine, send(mine, OTHER_CORE)), "join"))

    def first_step(wave, bundle):
        return send(bundle, along_y(SIGNS[wave])), send(bundle, across(SIGNS[wave]))

    def second_step(wave, a, b):
        cut = small(cut_kernel, (2, *whole), (a,), "cut")
        return send(b, along_y(SIGNS[wave])), send(cut, along_y(SIGNS[wave]))

    def pair(a, b, after):
        return small(pack_kernel, (2, 4, *whole), (a, b), "pair", after)

    def append(c, d, after):
        return small(append_kernel, (6, *whole), (c, d), "append", after)

    def swap(x):
        return send(x, OTHER_CORE)

    def holds(what, wave, theirs):
        first, second = what
        if second == "cut":
            return [(first, wave, theirs, (0, 4)), (second, wave, theirs, (4, 2))]
        return [(first, wave, theirs, 0), (second, wave, theirs, 1)]

    ab, cd = ("a", "b"), ("c", "cut")
    a_0, b_0 = first_step(0, bundles[0])
    a_1, b_1 = first_step(1, bundles[1])
    a_0, b_0, bundles[1] = lax.optimization_barrier((a_0, b_0, bundles[1]))
    c_0, d_0 = second_step(0, a_0, b_0)
    pair_0 = pair(a_0, b_0, ())
    out, written = assemble([
        (bundles[0], ("own", 0, False)), (bundles[1], ("own", 1, False)), (pair_0, holds(ab, 0, False)),
    ])
    their_pair_0 = swap(pair_0)
    rest_0 = append(c_0, d_0, (written, stepped))
    a_1, b_1, rest_0 = lax.optimization_barrier((a_1, b_1, rest_0))
    c_1, d_1 = second_step(1, a_1, b_1)
    pair_1 = pair(a_1, b_1, ())
    their_pair_1 = swap(pair_1)
    out, written = assemble([
        (their_pair_0, holds(ab, 0, True)), (pair_1, holds(ab, 1, False)), (rest_0, holds(cd, 0, False)),
    ], out)
    their_rest_0 = swap(rest_0)
    rest_1 = append(c_1, d_1, (written,))
    out, _ = assemble([
        (their_rest_0, holds(cd, 0, True)), (their_pair_1, holds(ab, 1, True)), (rest_1, holds(cd, 1, False)),
    ], out)
    out, _ = assemble([(swap(rest_1), holds(cd, 1, True))], out)
    return master, fresh_moment, out.reshape(512, 2 * HALF)


def solution(mesh):
    return jax.shard_map(
        on_device,
        mesh=mesh,
        in_specs=(P("island", "fsdp", None), P("fsdp", None), P("fsdp", None)),
        out_specs=(P("fsdp", None), P("fsdp", None), P()),
        check_vma=False,
    )
```

time: 81.1 us -> 86.6 us (1.068)
  waiting for transfers between devices: 24.6 us -> 33.9 us
  Pallas kernels: 10.1 us -> 8.17 us
  starting transfers between devices: 42.4 us -> 40.6 us
    ppermute x28 -> x25, waiting for transfers between devices: 24.6 us -> 33.9 us  [send(): return lax.ppermute(x, AXES, to)]
    pallas_call x6 -> x4, Pallas kernels: 8.61 us -> 6.6 us  [assemble(): pl.pallas_call(functools.partial(assemble_kernel, where), out_shape=(shap...]
    ppermute x28 -> x25, starting transfers between devices: 42.4 us -> 40.6 us  [send(): return lax.ppermute(x, AXES, to)]
  transfers between devices with their start and end apart: 28 -> 25, of which waited for: 10 -> 11; matrix products, arithmetic and copies ran while one was open for 1% -> 1% of each run, Pallas kernels for 10% -> 7%
where the time goes in v3:
time: 86.6 us; the launch traced here: 86.4 us
  starting transfers between devices  40.6 us (47%)
  waiting for transfers between devices  33.9 us (39%)
  Pallas kernels  8.17 us (9%)
  local copies, waits for them, and re-layouts  1.85 us (2%)
  other arithmetic  0.97 us (1%)
  between operations  0.94 us (1%)
    ppermute x25, starting transfers between devices, send(): return lax.ppermute(x, AXES, to)  40.6 us
    ppermute x25, waiting for transfers between devices, send(): return lax.ppermute(x, AXES, to)  33.9 us
    pallas_call x4, Pallas kernels, assemble(): pl.pallas_call(functools.partial(assemble_kernel, where), out_shape=(shap...  6.6 us
    unnamed x4, local copies, waits for them, and re-layouts  1.85 us
  transfers between devices with their start and end apart: 25, of which 11 were waited for; matrix products, arithmetic and copies ran while one was open for 1% of the time, Pallas kernels for 7%

profile of v3, /device:TPU:1, one launch (start us, length us, event | category | flops | bytes accessed | tf_op | source)
XLA Modules:
  0.0 86.4 jit_solution(7098956326979338663)
XLA Ops:
  0.6 0.9 %copy-done = f32[8,8192]{1,0:T(8,128)S(1)} copy-done((f32[8,8192]{1,0:T(8,128)S(1)}, f32[8,8192]{1,0:T(8,128)}, u32[]{:S(2)}) %copy-start) | copy-done | bytes 262168
  1.6 0.9 %copy-done.1 = bf16[1,8,8192]{2,1,0:T(8,128)(2,1)S(1)} copy-done((bf16[1,8,8192]{2,1,0:T(8,128)(2,1)S(1)}, bf16[1,8,8192]{2,1,0:T(8,128)(2,1)}, u32[]{:S(2)}) %copy-start.1) | copy-done | bytes 131096
  2.5 0.2 encode.1
  2.7 2.7 %collective-permute-start.2 = (bf16[8,4096]{1,0:T(8,128)(2,1)S(1)}, bf16[8,4096]{1,0:T(8,128)(2,1)S(1)}, u32[]{:S(2)}, u32[]{:S(2)}) collective-permute-start(bf16[8,4096]{1,0:T(8,128)(2,1)S(1)} %get-tuple-element.24), channel_id=1, source_target_pairs={{0,192},{1,193},{2,194},{3,195},{4,196},{5,197},{6,198},{7,199},{8... | collective-permute-start | bytes 196616 | tf_op jit(solution)/shard_map/ppermute | solution.py:58
  5.4 0.7 collective-permute-start
  6.1 1.3 %collective-permute-start.1 = (bf16[8,4096]{1,0:T(8,128)(2,1)S(1)}, bf16[8,4096]{1,0:T(8,128)(2,1)S(1)}, u32[]{:S(2)}, u32[]{:S(2)}) collective-permute-start(bf16[8,4096]{1,0:T(8,128)(2,1)S(1)} %get-tuple-element.23.keep), channel_id=1, source_target_pairs={{0,128},{1,129},{2,130},{3,131},{4,132},{5,133},{6,134},{7,135},{8... | collective-permute-start | bytes 196616 | tf_op jit(solution)/shard_map/ppermute | solution.py:58
  7.4 1.0 %broadcast_multiply_fusion.decayed = f32[8,8192]{1,0:T(8,128)S(1)} fusion(f32[8,8192]{1,0:T(8,128)} %param.5), kind=kLoop, calls=%fused_computation | loop fusion | flops 65536 | bytes 524288 | tf_op jit(solution)/shard_map/mul | solution.py:225
  8.3 2.3 %collective-permute-done.1.from_chip = bf16[8,4096]{1,0:T(8,128)(2,1)S(1)} collective-permute-done((bf16[8,4096]{1,0:T(8,128)(2,1)S(1)}, bf16[8,4096]{1,0:T(8,128)(2,1)S(1)}, u32[]{:S(2)}, u32[]{:S(2)}) %collective-permute-start.1) | collective-permute-done | bytes 65568 | tf_op jit(solution)/shard_map/ppermute | solution.py:58
  10.7 0.0 collective-permute-done.2.from_both
  10.7 0.0 collective-permute-done.from_core
  10.7 0.1 half_step.1
  10.7 2.4 %collective-permute-start.13 = (bf16[8,4096]{1,0:T(8,128)(2,1)S(1)}, bf16[8,4096]{1,0:T(8,128)(2,1)S(1)}, u32[]{:S(2)}, u32[]{:S(2)}) collective-permute-start(bf16[8,4096]{1,0:T(8,128)(2,1)S(1)} %get-tuple-element.29.refs_0_), channel_id=1, source_target_pairs={{0,3},{1,2},{2,1},{3,0},{4,7},{5,6},{6,5},{7,4},{8,11},{9,10},{10,... | collective-permute-start | bytes 196616 | tf_op jit(solution)/shard_map/ppermute | solution.py:58
  13.2 0.0 collective-permute-start.12
  13.2 1.2 %collective-permute-start.11 = (bf16[8,4096]{1,0:T(8,128)(2,1)S(1)}, bf16[8,4096]{1,0:T(8,128)(2,1)S(1)}, u32[]{:S(2)}, u32[]{:S(2)}) collective-permute-start(bf16[8,4096]{1,0:T(8,128)(2,1)S(1)} %get-tuple-element.29.refs_0_), channel_id=1, source_target_pairs={{0,1},{1,0},{2,3},{3,2},{4,5},{5,4},{6,7},{7,6},{8,9},{9,8},{10,11... | collective-permute-start | bytes 196616 | tf_op jit(solution)/shard_map/ppermute | solution.py:58
  14.4 4.9 %collective-permute-start.4 = (bf16[8,4096]{1,0:T(8,128)(2,1)S(1)}, bf16[8,4096]{1,0:T(8,128)(2,1)S(1)}, u32[]{:S(2)}, u32[]{:S(2)}) collective-permute-start(bf16[8,4096]{1,0:T(8,128)(2,1)S(1)} %get-tuple-element.29.refs_0_), channel_id=1, source_target_pairs={{0,4},{1,5},{2,6},{3,7},{4,0},{5,1},{6,2},{7,3},{8,12},{9,13},{10,... | collective-permute-start | bytes 196616 | tf_op jit(solution)/shard_map/ppermute | solution.py:58
  19.3 0.0 collective-permute-done.13.refs_3_
  19.3 0.0 collective-permute-done.12.refs_2_
  19.3 0.0 collective-permute-done.11.refs_1_
  19.3 3.7 %collective-permute-done.4.refs_0_.refs_4_ = bf16[8,4096]{1,0:T(8,128)(2,1)S(1)} collective-permute-done((bf16[8,4096]{1,0:T(8,128)(2,1)S(1)}, bf16[8,4096]{1,0:T(8,128)(2,1)S(1)}, u32[]{:S(2)}, u32[]{:S(2)}) %collective-permute-start.4) | collective-permute-done | bytes 65568 | tf_op jit(solution)/shard_map/ppermute | solution.py:58
  23.1 3.0 %collective-permute-start.14 = (bf16[4,8,4096]{2,1,0:T(8,128)(2,1)S(1)}, bf16[4,8,4096]{2,1,0:T(8,128)(2,1)S(1)}, u32[]{:S(2)}, u32[]{:S(2)}) collective-permute-start(bf16[4,8,4096]{2,1,0:T(8,128)(2,1)S(1)} %z_pieces.3.mine), channel_id=1, source_target_pairs={{0,64},{1,65},{2,66},{3,67},{4,68},{5,69},{6,70},{7,71},{8,72},{9,... | collective-permute-start | bytes 786440 | tf_op jit(solution)/shard_map/ppermute | solution.py:58
  26.1 1.2 %collective-permute-done.14.theirs = bf16[4,8,4096]{2,1,0:T(8,128)(2,1)S(1)} collective-permute-done((bf16[4,8,4096]{2,1,0:T(8,128)(2,1)S(1)}, bf16[4,8,4096]{2,1,0:T(8,128)(2,1)S(1)}, u32[]{:S(2)}, u32[]{:S(2)}) %collective-permute-start.14) | collective-permute-done | bytes 262176 | tf_op jit(solution)/shard_map/ppermute | solution.py:58
  27.2 0.1 join.3.refs_0_
  27.3 3.9 %collective-permute-start.16 = (bf16[4,8,8192]{2,1,0:T(8,128)(2,1)S(1)}, bf16[4,8,8192]{2,1,0:T(8,128)(2,1)S(1)}, u32[]{:S(2)}, u32[]{:S(2)}) collective-permute-start(bf16[4,8,8192]{2,1,0:T(8,128)(2,1)S(1)} %join.3.refs_0_), channel_id=1, source_target_pairs={{0,160},{1,161},{2,162},{3,163},{4,164},{5,165},{6,166},{7,167},{8... | collective-permute-start | bytes 1572872 | tf_op jit(solution)/shard_map/ppermute | solution.py:58
  31.2 1.3 %collective-permute-start.15 = (bf16[4,8,8192]{2,1,0:T(8,128)(2,1)S(1)}, bf16[4,8,8192]{2,1,0:T(8,128)(2,1)S(1)}, u32[]{:S(2)}, u32[]{:S(2)}) collective-permute-start(bf16[4,8,8192]{2,1,0:T(8,128)(2,1)S(1)} %join.3.refs_0_), channel_id=1, source_target_pairs={{0,24},{1,25},{2,26},{3,27},{4,28},{5,29},{6,30},{7,31},{8,0},{9,1... | collective-permute-start | bytes 1572872 | tf_op jit(solution)/shard_map/ppermute | solution.py:58
  32.5 1.6 %collective-permute-start.7 = (bf16[8,4096]{1,0:T(8,128)(2,1)S(1)}, bf16[8,4096]{1,0:T(8,128)(2,1)S(1)}, u32[]{:S(2)}, u32[]{:S(2)}) collective-permute-start(bf16[8,4096]{1,0:T(8,128)(2,1)S(1)} %collective-permute-done.4.refs_0_.refs_4_), channel_id=1, source_target_pairs={{0,3},{1,2},{2,1},{3,0},{4,7},{5,6},{6,5},{7,4},{8,11},{9,10},{10,... | collective-permute-start | bytes 196616 | tf_op jit(solution)/shard_map/ppermute | solution.py:58
  34.1 1.8 %collective-permute-start.6 = (bf16[8,4096]{1,0:T(8,128)(2,1)S(1)}, bf16[8,4096]{1,0:T(8,128)(2,1)S(1)}, u32[]{:S(2)}, u32[]{:S(2)}) collective-permute-start(bf16[8,4096]{1,0:T(8,128)(2,1)S(1)} %collective-permute-done.4.refs_0_.refs_4_), channel_id=1, source_target_pairs={{0,2},{1,3},{2,0},{3,1},{4,6},{5,7},{6,4},{7,5},{8,10},{9,11},{10,... | collective-permute-start | bytes 196616 | tf_op jit(solution)/shard_map/ppermute | solution.py:58
  36.0 0.1 collective-permute-start.5
  36.1 1.4 %collective-permute-done.7.refs_3_ = bf16[8,4096]{1,0:T(8,128)(2,1)S(1)} collective-permute-done((bf16[8,4096]{1,0:T(8,128)(2,1)S(1)}, bf16[8,4096]{1,0:T(8,128)(2,1)S(1)}, u32[]{:S(2)}, u32[]{:S(2)}) %collective-permute-start.7) | collective-permute-done | bytes 65568 | tf_op jit(solution)/shard_map/ppermute | solution.py:58
  37.5 3.2 %collective-permute-done.6.refs_2_ = bf16[8,4096]{1,0:T(8,128)(2,1)S(1)} collective-permute-done((bf16[8,4096]{1,0:T(8,128)(2,1)S(1)}, bf16[8,4096]{1,0:T(8,128)(2,1)S(1)}, u32[]{:S(2)}, u32[]{:S(2)}) %collective-permute-start.6) | collective-permute-done | bytes 65568 | tf_op jit(solution)/shard_map/ppermute | solution.py:58
  40.7 0.0 collective-permute-done.5.refs_1_
  40.7 2.5 %collective-permute-start.8 = (bf16[4,8,4096]{2,1,0:T(8,128)(2,1)S(1)}, bf16[4,8,4096]{2,1,0:T(8,128)(2,1)S(1)}, u32[]{:S(2)}, u32[]{:S(2)}) collective-permute-start(bf16[4,8,4096]{2,1,0:T(8,128)(2,1)S(1)} %z_pieces.2.mine), channel_id=1, source_target_pairs={{0,64},{1,65},{2,66},{3,67},{4,68},{5,69},{6,70},{7,71},{8,72},{9,... | collective-permute-start | bytes 786440 | tf_op jit(solution)/shard_map/ppermute | solution.py:58
  43.2 1.2 %collective-permute-done.8.theirs = bf16[4,8,4096]{2,1,0:T(8,128)(2,1)S(1)} collective-permute-done((bf16[4,8,4096]{2,1,0:T(8,128)(2,1)S(1)}, bf16[4,8,4096]{2,1,0:T(8,128)(2,1)S(1)}, u32[]{:S(2)}, u32[]{:S(2)}) %collective-permute-start.8) | collective-permute-done | bytes 262176 | tf_op jit(solution)/shard_map/ppermute | solution.py:58
  44.3 0.1 join.2.refs_1_
  44.4 0.0 collective-permute-done.16.second
  44.4 0.8 collective-permute-done.15.array.first
  45.2 0.1 pair.2.refs_2_
  45.2 0.1 collective-permute-start.21
  45.3 0.2 collective-permute-start.17
  45.5 3.4 %collective-permute-start.10 = (bf16[4,8,8192]{2,1,0:T(8,128)(2,1)S(1)}, bf16[4,8,8192]{2,1,0:T(8,128)(2,1)S(1)}, u32[]{:S(2)}, u32[]{:S(2)}) collective-permute-start(bf16[4,8,8192]{2,1,0:T(8,128)(2,1)S(1)} %join.2.refs_1_), channel_id=1, source_target_pairs={{0,160},{1,161},{2,162},{3,163},{4,164},{5,165},{6,166},{7,167},{8... | collective-permute-start | bytes 1572872 | tf_op jit(solution)/shard_map/ppermute | solution.py:58
  49.0 1.1 %collective-permute-start.9 = (bf16[4,8,8192]{2,1,0:T(8,128)(2,1)S(1)}, bf16[4,8,8192]{2,1,0:T(8,128)(2,1)S(1)}, u32[]{:S(2)}, u32[]{:S(2)}) collective-permute-start(bf16[4,8,8192]{2,1,0:T(8,128)(2,1)S(1)} %join.2.refs_1_), channel_id=1, source_target_pairs={{0,8},{1,9},{2,10},{3,11},{4,12},{5,13},{6,14},{7,15},{8,16},{9,17... | collective-permute-start | bytes 1572872 | tf_op jit(solution)/shard_map/ppermute | solution.py:58
  50.0 1.3 %collective-permute-done.3.theirs = f32[8,4096]{1,0:T(8,128)S(1)} collective-permute-done((f32[8,4096]{1,0:T(8,128)S(1)}, f32[8,4096]{1,0:T(8,128)S(1)}, u32[]{:S(2)}, u32[]{:S(2)}) %collective-permute-start.3) | collective-permute-done | bytes 131104 | tf_op jit(solution)/shard_map/ppermute | solution.py:58
  51.4 0.4 collective-permute-start.18
  51.8 0.9 %whole_step.1 = (f32[8,8192]{1,0:T(8,128)}, f32[8,8192]{1,0:T(8,128)}, f32[8,128]{1,0:T(8,128)S(1)}) custom-call(f32[8,4096]{1,0:T(8,128)S(1)} %get-tuple-element.26.mine, f32[8,4096]{1,0:T(8,128)S(1)} %collective-permute-done.3.theirs, f32[8,8192]{1,0:T(8,128)S(1)} %get-tuple-element.25.base, f32[8,8192]{1,0:T(8,128)S(1)} %broadcast_multiply_fusion.decayed), custom_call_target="tpu_custom_call" | custom-call | flops 1048576 | bytes 1048576 | tf_op jit(solution)/shard_map/whole_step/pallas_call | solution.py:188
  52.6 1.3 %assemble.4 = (bf16[8,8,8,8192]{3,2,1,0:T(8,128)(2,1)}, f32[8,128]{1,0:T(8,128)S(1)}) custom-call(bf16[4,8,8192]{2,1,0:T(8,128)(2,1)S(1)} %join.3.refs_0_, bf16[4,8,8192]{2,1,0:T(8,128)(2,1)S(1)} %join.2.refs_1_, bf16[2,4,8,8192]{3,2,1,0:T(8,128)(2,1)S(1)} %pair.2.refs_2_), custom_call_target="tpu_custom_call" | custom-call | flops 4194304 | bytes 4194304 | tf_op jit(solution)/shard_map/assemble/pallas_call | solution.py:207
  54.0 7.3 %collective-permute-done.18.second = bf16[2,8,8192]{2,1,0:T(8,128)(2,1)S(1)} collective-permute-done((bf16[2,8,8192]{2,1,0:T(8,128)(2,1)S(1)}, bf16[2,8,8192]{2,1,0:T(8,128)(2,1)S(1)}, u32[]{:S(2)}, u32[]{:S(2)}) %collective-permute-start.18) | collective-permute-done | bytes 262176 | tf_op jit(solution)/shard_map/ppermute | solution.py:58
  61.3 0.0 collective-permute-done.17.first
  61.3 0.1 append.2.refs_2_
  61.3 0.0 collective-permute-done.10.second
  61.3 6.0 %collective-permute-done.9.array.first = bf16[4,8,8192]{2,1,0:T(8,128)(2,1)S(1)} collective-permute-done((bf16[4,8,8192]{2,1,0:T(8,128)(2,1)S(1)}, bf16[4,8,8192]{2,1,0:T(8,128)(2,1)S(1)}, u32[]{:S(2)}, u32[]{:S(2)}) %collective-permute-start.9) | collective-permute-done | bytes 524320 | tf_op jit(solution)/shard_map/ppermute | solution.py:58
  67.4 3.2 %collective-permute-start.19 = (bf16[4,8,8192]{2,1,0:T(8,128)(2,1)S(1)}, bf16[4,8,8192]{2,1,0:T(8,128)(2,1)S(1)}, u32[]{:S(2)}, u32[]{:S(2)}) collective-permute-start(bf16[4,8,8192]{2,1,0:T(8,128)(2,1)S(1)} %collective-permute-done.10.second), channel_id=1, source_target_pairs={{0,8},{1,9},{2,10},{3,11},{4,12},{5,13},{6,14},{7,15},{8,16},{9,17... | collective-permute-start | bytes 1572872 | tf_op jit(solution)/shard_map/ppermute | solution.py:58
  70.6 0.1 pair.3.refs_1_
  70.7 0.1 collective-permute-start.24
  70.8 1.6 %collective-permute-start.20 = (bf16[2,8,8192]{2,1,0:T(8,128)(2,1)S(1)}, bf16[2,8,8192]{2,1,0:T(8,128)(2,1)S(1)}, u32[]{:S(2)}, u32[]{:S(2)}) collective-permute-start(bf16[2,8,8192]{2,1,0:T(8,128)(2,1)S(1)} %cut.3), channel_id=1, source_target_pairs={{0,8},{1,9},{2,10},{3,11},{4,12},{5,13},{6,14},{7,15},{8,16},{9,17... | collective-permute-start | bytes 786440 | tf_op jit(solution)/shard_map/ppermute | solution.py:58
  72.4 0.0 collective-permute-start.23
  72.4 0.0 collective-permute-done.21.refs_0_
  72.4 1.6 %assemble.5 = (bf16[8,8,8,8192]{3,2,1,0:T(8,128)(2,1)}, f32[8,128]{1,0:T(8,128)S(1)}) custom-call(bf16[2,4,8,8192]{3,2,1,0:T(8,128)(2,1)S(1)} %collective-permute-done.21.refs_0_, bf16[2,4,8,8192]{3,2,1,0:T(8,128)(2,1)S(1)} %pair.3.refs_1_, bf16[6,8,8192]{2,1,0:T(8,128)(2,1)S(1)} %append.2.refs_2_, ...), custom_call_target="tpu_custom_call", output_to_operand_aliasing={{0}: (3, {})} | custom-call | flops 5767168 | bytes 5767168 | tf_op jit(solution)/shard_map/assemble/pallas_call | solution.py:207
  74.1 5.5 %collective-permute-done.20.second = bf16[2,8,8192]{2,1,0:T(8,128)(2,1)S(1)} collective-permute-done((bf16[2,8,8192]{2,1,0:T(8,128)(2,1)S(1)}, bf16[2,8,8192]{2,1,0:T(8,128)(2,1)S(1)}, u32[]{:S(2)}, u32[]{:S(2)}) %collective-permute-start.20) | collective-permute-done | bytes 262176 | tf_op jit(solution)/shard_map/ppermute | solution.py:58
  79.5 0.0 collective-permute-done.19.first
  79.5 0.1 append.3.refs_2_
  79.6 3.0 %collective-permute-start.22 = (bf16[6,8,8192]{2,1,0:T(8,128)(2,1)S(1)}, bf16[6,8,8192]{2,1,0:T(8,128)(2,1)S(1)}, u32[]{:S(2)}, u32[]{:S(2)}) collective-permute-start(bf16[6,8,8192]{2,1,0:T(8,128)(2,1)S(1)} %append.3.refs_2_), channel_id=1, source_target_pairs={{0,64},{1,65},{2,66},{3,67},{4,68},{5,69},{6,70},{7,71},{8,72},{9,... | collective-permute-start | bytes 2359304 | tf_op jit(solution)/shard_map/ppermute | solution.py:58
  82.6 0.0 collective-permute-done.23.refs_0_
  82.6 0.0 collective-permute-done.24.refs_1_
  82.6 2.1 %assemble.6 = (bf16[8,8,8,8192]{3,2,1,0:T(8,128)(2,1)}, f32[8,128]{1,0:T(8,128)}) custom-call(bf16[6,8,8192]{2,1,0:T(8,128)(2,1)S(1)} %collective-permute-done.23.refs_0_, bf16[2,4,8,8192]{3,2,1,0:T(8,128)(2,1)S(1)} %collective-permute-done.24.refs_1_, bf16[6,8,8192]{2,1,0:T(8,128)(2,1)S(1)} %append.3.refs_2_, ...), custom_call_target="tpu_custom_call", output_to_operand_aliasing={{0}: (3, {})} | custom-call | flops 5242880 | bytes 5242880 | tf_op jit(solution)/shard_map/assemble/pallas_call | solution.py:207
  84.7 1.5 %assemble.7 = (bf16[8,8,8,8192]{3,2,1,0:T(8,128)(2,1)}, f32[8,128]{1,0:T(8,128)}) custom-call(bf16[6,8,8192]{2,1,0:T(8,128)(2,1)S(1)} %collective-permute-done.22.refs_0_, bf16[8,8,8,8192]{3,2,1,0:T(8,128)(2,1)} %get-tuple-element.41.refs_1_), custom_call_target="tpu_custom_call", output_to_operand_aliasing={{0}: (1, {})} | custom-call | flops 1572864 | bytes 1572864 | tf_op jit(solution)/shard_map/assemble/pallas_call | solution.py:207
  (8 shorter events, 0.1 us)
Async XLA Ops:
  0.6 1.0 %copy-start = (f32[8,8192]{1,0:T(8,128)S(1)}, f32[8,8192]{1,0:T(8,128)}, u32[]{:S(2)}) copy-start(f32[8,8192]{1,0:T(8,128)} %base.1) | copy-start | bytes 786436
  1.6 0.9 %copy-start.1 = (bf16[1,8,8192]{2,1,0:T(8,128)(2,1)S(1)}, bf16[1,8,8192]{2,1,0:T(8,128)(2,1)}, u32[]{:S(2)}) copy-start(bf16[1,8,8192]{2,1,0:T(8,128)(2,1)} %weights.1) | copy-start | bytes 393220
  2.7 8.0 %collective-permute-start.2 = (bf16[8,4096]{1,0:T(8,128)(2,1)S(1)}, bf16[8,4096]{1,0:T(8,128)(2,1)S(1)}, u32[]{:S(2)}, u32[]{:S(2)}) collective-permute-start(bf16[8,4096]{1,0:T(8,128)(2,1)S(1)} %get-tuple-element.24), channel_id=1, source_target_pairs={{0,192},{1,193},{2,194},{3,195},{4,196},{5,197},{6,198},{7,199},{8... | collective-permute-start | bytes 196616 | tf_op jit(solution)/shard_map/ppermute | solution.py:58
  5.4 5.3 %collective-permute-start = (bf16[8,4096]{1,0:T(8,128)(2,1)S(1)}, bf16[8,4096]{1,0:T(8,128)(2,1)S(1)}, u32[]{:S(2)}, u32[]{:S(2)}) collective-permute-start(bf16[8,4096]{1,0:T(8,128)(2,1)S(1)} %get-tuple-element.24), channel_id=1, source_target_pairs={{0,64},{1,65},{2,66},{3,67},{4,68},{5,69},{6,70},{7,71},{8,72},{9,... | collective-permute-start | bytes 196616 | tf_op jit(solution)/shard_map/ppermute | solution.py:58
  6.1 4.6 %collective-permute-start.1 = (bf16[8,4096]{1,0:T(8,128)(2,1)S(1)}, bf16[8,4096]{1,0:T(8,128)(2,1)S(1)}, u32[]{:S(2)}, u32[]{:S(2)}) collective-permute-start(bf16[8,4096]{1,0:T(8,128)(2,1)S(1)} %get-tuple-element.23.keep), channel_id=1, source_target_pairs={{0,128},{1,129},{2,130},{3,131},{4,132},{5,133},{6,134},{7,135},{8... | collective-permute-start | bytes 196616 | tf_op jit(solution)/shard_map/ppermute | solution.py:58
  10.7 8.6 %collective-permute-start.13 = (bf16[8,4096]{1,0:T(8,128)(2,1)S(1)}, bf16[8,4096]{1,0:T(8,128)(2,1)S(1)}, u32[]{:S(2)}, u32[]{:S(2)}) collective-permute-start(bf16[8,4096]{1,0:T(8,128)(2,1)S(1)} %get-tuple-element.29.refs_0_), channel_id=1, source_target_pairs={{0,3},{1,2},{2,1},{3,0},{4,7},{5,6},{6,5},{7,4},{8,11},{9,10},{10,... | collective-permute-start | bytes 196616 | tf_op jit(solution)/shard_map/ppermute | solution.py:58
  13.2 6.1 %collective-permute-start.12 = (bf16[8,4096]{1,0:T(8,128)(2,1)S(1)}, bf16[8,4096]{1,0:T(8,128)(2,1)S(1)}, u32[]{:S(2)}, u32[]{:S(2)}) collective-permute-start(bf16[8,4096]{1,0:T(8,128)(2,1)S(1)} %get-tuple-element.29.refs_0_), channel_id=1, source_target_pairs={{0,2},{1,3},{2,0},{3,1},{4,6},{5,7},{6,4},{7,5},{8,10},{9,11},{10,... | collective-permute-start | bytes 196616 | tf_op jit(solution)/shard_map/ppermute | solution.py:58
  13.2 6.1 %collective-permute-start.11 = (bf16[8,4096]{1,0:T(8,128)(2,1)S(1)}, bf16[8,4096]{1,0:T(8,128)(2,1)S(1)}, u32[]{:S(2)}, u32[]{:S(2)}) collective-permute-start(bf16[8,4096]{1,0:T(8,128)(2,1)S(1)} %get-tuple-element.29.refs_0_), channel_id=1, source_target_pairs={{0,1},{1,0},{2,3},{3,2},{4,5},{5,4},{6,7},{7,6},{8,9},{9,8},{10,11... | collective-permute-start | bytes 196616 | tf_op jit(solution)/shard_map/ppermute | solution.py:58
  14.4 8.7 %collective-permute-start.4 = (bf16[8,4096]{1,0:T(8,128)(2,1)S(1)}, bf16[8,4096]{1,0:T(8,128)(2,1)S(1)}, u32[]{:S(2)}, u32[]{:S(2)}) collective-permute-start(bf16[8,4096]{1,0:T(8,128)(2,1)S(1)} %get-tuple-element.29.refs_0_), channel_id=1, source_target_pairs={{0,4},{1,5},{2,6},{3,7},{4,0},{5,1},{6,2},{7,3},{8,12},{9,13},{10,... | collective-permute-start | bytes 196616 | tf_op jit(solution)/shard_map/ppermute | solution.py:58
  23.1 4.2 %collective-permute-start.14 = (bf16[4,8,4096]{2,1,0:T(8,128)(2,1)S(1)}, bf16[4,8,4096]{2,1,0:T(8,128)(2,1)S(1)}, u32[]{:S(2)}, u32[]{:S(2)}) collective-permute-start(bf16[4,8,4096]{2,1,0:T(8,128)(2,1)S(1)} %z_pieces.3.mine), channel_id=1, source_target_pairs={{0,64},{1,65},{2,66},{3,67},{4,68},{5,69},{6,70},{7,71},{8,72},{9,... | collective-permute-start | bytes 786440 | tf_op jit(solution)/shard_map/ppermute | solution.py:58
  27.3 17.1 %collective-permute-start.16 = (bf16[4,8,8192]{2,1,0:T(8,128)(2,1)S(1)}, bf16[4,8,8192]{2,1,0:T(8,128)(2,1)S(1)}, u32[]{:S(2)}, u32[]{:S(2)}) collective-permute-start(bf16[4,8,8192]{2,1,0:T(8,128)(2,1)S(1)} %join.3.refs_0_), channel_id=1, source_target_pairs={{0,160},{1,161},{2,162},{3,163},{4,164},{5,165},{6,166},{7,167},{8... | collective-permute-start | bytes 1572872 | tf_op jit(solution)/shard_map/ppermute | solution.py:58
  31.2 14.0 %collective-permute-start.15 = (bf16[4,8,8192]{2,1,0:T(8,128)(2,1)S(1)}, bf16[4,8,8192]{2,1,0:T(8,128)(2,1)S(1)}, u32[]{:S(2)}, u32[]{:S(2)}) collective-permute-start(bf16[4,8,8192]{2,1,0:T(8,128)(2,1)S(1)} %join.3.refs_0_), channel_id=1, source_target_pairs={{0,24},{1,25},{2,26},{3,27},{4,28},{5,29},{6,30},{7,31},{8,0},{9,1... | collective-permute-start | bytes 1572872 | tf_op jit(solution)/shard_map/ppermute | solution.py:58
  32.5 5.0 %collective-permute-start.7 = (bf16[8,4096]{1,0:T(8,128)(2,1)S(1)}, bf16[8,4096]{1,0:T(8,128)(2,1)S(1)}, u32[]{:S(2)}, u32[]{:S(2)}) collective-permute-start(bf16[8,4096]{1,0:T(8,128)(2,1)S(1)} %collective-permute-done.4.refs_0_.refs_4_), channel_id=1, source_target_pairs={{0,3},{1,2},{2,1},{3,0},{4,7},{5,6},{6,5},{7,4},{8,11},{9,10},{10,... | collective-permute-start | bytes 196616 | tf_op jit(solution)/shard_map/ppermute | solution.py:58
  34.1 6.5 %collective-permute-start.6 = (bf16[8,4096]{1,0:T(8,128)(2,1)S(1)}, bf16[8,4096]{1,0:T(8,128)(2,1)S(1)}, u32[]{:S(2)}, u32[]{:S(2)}) collective-permute-start(bf16[8,4096]{1,0:T(8,128)(2,1)S(1)} %collective-permute-done.4.refs_0_.refs_4_), channel_id=1, source_target_pairs={{0,2},{1,3},{2,0},{3,1},{4,6},{5,7},{6,4},{7,5},{8,10},{9,11},{10,... | collective-permute-start | bytes 196616 | tf_op jit(solution)/shard_map/ppermute | solution.py:58
  36.0 4.7 %collective-permute-start.5 = (bf16[8,4096]{1,0:T(8,128)(2,1)S(1)}, bf16[8,4096]{1,0:T(8,128)(2,1)S(1)}, u32[]{:S(2)}, u32[]{:S(2)}) collective-permute-start(bf16[8,4096]{1,0:T(8,128)(2,1)S(1)} %collective-permute-done.4.refs_0_.refs_4_), channel_id=1, source_target_pairs={{0,1},{1,0},{2,3},{3,2},{4,5},{5,4},{6,7},{7,6},{8,9},{9,8},{10,11... | collective-permute-start | bytes 196616 | tf_op jit(solution)/shard_map/ppermute | solution.py:58
  40.7 3.6 %collective-permute-start.8 = (bf16[4,8,4096]{2,1,0:T(8,128)(2,1)S(1)}, bf16[4,8,4096]{2,1,0:T(8,128)(2,1)S(1)}, u32[]{:S(2)}, u32[]{:S(2)}) collective-permute-start(bf16[4,8,4096]{2,1,0:T(8,128)(2,1)S(1)} %z_pieces.2.mine), channel_id=1, source_target_pairs={{0,64},{1,65},{2,66},{3,67},{4,68},{5,69},{6,70},{7,71},{8,72},{9,... | collective-permute-start | bytes 786440 | tf_op jit(solution)/shard_map/ppermute | solution.py:58
  45.2 27.2 %collective-permute-start.21 = (bf16[2,4,8,8192]{3,2,1,0:T(8,128)(2,1)S(1)}, bf16[2,4,8,8192]{3,2,1,0:T(8,128)(2,1)S(1)}, u32[]{:S(2)}, u32[]{:S(2)}) collective-permute-start(bf16[2,4,8,8192]{3,2,1,0:T(8,128)(2,1)S(1)} %pair.2.refs_2_), channel_id=1, source_target_pairs={{0,64},{1,65},{2,66},{3,67},{4,68},{5,69},{6,70},{7,71},{8,72},{9,... | collective-permute-start | bytes 3145736 | tf_op jit(solution)/shard_map/ppermute | solution.py:58
  45.3 15.9 %collective-permute-start.17 = (bf16[4,8,8192]{2,1,0:T(8,128)(2,1)S(1)}, bf16[4,8,8192]{2,1,0:T(8,128)(2,1)S(1)}, u32[]{:S(2)}, u32[]{:S(2)}) collective-permute-start(bf16[4,8,8192]{2,1,0:T(8,128)(2,1)S(1)} %collective-permute-done.16.second), channel_id=1, source_target_pairs={{0,24},{1,25},{2,26},{3,27},{4,28},{5,29},{6,30},{7,31},{8,0},{9,1... | collective-permute-start | bytes 1572872 | tf_op jit(solution)/shard_map/ppermute | solution.py:58
  45.5 15.8 %collective-permute-start.10 = (bf16[4,8,8192]{2,1,0:T(8,128)(2,1)S(1)}, bf16[4,8,8192]{2,1,0:T(8,128)(2,1)S(1)}, u32[]{:S(2)}, u32[]{:S(2)}) collective-permute-start(bf16[4,8,8192]{2,1,0:T(8,128)(2,1)S(1)} %join.2.refs_1_), channel_id=1, source_target_pairs={{0,160},{1,161},{2,162},{3,163},{4,164},{5,165},{6,166},{7,167},{8... | collective-permute-start | bytes 1572872 | tf_op jit(solution)/shard_map/ppermute | solution.py:58
  49.0 18.4 %collective-permute-start.9 = (bf16[4,8,8192]{2,1,0:T(8,128)(2,1)S(1)}, bf16[4,8,8192]{2,1,0:T(8,128)(2,1)S(1)}, u32[]{:S(2)}, u32[]{:S(2)}) collective-permute-start(bf16[4,8,8192]{2,1,0:T(8,128)(2,1)S(1)} %join.2.refs_1_), channel_id=1, source_target_pairs={{0,8},{1,9},{2,10},{3,11},{4,12},{5,13},{6,14},{7,15},{8,16},{9,17... | collective-permute-start | bytes 1572872 | tf_op jit(solution)/shard_map/ppermute | solution.py:58
  50.0 1.3 %collective-permute-start.3 = (f32[8,4096]{1,0:T(8,128)S(1)}, f32[8,4096]{1,0:T(8,128)S(1)}, u32[]{:S(2)}, u32[]{:S(2)}) collective-permute-start(f32[8,4096]{1,0:T(8,128)S(1)} %get-tuple-element.26.mine), channel_id=1, source_target_pairs={{0,64},{1,65},{2,66},{3,67},{4,68},{5,69},{6,70},{7,71},{8,72},{9,... | collective-permute-start | bytes 393224 | tf_op jit(solution)/shard_map/ppermute | solution.py:58
  51.4 9.9 %collective-permute-start.18 = (bf16[2,8,8192]{2,1,0:T(8,128)(2,1)S(1)}, bf16[2,8,8192]{2,1,0:T(8,128)(2,1)S(1)}, u32[]{:S(2)}, u32[]{:S(2)}) collective-permute-start(bf16[2,8,8192]{2,1,0:T(8,128)(2,1)S(1)} %cut.2), channel_id=1, source_target_pairs={{0,24},{1,25},{2,26},{3,27},{4,28},{5,29},{6,30},{7,31},{8,0},{9,1... | collective-permute-start | bytes 786440 | tf_op jit(solution)/shard_map/ppermute | solution.py:58
  67.4 12.2 %collective-permute-start.19 = (bf16[4,8,8192]{2,1,0:T(8,128)(2,1)S(1)}, bf16[4,8,8192]{2,1,0:T(8,128)(2,1)S(1)}, u32[]{:S(2)}, u32[]{:S(2)}) collective-permute-start(bf16[4,8,8192]{2,1,0:T(8,128)(2,1)S(1)} %collective-permute-done.10.second), channel_id=1, source_target_pairs={{0,8},{1,9},{2,10},{3,11},{4,12},{5,13},{6,14},{7,15},{8,16},{9,17... | collective-permute-start | bytes 1572872 | tf_op jit(solution)/shard_map/ppermute | solution.py:58
  70.7 11.9 %collective-permute-start.24 = (bf16[2,4,8,8192]{3,2,1,0:T(8,128)(2,1)S(1)}, bf16[2,4,8,8192]{3,2,1,0:T(8,128)(2,1)S(1)}, u32[]{:S(2)}, u32[]{:S(2)}) collective-permute-start(bf16[2,4,8,8192]{3,2,1,0:T(8,128)(2,1)S(1)} %pair.3.refs_1_), channel_id=1, source_target_pairs={{0,64},{1,65},{2,66},{3,67},{4,68},{5,69},{6,70},{7,71},{8,72},{9,... | collective-permute-start | bytes 3145736 | tf_op jit(solution)/shard_map/ppermute | solution.py:58
  70.8 8.7 %collective-permute-start.20 = (bf16[2,8,8192]{2,1,0:T(8,128)(2,1)S(1)}, bf16[2,8,8192]{2,1,0:T(8,128)(2,1)S(1)}, u32[]{:S(2)}, u32[]{:S(2)}) collective-permute-start(bf16[2,8,8192]{2,1,0:T(8,128)(2,1)S(1)} %cut.3), channel_id=1, source_target_pairs={{0,8},{1,9},{2,10},{3,11},{4,12},{5,13},{6,14},{7,15},{8,16},{9,17... | collective-permute-start | bytes 786440 | tf_op jit(solution)/shard_map/ppermute | solution.py:58
  72.4 10.1 %collective-permute-start.23 = (bf16[6,8,8192]{2,1,0:T(8,128)(2,1)S(1)}, bf16[6,8,8192]{2,1,0:T(8,128)(2,1)S(1)}, u32[]{:S(2)}, u32[]{:S(2)}) collective-permute-start(bf16[6,8,8192]{2,1,0:T(8,128)(2,1)S(1)} %append.2.refs_2_), channel_id=1, source_target_pairs={{0,64},{1,65},{2,66},{3,67},{4,68},{5,69},{6,70},{7,71},{8,72},{9,... | collective-permute-start | bytes 2359304 | tf_op jit(solution)/shard_map/ppermute | solution.py:58
  79.6 5.1 %collective-permute-start.22 = (bf16[6,8,8192]{2,1,0:T(8,128)(2,1)S(1)}, bf16[6,8,8192]{2,1,0:T(8,128)(2,1)S(1)}, u32[]{:S(2)}, u32[]{:S(2)}) collective-permute-start(bf16[6,8,8192]{2,1,0:T(8,128)(2,1)S(1)} %append.3.refs_2_), channel_id=1, source_target_pairs={{0,64},{1,65},{2,66},{3,67},{4,68},{5,69},{6,70},{7,71},{8,72},{9,... | collective-permute-start | bytes 2359304 | tf_op jit(solution)/shard_map/ppermute | solution.py:58

commit v4 on v3

v4 whole, which is shorter than its diff:
```python
import functools

import jax
import jax.numpy as jnp
from jax import lax
from jax.experimental import pallas as pl
from jax.experimental.pallas import tpu as pltpu
from jax.sharding import PartitionSpec as P

BLOCK = 128

epsilon = 1e-06
code_limit = 31.0
momentum_decay = 0.9
outer_rate = 0.7

AXES = ("island", "fsdp")
HALF = 4096
ROWS = 8
PARTS = ((0, 3), (3, 3), (6, 2))


def all_places():
    for x_lo in range(2):
        for core in range(2):
            for x_hi in range(2):
                for y in range(4):
                    for z in range(8):
                        yield x_lo, core, x_hi, y, z


def number(place):
    x_lo, core, x_hi, y, z = place
    return (x_lo * 2 + core) * 64 + (x_hi * 4 + y % 4) * 8 + z


def pairs(target):
    return [(number(p), number(target(*p))) for p in all_places()]


OTHER_CORE = pairs(lambda x_lo, core, x_hi, y, z: (x_lo, 1 - core, x_hi, y, z))
OTHER_CHIP = pairs(lambda x_lo, core, x_hi, y, z: (1 - x_lo, core, x_hi, y, z))
OTHER_BOTH = pairs(lambda x_lo, core, x_hi, y, z: (1 - x_lo, 1 - core, x_hi, y, z))


def from_z(step):
    return pairs(lambda x_lo, core, x_hi, y, z: (x_lo, core, x_hi, y, (z - step) % 8))


FROM_PAIR = pairs(lambda x_lo, core, x_hi, y, z: (x_lo, core, x_hi, y, z ^ 1))


def from_y(step):
    return pairs(lambda x_lo, core, x_hi, y, z: (x_lo, core, x_hi, y - step, z))


FROM_X = pairs(lambda x_lo, core, x_hi, y, z: (1 - x_lo, core, 1 - x_hi, y, z))


def send(x, to):
    return lax.ppermute(x, AXES, to)


def my_core():
    return lax.rem(lax.axis_index("island"), 2)


def my_z():
    return lax.rem(lax.axis_index("fsdp"), 8)


def my_y():
    return lax.rem(lax.div(lax.axis_index("fsdp"), 8), 4)


def my_x_hi():
    return lax.div(lax.axis_index("fsdp"), 32)


def encode_kernel(weights, base, keep, give, base_near):
    core = my_core()
    for out, half in ((keep, core), (give, 1 - core)):
        for block in range(HALF // BLOCK):
            at = pl.multiple_of(half * HALF + block * BLOCK, BLOCK)
            outer_grad = base[:, pl.ds(at, BLOCK)] - weights[0, :, pl.ds(at, BLOCK)].astype(jnp.float32)
            largest = jnp.max(jnp.abs(outer_grad), axis=1, keepdims=True)
            block_scale = (largest + epsilon) / code_limit
            code_values = (outer_grad / block_scale).astype(jnp.bfloat16)
            decoded = code_values.astype(jnp.float32) * block_scale
            out[:, block * BLOCK:(block + 1) * BLOCK] = decoded.astype(jnp.bfloat16)
    base_near[...] = base[...]


def outer_step(summed, base_rows, decayed_rows):
    averaged = summed * 0.25
    fresh_moment = decayed_rows + averaged
    fresh_master = base_rows - outer_rate * (averaged + momentum_decay * fresh_moment)
    return fresh_master, fresh_moment


def half_step_kernel(keep, from_core, from_chip, from_both, base, decayed, summed, fresh):
    start = pl.multiple_of(my_core() * HALF, HALF)
    f32 = lambda ref: ref[...].astype(jnp.float32)
    total = (f32(keep) + f32(from_core)) + (f32(from_chip) + f32(from_both))
    summed[...] = total
    master, _ = outer_step(total, base[:, pl.ds(start, HALF)], decayed[:, pl.ds(start, HALF)])
    fresh[...] = master.astype(jnp.bfloat16)


def whole_step_kernel(mine, theirs, base, decayed, master_out, moment_out, written):
    written[...] = jnp.zeros_like(written)
    core = my_core()
    for summed, half in ((mine, core), (theirs, 1 - core)):
        start = pl.multiple_of(half * HALF, HALF)
        master, fresh = outer_step(summed[...], base[:, pl.ds(start, HALF)], decayed[:, pl.ds(start, HALF)])
        master_out[:, pl.ds(start, HALF)] = master
        moment_out[:, pl.ds(start, HALF)] = fresh


def pair_kernel(own, other, out):
    out[0], out[1] = own[...], other[...]


def bundle_kernel(*refs):
    *couples, out = refs
    z = my_z()
    for step, couple in zip((0, 2, 4, 6), couples):
        for i in range(2):
            out[pl.ds(lax.rem((z ^ i) + step, 8), 1)] = couple[i][None]


def pack_kernel(count, *refs):
    for i in range(count):
        refs[-1][i] = refs[i][...]


def cut_kernel(up, down, across, *outs):
    for ref, (start, count), out in zip((up, down, across), PARTS, outs):
        out[...] = ref[start:start + count]


def last_kernel(*refs):
    for ref, (start, count) in zip(refs, PARTS):
        refs[-1][start:start + count] = ref[...]


def assemble_kernel(where, *refs):
    *refs, out, written, sems = refs
    core, todo = my_core(), []
    for i, (array, place, theirs, flip, up) in enumerate(where):
        source = refs[array] if place is None else refs[array].at[place]
        block = (my_x_hi() ^ flip) * 4 + lax.rem(my_y() + up, 4)
        start = pl.multiple_of((1 - core if theirs else core) * HALF, HALF)
        todo.append(pltpu.make_async_copy(source, out.at[block, :, :, pl.ds(start, HALF)], sems.at[i]))
    for copy in todo:
        copy.start()
    for copy in todo:
        copy.wait()
    written[...] = jnp.zeros_like(written)


VMEM = pl.BlockSpec(memory_space=pltpu.VMEM)
ANY = pl.BlockSpec(memory_space=pl.ANY)


def shape(dims, kind):
    return jax.ShapeDtypeStruct(dims, kind)


def hints(moved, scratch):
    return {
        "cost_estimate": pl.CostEstimate(flops=moved, bytes_accessed=moved, transcendentals=0),
        "compiler_params": pltpu.CompilerParams(vmem_limit_bytes=scratch),
    }


def local(kernel, outs, given, scratch=(), grant=4 << 20, name=None, **more):
    return pl.pallas_call(
        kernel,
        out_shape=tuple(shape(*out) for out in outs),
        in_specs=more.pop("in_specs", [VMEM] * len(given)),
        out_specs=(VMEM,) * len(outs),
        scratch_shapes=scratch,
        name=name,
        **hints(1 << 20, grant),
    )(*given)


def assemble(given, out=None):
    where = []
    for array, (_, theirs, places) in enumerate(given):
        packed = isinstance(places, list)
        where.extend((array, i if packed else None, theirs, *at) for i, at in enumerate(places if packed else [places]))
    given = [array for array, _, _ in given] + ([] if out is None else [out])
    return pl.pallas_call(
        functools.partial(assemble_kernel, where),
        out_shape=(shape((8, 8, ROWS, 2 * HALF), jnp.bfloat16), shape((8, 128), jnp.float32)),
        in_specs=[ANY] * len(given),
        out_specs=(ANY, VMEM),
        scratch_shapes=[pltpu.SemaphoreType.DMA((len(where),))],
        input_output_aliases={} if out is None else {len(given) - 1: 0},
        name="assemble",
        **hints(len(where) << 20, 1 << 20),
    )(*given)


def on_device(local_weights, base_in, moment_in):
    bf16, f32 = jnp.bfloat16, jnp.float32
    half, whole = (ROWS, HALF), (ROWS, 2 * HALF)
    keep, give, base = local(
        encode_kernel, [(half, bf16), (half, bf16), (whole, f32)], (local_weights, base_in), name="encode",
    )
    decayed = momentum_decay * moment_in
    from_both, from_chip, from_core = send(give, OTHER_BOTH), send(keep, OTHER_CHIP), send(give, OTHER_CORE)
    summed, fresh = local(
        half_step_kernel, [(half, f32), (half, bf16)],
        (keep, from_core, from_chip, from_both, base, decayed), name="half_step",
    )

    theirs_summed = send(summed, OTHER_CORE)
    master, fresh_moment, stepped = local(
        whole_step_kernel, [(whole, f32)] * 2 + [((8, 128), f32)], (summed, theirs_summed, base, decayed), name="whole_step",
    )

    def swap(x):
        return send(x, OTHER_CORE)

    def pack(arrays, after):
        return local(
            functools.partial(pack_kernel, len(arrays)), [((len(arrays), *bundle.shape), bf16)], [*arrays, *after],
            name="pack", grant=1 << 20, in_specs=[VMEM] * len(arrays) + [ANY] * len(after),
        )[0]

    couple, = local(pair_kernel, [((2, *half), bf16)], (fresh, send(fresh, FROM_PAIR)), name="couple")
    couples = [couple] + [send(couple, from_z(step)) for step in (2, 4, 6)]
    bundle, = local(bundle_kernel, [((8, *half), bf16)], couples, name="bundle")
    up, down, across = send(bundle, from_y(1)), send(bundle, from_y(-1)), send(bundle, FROM_X)
    up_up, down_across, up_across = send(up, from_y(1)), send(across, from_y(-1)), send(up, FROM_X)
    cuts = local(
        cut_kernel, [((count, *half), bf16) for _, count in PARTS], (up_across, down_across, up_up), name="cut",
    )
    parts = [send(x, to) for x, to in zip(cuts, (from_y(1), from_y(-1), FROM_X))]

    first_places, second_places = [(0, 1), (0, 3), (1, 0)], [(0, 2), (1, 3), (1, 1)]
    their_bundle = swap(bundle)
    first = pack((up, down, across), (stepped,))
    their_first = swap(first)
    out, written = assemble([(bundle, False, (0, 0)), (their_bundle, True, (0, 0)), (first, False, first_places)])
    second = pack((up_up, down_across, up_across), (written,))
    their_second = swap(second)
    out, written = assemble(
        [(their_first, True, first_places), (second, False, second_places), (their_second, True, second_places)], out,
    )
    last, = local(
        last_kernel, [((8, *half), bf16)], [*parts, written], name="last", grant=1 << 20, in_specs=[VMEM] * 3 + [ANY],
    )
    out, _ = assemble([(last, False, (1, 2)), (swap(last), True, (1, 2))], out)
    return master, fresh_moment, out.reshape(512, 2 * HALF)


def solution(mesh):
    return jax.shard_map(
        on_device,
        mesh=mesh,
        in_specs=(P("island", "fsdp", None), P("fsdp", None), P("fsdp", None)),
        out_specs=(P("fsdp", None), P("fsdp", None), P()),
        check_vma=False,
    )
```

time: 86.6 us -> 79.4 us (0.917)
  starting transfers between devices: 40.6 us -> 32.4 us
  waiting for transfers between devices: 33.9 us -> 36.5 us
  Pallas kernels: 8.17 us -> 6.8 us
    ppermute x25 -> x21, starting transfers between devices: 40.6 us -> 32.4 us  [send(): return lax.ppermute(x, AXES, to)]
    ppermute x25 -> x21, waiting for transfers between devices: 33.9 us -> 36.5 us  [send(): return lax.ppermute(x, AXES, to)]
    pallas_call x4 -> x3, Pallas kernels: 6.6 us -> 5.35 us  [assemble(): pl.pallas_call(functools.partial(assemble_kernel, where), out_shape=(shap...]
  transfers between devices with their start and end apart: 25 -> 21, of which waited for: 11 -> 12; matrix products, arithmetic and copies ran while one was open for 1% -> 1% of each run, Pallas kernels for 7% -> 6%
where the time goes in v4:
time: 79.4 us; the launch traced here: 79.3 us
  waiting for transfers between devices  36.5 us (46%)
  starting transfers between devices  32.4 us (41%)
  Pallas kernels  6.8 us (9%)
  local copies, waits for them, and re-layouts  1.85 us (2%)
  other arithmetic  0.97 us (1%)
    ppermute x21, waiting for transfers between devices, send(): return lax.ppermute(x, AXES, to)  36.5 us
    ppermute x21, starting transfers between devices, send(): return lax.ppermute(x, AXES, to)  32.4 us
    pallas_call x3, Pallas kernels, assemble(): pl.pallas_call(functools.partial(assemble_kernel, where), out_shape=(shap...  5.35 us
    unnamed x4, local copies, waits for them, and re-layouts  1.85 us
  transfers between devices with their start and end apart: 21, of which 12 were waited for; matrix products, arithmetic and copies ran while one was open for 1% of the time, Pallas kernels for 6%

profile of v4, /device:TPU:1, one launch (start us, length us, event | category | flops | bytes accessed | tf_op | source)
XLA Modules:
  0.0 79.3 jit_solution(6998601913811728597)
XLA Ops:
  0.6 0.0 copy-start
  0.6 0.9 %copy-done = f32[8,8192]{1,0:T(8,128)S(1)} copy-done((f32[8,8192]{1,0:T(8,128)S(1)}, f32[8,8192]{1,0:T(8,128)}, u32[]{:S(2)}) %copy-start) | copy-done | bytes 262168
  1.6 0.0 copy-start.1
  1.6 0.9 %copy-done.1 = bf16[1,8,8192]{2,1,0:T(8,128)(2,1)S(1)} copy-done((bf16[1,8,8192]{2,1,0:T(8,128)(2,1)S(1)}, bf16[1,8,8192]{2,1,0:T(8,128)(2,1)}, u32[]{:S(2)}) %copy-start.1) | copy-done | bytes 131096
  2.5 0.2 encode.1
  2.7 2.7 %collective-permute-start.2 = (bf16[8,4096]{1,0:T(8,128)(2,1)S(1)}, bf16[8,4096]{1,0:T(8,128)(2,1)S(1)}, u32[]{:S(2)}, u32[]{:S(2)}) collective-permute-start(bf16[8,4096]{1,0:T(8,128)(2,1)S(1)} %get-tuple-element.20), channel_id=1, source_target_pairs={{0,192},{1,193},{2,194},{3,195},{4,196},{5,197},{6,198},{7,199},{8... | collective-permute-start | bytes 196616 | tf_op jit(solution)/shard_map/ppermute | solution.py:61
  5.4 0.7 collective-permute-start
  6.1 1.3 %collective-permute-start.1 = (bf16[8,4096]{1,0:T(8,128)(2,1)S(1)}, bf16[8,4096]{1,0:T(8,128)(2,1)S(1)}, u32[]{:S(2)}, u32[]{:S(2)}) collective-permute-start(bf16[8,4096]{1,0:T(8,128)(2,1)S(1)} %get-tuple-element.19.keep), channel_id=1, source_target_pairs={{0,128},{1,129},{2,130},{3,131},{4,132},{5,133},{6,134},{7,135},{8... | collective-permute-start | bytes 196616 | tf_op jit(solution)/shard_map/ppermute | solution.py:61
  7.4 1.0 %broadcast_multiply_fusion.decayed = f32[8,8192]{1,0:T(8,128)S(1)} fusion(f32[8,8192]{1,0:T(8,128)} %param.5), kind=kLoop, calls=%fused_computation | loop fusion | flops 65536 | bytes 524288 | tf_op jit(solution)/shard_map/mul | solution.py:213
  8.3 2.3 %collective-permute-done.1.from_chip = bf16[8,4096]{1,0:T(8,128)(2,1)S(1)} collective-permute-done((bf16[8,4096]{1,0:T(8,128)(2,1)S(1)}, bf16[8,4096]{1,0:T(8,128)(2,1)S(1)}, u32[]{:S(2)}, u32[]{:S(2)}) %collective-permute-start.1) | collective-permute-done | bytes 65568 | tf_op jit(solution)/shard_map/ppermute | solution.py:61
  10.7 0.0 collective-permute-done.2.from_both
  10.7 0.0 collective-permute-done.from_core
  10.7 0.1 half_step.1
  10.7 0.1 collective-permute-start.4
  10.8 3.1 %collective-permute-done.4.other = bf16[8,4096]{1,0:T(8,128)(2,1)S(1)} collective-permute-done((bf16[8,4096]{1,0:T(8,128)(2,1)S(1)}, bf16[8,4096]{1,0:T(8,128)(2,1)S(1)}, u32[]{:S(2)}, u32[]{:S(2)}) %collective-permute-start.4) | collective-permute-done | bytes 65568 | tf_op jit(solution)/shard_map/ppermute | solution.py:61
  14.0 1.3 %collective-permute-start.7 = (bf16[2,8,4096]{2,1,0:T(8,128)(2,1)S(1)}, bf16[2,8,4096]{2,1,0:T(8,128)(2,1)S(1)}, u32[]{:S(2)}, u32[]{:S(2)}) collective-permute-start(bf16[2,8,4096]{2,1,0:T(8,128)(2,1)S(1)} %couple.1.refs_0_), channel_id=1, source_target_pairs={{0,2},{1,3},{2,4},{3,5},{4,6},{5,7},{6,0},{7,1},{8,10},{9,11},{10,... | collective-permute-start | bytes 393224 | tf_op jit(solution)/shard_map/ppermute | solution.py:61
  15.2 4.9 %collective-permute-start.6 = (bf16[2,8,4096]{2,1,0:T(8,128)(2,1)S(1)}, bf16[2,8,4096]{2,1,0:T(8,128)(2,1)S(1)}, u32[]{:S(2)}, u32[]{:S(2)}) collective-permute-start(bf16[2,8,4096]{2,1,0:T(8,128)(2,1)S(1)} %couple.1.refs_0_), channel_id=1, source_target_pairs={{0,4},{1,5},{2,6},{3,7},{4,0},{5,1},{6,2},{7,3},{8,12},{9,13},{10,... | collective-permute-start | bytes 393224 | tf_op jit(solution)/shard_map/ppermute | solution.py:61
  20.1 2.4 %collective-permute-start.5 = (bf16[2,8,4096]{2,1,0:T(8,128)(2,1)S(1)}, bf16[2,8,4096]{2,1,0:T(8,128)(2,1)S(1)}, u32[]{:S(2)}, u32[]{:S(2)}) collective-permute-start(bf16[2,8,4096]{2,1,0:T(8,128)(2,1)S(1)} %couple.1.refs_0_), channel_id=1, source_target_pairs={{0,6},{1,7},{2,0},{3,1},{4,2},{5,3},{6,4},{7,5},{8,14},{9,15},{10,... | collective-permute-start | bytes 393224 | tf_op jit(solution)/shard_map/ppermute | solution.py:61
  22.5 0.0 collective-permute-done.7.refs_3_
  22.5 4.9 %collective-permute-done.6.refs_2_ = bf16[2,8,4096]{2,1,0:T(8,128)(2,1)S(1)} collective-permute-done((bf16[2,8,4096]{2,1,0:T(8,128)(2,1)S(1)}, bf16[2,8,4096]{2,1,0:T(8,128)(2,1)S(1)}, u32[]{:S(2)}, u32[]{:S(2)}) %collective-permute-start.6) | collective-permute-done | bytes 131104 | tf_op jit(solution)/shard_map/ppermute | solution.py:61
  27.5 3.4 %collective-permute-done.5.refs_1_ = bf16[2,8,4096]{2,1,0:T(8,128)(2,1)S(1)} collective-permute-done((bf16[2,8,4096]{2,1,0:T(8,128)(2,1)S(1)}, bf16[2,8,4096]{2,1,0:T(8,128)(2,1)S(1)}, u32[]{:S(2)}, u32[]{:S(2)}) %collective-permute-start.5) | collective-permute-done | bytes 131104 | tf_op jit(solution)/shard_map/ppermute | solution.py:61
  30.9 3.4 %collective-permute-start.10 = (bf16[8,8,4096]{2,1,0:T(8,128)(2,1)S(1)}, bf16[8,8,4096]{2,1,0:T(8,128)(2,1)S(1)}, u32[]{:S(2)}, u32[]{:S(2)}) collective-permute-start(bf16[8,8,4096]{2,1,0:T(8,128)(2,1)S(1)} %bundle.1.refs_0_), channel_id=1, source_target_pairs={{0,160},{1,161},{2,162},{3,163},{4,164},{5,165},{6,166},{7,167},{8... | collective-permute-start | bytes 1572872 | tf_op jit(solution)/shard_map/ppermute | solution.py:61
  34.3 2.7 %collective-permute-start.8 = (bf16[8,8,4096]{2,1,0:T(8,128)(2,1)S(1)}, bf16[8,8,4096]{2,1,0:T(8,128)(2,1)S(1)}, u32[]{:S(2)}, u32[]{:S(2)}) collective-permute-start(bf16[8,8,4096]{2,1,0:T(8,128)(2,1)S(1)} %bundle.1.refs_0_), channel_id=1, source_target_pairs={{0,24},{1,25},{2,26},{3,27},{4,28},{5,29},{6,30},{7,31},{8,0},{9,1... | collective-permute-start | bytes 1572872 | tf_op jit(solution)/shard_map/ppermute | solution.py:61
  37.0 3.3 %collective-permute-start.3 = (f32[8,4096]{1,0:T(8,128)S(1)}, f32[8,4096]{1,0:T(8,128)S(1)}, u32[]{:S(2)}, u32[]{:S(2)}) collective-permute-start(f32[8,4096]{1,0:T(8,128)S(1)} %get-tuple-element.22.mine), channel_id=1, source_target_pairs={{0,64},{1,65},{2,66},{3,67},{4,68},{5,69},{6,70},{7,71},{8,72},{9,... | collective-permute-start | bytes 393224 | tf_op jit(solution)/shard_map/ppermute | solution.py:61
  40.3 0.0 collective-permute-start.16
  40.3 0.0 collective-permute-start.18
  40.3 3.5 %collective-permute-done.10.refs_2_ = bf16[8,8,4096]{2,1,0:T(8,128)(2,1)S(1)} collective-permute-done((bf16[8,8,4096]{2,1,0:T(8,128)(2,1)S(1)}, bf16[8,8,4096]{2,1,0:T(8,128)(2,1)S(1)}, u32[]{:S(2)}, u32[]{:S(2)}) %collective-permute-start.10) | collective-permute-done | bytes 524320 | tf_op jit(solution)/shard_map/ppermute | solution.py:61
  43.8 1.3 %collective-permute-start.11 = (bf16[8,8,4096]{2,1,0:T(8,128)(2,1)S(1)}, bf16[8,8,4096]{2,1,0:T(8,128)(2,1)S(1)}, u32[]{:S(2)}, u32[]{:S(2)}) collective-permute-start(bf16[8,8,4096]{2,1,0:T(8,128)(2,1)S(1)} %collective-permute-done.10.refs_2_), channel_id=1, source_target_pairs={{0,8},{1,9},{2,10},{3,11},{4,12},{5,13},{6,14},{7,15},{8,16},{9,17... | collective-permute-start | bytes 1572872 | tf_op jit(solution)/shard_map/ppermute | solution.py:61
  45.1 0.1 collective-permute-done.8.refs_0_
  45.2 3.4 %collective-permute-start.12 = (bf16[8,8,4096]{2,1,0:T(8,128)(2,1)S(1)}, bf16[8,8,4096]{2,1,0:T(8,128)(2,1)S(1)}, u32[]{:S(2)}, u32[]{:S(2)}) collective-permute-start(bf16[8,8,4096]{2,1,0:T(8,128)(2,1)S(1)} %collective-permute-done.8.refs_0_), channel_id=1, source_target_pairs={{0,24},{1,25},{2,26},{3,27},{4,28},{5,29},{6,30},{7,31},{8,0},{9,1... | collective-permute-start | bytes 1572872 | tf_op jit(solution)/shard_map/ppermute | solution.py:61
  48.6 0.0 collective-permute-done.3.theirs
  48.6 0.4 collective-permute-start.9
  49.0 0.9 %whole_step.1 = (f32[8,8192]{1,0:T(8,128)}, f32[8,8192]{1,0:T(8,128)}, f32[8,128]{1,0:T(8,128)S(1)}) custom-call(f32[8,4096]{1,0:T(8,128)S(1)} %get-tuple-element.22.mine, f32[8,4096]{1,0:T(8,128)S(1)} %collective-permute-done.3.theirs, f32[8,8192]{1,0:T(8,128)S(1)} %get-tuple-element.21.base, f32[8,8192]{1,0:T(8,128)S(1)} %broadcast_multiply_fusion.decayed), custom_call_target="tpu_custom_call" | custom-call | flops 1048576 | bytes 1048576 | tf_op jit(solution)/shard_map/whole_step/pallas_call | solution.py:178
  49.9 5.2 %collective-permute-done.16.refs_1_ = bf16[8,8,4096]{2,1,0:T(8,128)(2,1)S(1)} collective-permute-done((bf16[8,8,4096]{2,1,0:T(8,128)(2,1)S(1)}, bf16[8,8,4096]{2,1,0:T(8,128)(2,1)S(1)}, u32[]{:S(2)}, u32[]{:S(2)}) %collective-permute-start.16) | collective-permute-done | bytes 524320 | tf_op jit(solution)/shard_map/ppermute | solution.py:61
  55.1 0.1 pack.2.refs_2_
  55.2 1.3 %collective-permute-start.17 = (bf16[3,8,8,4096]{3,2,1,0:T(8,128)(2,1)S(1)}, bf16[3,8,8,4096]{3,2,1,0:T(8,128)(2,1)S(1)}, u32[]{:S(2)}, u32[]{:S(2)}) collective-permute-start(bf16[3,8,8,4096]{3,2,1,0:T(8,128)(2,1)S(1)} %pack.2.refs_2_), channel_id=1, source_target_pairs={{0,64},{1,65},{2,66},{3,67},{4,68},{5,69},{6,70},{7,71},{8,72},{9,... | collective-permute-start | bytes 4718600 | tf_op jit(solution)/shard_map/ppermute | solution.py:61
  56.4 0.0 collective-permute-done.18.refs_1_
  56.4 1.5 %assemble.3 = (bf16[8,8,8,8192]{3,2,1,0:T(8,128)(2,1)}, f32[8,128]{1,0:T(8,128)S(1)}) custom-call(bf16[8,8,4096]{2,1,0:T(8,128)(2,1)S(1)} %bundle.1.refs_0_, bf16[8,8,4096]{2,1,0:T(8,128)(2,1)S(1)} %collective-permute-done.18.refs_1_, bf16[3,8,8,4096]{3,2,1,0:T(8,128)(2,1)S(1)} %pack.2.refs_2_), custom_call_target="tpu_custom_call" | custom-call | flops 5242880 | bytes 5242880 | tf_op jit(solution)/shard_map/assemble/pallas_call | solution.py:195
  58.0 8.3 %collective-permute-done.11.down.refs_1_ = bf16[8,8,4096]{2,1,0:T(8,128)(2,1)S(1)} collective-permute-done((bf16[8,8,4096]{2,1,0:T(8,128)(2,1)S(1)}, bf16[8,8,4096]{2,1,0:T(8,128)(2,1)S(1)}, u32[]{:S(2)}, u32[]{:S(2)}) %collective-permute-start.11) | collective-permute-done | bytes 524320 | tf_op jit(solution)/shard_map/ppermute | solution.py:61
  66.3 0.0 collective-permute-done.12.across.refs_0_
  66.3 0.0 collective-permute-done.9.up.refs_2_
  66.3 0.1 pack.3.refs_1_
  66.4 0.9 %collective-permute-start.19 = (bf16[3,8,8,4096]{3,2,1,0:T(8,128)(2,1)S(1)}, bf16[3,8,8,4096]{3,2,1,0:T(8,128)(2,1)S(1)}, u32[]{:S(2)}, u32[]{:S(2)}) collective-permute-start(bf16[3,8,8,4096]{3,2,1,0:T(8,128)(2,1)S(1)} %pack.3.refs_1_), channel_id=1, source_target_pairs={{0,64},{1,65},{2,66},{3,67},{4,68},{5,69},{6,70},{7,71},{8,72},{9,... | collective-permute-start | bytes 4718600 | tf_op jit(solution)/shard_map/ppermute | solution.py:61
  67.3 0.1 collective-permute-start.13
  67.4 1.5 %collective-permute-start.14 = (bf16[3,8,4096]{2,1,0:T(8,128)(2,1)S(1)}, bf16[3,8,4096]{2,1,0:T(8,128)(2,1)S(1)}, u32[]{:S(2)}, u32[]{:S(2)}) collective-permute-start(bf16[3,8,4096]{2,1,0:T(8,128)(2,1)S(1)} %get-tuple-element.27), channel_id=1, source_target_pairs={{0,8},{1,9},{2,10},{3,11},{4,12},{5,13},{6,14},{7,15},{8,16},{9,17... | collective-permute-start | bytes 589832 | tf_op jit(solution)/shard_map/ppermute | solution.py:61
  68.9 0.0 collective-permute-start.15
  68.9 0.0 collective-permute-done.17.refs_0_
  68.9 1.4 %collective-permute-done.19.refs_2_ = bf16[3,8,8,4096]{3,2,1,0:T(8,128)(2,1)S(1)} collective-permute-done((bf16[3,8,8,4096]{3,2,1,0:T(8,128)(2,1)S(1)}, bf16[3,8,8,4096]{3,2,1,0:T(8,128)(2,1)S(1)}, u32[]{:S(2)}, u32[]{:S(2)}) %collective-permute-start.19) | collective-permute-done | bytes 1572896 | tf_op jit(solution)/shard_map/ppermute | solution.py:61
  70.3 2.2 %assemble.4 = (bf16[8,8,8,8192]{3,2,1,0:T(8,128)(2,1)}, f32[8,128]{1,0:T(8,128)S(1)}) custom-call(bf16[3,8,8,4096]{3,2,1,0:T(8,128)(2,1)S(1)} %collective-permute-done.17.refs_0_, bf16[3,8,8,4096]{3,2,1,0:T(8,128)(2,1)S(1)} %pack.3.refs_1_, bf16[3,8,8,4096]{3,2,1,0:T(8,128)(2,1)S(1)} %collective-permute-done.19.refs_2_, ...), custom_call_target="tpu_custom_call", output_to_operand_aliasing={{0}: (3, {})} | custom-call | flops 9437184 | bytes 9437184 | tf_op jit(solution)/shard_map/assemble/pallas_call | solution.py:195
  72.6 2.0 %collective-permute-done.15.refs_2_ = bf16[2,8,4096]{2,1,0:T(8,128)(2,1)S(1)} collective-permute-done((bf16[2,8,4096]{2,1,0:T(8,128)(2,1)S(1)}, bf16[2,8,4096]{2,1,0:T(8,128)(2,1)S(1)}, u32[]{:S(2)}, u32[]{:S(2)}) %collective-permute-start.15) | collective-permute-done | bytes 131104 | tf_op jit(solution)/shard_map/ppermute | solution.py:61
  74.6 0.0 collective-permute-done.13.refs_0_
  74.6 0.7 collective-permute-done.14.refs_1_
  75.3 0.9 %collective-permute-start.20 = (bf16[8,8,4096]{2,1,0:T(8,128)(2,1)S(1)}, bf16[8,8,4096]{2,1,0:T(8,128)(2,1)S(1)}, u32[]{:S(2)}, u32[]{:S(2)}) collective-permute-start(bf16[8,8,4096]{2,1,0:T(8,128)(2,1)S(1)} %last.1.refs_0_), channel_id=1, source_target_pairs={{0,64},{1,65},{2,66},{3,67},{4,68},{5,69},{6,70},{7,71},{8,72},{9,... | collective-permute-start | bytes 1572872 | tf_op jit(solution)/shard_map/ppermute | solution.py:61
  76.2 1.5 %collective-permute-done.20.refs_1_ = bf16[8,8,4096]{2,1,0:T(8,128)(2,1)S(1)} collective-permute-done((bf16[8,8,4096]{2,1,0:T(8,128)(2,1)S(1)}, bf16[8,8,4096]{2,1,0:T(8,128)(2,1)S(1)}, u32[]{:S(2)}, u32[]{:S(2)}) %collective-permute-start.20) | collective-permute-done | bytes 524320 | tf_op jit(solution)/shard_map/ppermute | solution.py:61
  77.7 1.6 %assemble.5 = (bf16[8,8,8,8192]{3,2,1,0:T(8,128)(2,1)}, f32[8,128]{1,0:T(8,128)}) custom-call(bf16[8,8,4096]{2,1,0:T(8,128)(2,1)S(1)} %last.1.refs_0_, bf16[8,8,4096]{2,1,0:T(8,128)(2,1)S(1)} %collective-permute-done.20.refs_1_, bf16[8,8,8,8192]{3,2,1,0:T(8,128)(2,1)} %get-tuple-element.33.refs_2_), custom_call_target="tpu_custom_call", output_to_operand_aliasing={{0}: (2, {})} | custom-call | flops 2097152 | bytes 2097152 | tf_op jit(solution)/shard_map/assemble/pallas_call | solution.py:195
  (4 shorter events, 0.1 us)
Async XLA Ops:
  0.6 1.0 %copy-start = (f32[8,8192]{1,0:T(8,128)S(1)}, f32[8,8192]{1,0:T(8,128)}, u32[]{:S(2)}) copy-start(f32[8,8192]{1,0:T(8,128)} %base.1) | copy-start | bytes 786436
  1.6 0.9 %copy-start.1 = (bf16[1,8,8192]{2,1,0:T(8,128)(2,1)S(1)}, bf16[1,8,8192]{2,1,0:T(8,128)(2,1)}, u32[]{:S(2)}) copy-start(bf16[1,8,8192]{2,1,0:T(8,128)(2,1)} %weights.1) | copy-start | bytes 393220
  2.7 8.0 %collective-permute-start.2 = (bf16[8,4096]{1,0:T(8,128)(2,1)S(1)}, bf16[8,4096]{1,0:T(8,128)(2,1)S(1)}, u32[]{:S(2)}, u32[]{:S(2)}) collective-permute-start(bf16[8,4096]{1,0:T(8,128)(2,1)S(1)} %get-tuple-element.20), channel_id=1, source_target_pairs={{0,192},{1,193},{2,194},{3,195},{4,196},{5,197},{6,198},{7,199},{8... | collective-permute-start | bytes 196616 | tf_op jit(solution)/shard_map/ppermute | solution.py:61
  5.4 5.3 %collective-permute-start = (bf16[8,4096]{1,0:T(8,128)(2,1)S(1)}, bf16[8,4096]{1,0:T(8,128)(2,1)S(1)}, u32[]{:S(2)}, u32[]{:S(2)}) collective-permute-start(bf16[8,4096]{1,0:T(8,128)(2,1)S(1)} %get-tuple-element.20), channel_id=1, source_target_pairs={{0,64},{1,65},{2,66},{3,67},{4,68},{5,69},{6,70},{7,71},{8,72},{9,... | collective-permute-start | bytes 196616 | tf_op jit(solution)/shard_map/ppermute | solution.py:61
  6.1 4.6 %collective-permute-start.1 = (bf16[8,4096]{1,0:T(8,128)(2,1)S(1)}, bf16[8,4096]{1,0:T(8,128)(2,1)S(1)}, u32[]{:S(2)}, u32[]{:S(2)}) collective-permute-start(bf16[8,4096]{1,0:T(8,128)(2,1)S(1)} %get-tuple-element.19.keep), channel_id=1, source_target_pairs={{0,128},{1,129},{2,130},{3,131},{4,132},{5,133},{6,134},{7,135},{8... | collective-permute-start | bytes 196616 | tf_op jit(solution)/shard_map/ppermute | solution.py:61
  10.7 3.2 %collective-permute-start.4 = (bf16[8,4096]{1,0:T(8,128)(2,1)S(1)}, bf16[8,4096]{1,0:T(8,128)(2,1)S(1)}, u32[]{:S(2)}, u32[]{:S(2)}) collective-permute-start(bf16[8,4096]{1,0:T(8,128)(2,1)S(1)} %get-tuple-element.25.own), channel_id=1, source_target_pairs={{0,1},{1,0},{2,3},{3,2},{4,5},{5,4},{6,7},{7,6},{8,9},{9,8},{10,11... | collective-permute-start | bytes 196616 | tf_op jit(solution)/shard_map/ppermute | solution.py:61
  14.0 8.6 %collective-permute-start.7 = (bf16[2,8,4096]{2,1,0:T(8,128)(2,1)S(1)}, bf16[2,8,4096]{2,1,0:T(8,128)(2,1)S(1)}, u32[]{:S(2)}, u32[]{:S(2)}) collective-permute-start(bf16[2,8,4096]{2,1,0:T(8,128)(2,1)S(1)} %couple.1.refs_0_), channel_id=1, source_target_pairs={{0,2},{1,3},{2,4},{3,5},{4,6},{5,7},{6,0},{7,1},{8,10},{9,11},{10,... | collective-permute-start | bytes 393224 | tf_op jit(solution)/shard_map/ppermute | solution.py:61
  15.2 12.2 %collective-permute-start.6 = (bf16[2,8,4096]{2,1,0:T(8,128)(2,1)S(1)}, bf16[2,8,4096]{2,1,0:T(8,128)(2,1)S(1)}, u32[]{:S(2)}, u32[]{:S(2)}) collective-permute-start(bf16[2,8,4096]{2,1,0:T(8,128)(2,1)S(1)} %couple.1.refs_0_), channel_id=1, source_target_pairs={{0,4},{1,5},{2,6},{3,7},{4,0},{5,1},{6,2},{7,3},{8,12},{9,13},{10,... | collective-permute-start | bytes 393224 | tf_op jit(solution)/shard_map/ppermute | solution.py:61
  20.1 10.7 %collective-permute-start.5 = (bf16[2,8,4096]{2,1,0:T(8,128)(2,1)S(1)}, bf16[2,8,4096]{2,1,0:T(8,128)(2,1)S(1)}, u32[]{:S(2)}, u32[]{:S(2)}) collective-permute-start(bf16[2,8,4096]{2,1,0:T(8,128)(2,1)S(1)} %couple.1.refs_0_), channel_id=1, source_target_pairs={{0,6},{1,7},{2,0},{3,1},{4,2},{5,3},{6,4},{7,5},{8,14},{9,15},{10,... | collective-permute-start | bytes 393224 | tf_op jit(solution)/shard_map/ppermute | solution.py:61
  30.9 12.9 %collective-permute-start.10 = (bf16[8,8,4096]{2,1,0:T(8,128)(2,1)S(1)}, bf16[8,8,4096]{2,1,0:T(8,128)(2,1)S(1)}, u32[]{:S(2)}, u32[]{:S(2)}) collective-permute-start(bf16[8,8,4096]{2,1,0:T(8,128)(2,1)S(1)} %bundle.1.refs_0_), channel_id=1, source_target_pairs={{0,160},{1,161},{2,162},{3,163},{4,164},{5,165},{6,166},{7,167},{8... | collective-permute-start | bytes 1572872 | tf_op jit(solution)/shard_map/ppermute | solution.py:61
  34.3 10.9 %collective-permute-start.8 = (bf16[8,8,4096]{2,1,0:T(8,128)(2,1)S(1)}, bf16[8,8,4096]{2,1,0:T(8,128)(2,1)S(1)}, u32[]{:S(2)}, u32[]{:S(2)}) collective-permute-start(bf16[8,8,4096]{2,1,0:T(8,128)(2,1)S(1)} %bundle.1.refs_0_), channel_id=1, source_target_pairs={{0,24},{1,25},{2,26},{3,27},{4,28},{5,29},{6,30},{7,31},{8,0},{9,1... | collective-permute-start | bytes 1572872 | tf_op jit(solution)/shard_map/ppermute | solution.py:61
  37.0 11.6 %collective-permute-start.3 = (f32[8,4096]{1,0:T(8,128)S(1)}, f32[8,4096]{1,0:T(8,128)S(1)}, u32[]{:S(2)}, u32[]{:S(2)}) collective-permute-start(f32[8,4096]{1,0:T(8,128)S(1)} %get-tuple-element.22.mine), channel_id=1, source_target_pairs={{0,64},{1,65},{2,66},{3,67},{4,68},{5,69},{6,70},{7,71},{8,72},{9,... | collective-permute-start | bytes 393224 | tf_op jit(solution)/shard_map/ppermute | solution.py:61
  40.3 14.8 %collective-permute-start.16 = (bf16[8,8,4096]{2,1,0:T(8,128)(2,1)S(1)}, bf16[8,8,4096]{2,1,0:T(8,128)(2,1)S(1)}, u32[]{:S(2)}, u32[]{:S(2)}) collective-permute-start(bf16[8,8,4096]{2,1,0:T(8,128)(2,1)S(1)} %bundle.1.refs_0_), channel_id=1, source_target_pairs={{0,8},{1,9},{2,10},{3,11},{4,12},{5,13},{6,14},{7,15},{8,16},{9,17... | collective-permute-start | bytes 1572872 | tf_op jit(solution)/shard_map/ppermute | solution.py:61
  40.3 16.1 %collective-permute-start.18 = (bf16[8,8,4096]{2,1,0:T(8,128)(2,1)S(1)}, bf16[8,8,4096]{2,1,0:T(8,128)(2,1)S(1)}, u32[]{:S(2)}, u32[]{:S(2)}) collective-permute-start(bf16[8,8,4096]{2,1,0:T(8,128)(2,1)S(1)} %bundle.1.refs_0_), channel_id=1, source_target_pairs={{0,64},{1,65},{2,66},{3,67},{4,68},{5,69},{6,70},{7,71},{8,72},{9,... | collective-permute-start | bytes 1572872 | tf_op jit(solution)/shard_map/ppermute | solution.py:61
  43.8 22.5 %collective-permute-start.11 = (bf16[8,8,4096]{2,1,0:T(8,128)(2,1)S(1)}, bf16[8,8,4096]{2,1,0:T(8,128)(2,1)S(1)}, u32[]{:S(2)}, u32[]{:S(2)}) collective-permute-start(bf16[8,8,4096]{2,1,0:T(8,128)(2,1)S(1)} %collective-permute-done.10.refs_2_), channel_id=1, source_target_pairs={{0,8},{1,9},{2,10},{3,11},{4,12},{5,13},{6,14},{7,15},{8,16},{9,17... | collective-permute-start | bytes 1572872 | tf_op jit(solution)/shard_map/ppermute | solution.py:61
  45.2 21.1 %collective-permute-start.12 = (bf16[8,8,4096]{2,1,0:T(8,128)(2,1)S(1)}, bf16[8,8,4096]{2,1,0:T(8,128)(2,1)S(1)}, u32[]{:S(2)}, u32[]{:S(2)}) collective-permute-start(bf16[8,8,4096]{2,1,0:T(8,128)(2,1)S(1)} %collective-permute-done.8.refs_0_), channel_id=1, source_target_pairs={{0,24},{1,25},{2,26},{3,27},{4,28},{5,29},{6,30},{7,31},{8,0},{9,1... | collective-permute-start | bytes 1572872 | tf_op jit(solution)/shard_map/ppermute | solution.py:61
  48.6 17.7 %collective-permute-start.9 = (bf16[8,8,4096]{2,1,0:T(8,128)(2,1)S(1)}, bf16[8,8,4096]{2,1,0:T(8,128)(2,1)S(1)}, u32[]{:S(2)}, u32[]{:S(2)}) collective-permute-start(bf16[8,8,4096]{2,1,0:T(8,128)(2,1)S(1)} %collective-permute-done.8.refs_0_), channel_id=1, source_target_pairs={{0,160},{1,161},{2,162},{3,163},{4,164},{5,165},{6,166},{7,167},{8... | collective-permute-start | bytes 1572872 | tf_op jit(solution)/shard_map/ppermute | solution.py:61
  55.2 13.7 %collective-permute-start.17 = (bf16[3,8,8,4096]{3,2,1,0:T(8,128)(2,1)S(1)}, bf16[3,8,8,4096]{3,2,1,0:T(8,128)(2,1)S(1)}, u32[]{:S(2)}, u32[]{:S(2)}) collective-permute-start(bf16[3,8,8,4096]{3,2,1,0:T(8,128)(2,1)S(1)} %pack.2.refs_2_), channel_id=1, source_target_pairs={{0,64},{1,65},{2,66},{3,67},{4,68},{5,69},{6,70},{7,71},{8,72},{9,... | collective-permute-start | bytes 4718600 | tf_op jit(solution)/shard_map/ppermute | solution.py:61
  66.4 3.9 %collective-permute-start.19 = (bf16[3,8,8,4096]{3,2,1,0:T(8,128)(2,1)S(1)}, bf16[3,8,8,4096]{3,2,1,0:T(8,128)(2,1)S(1)}, u32[]{:S(2)}, u32[]{:S(2)}) collective-permute-start(bf16[3,8,8,4096]{3,2,1,0:T(8,128)(2,1)S(1)} %pack.3.refs_1_), channel_id=1, source_target_pairs={{0,64},{1,65},{2,66},{3,67},{4,68},{5,69},{6,70},{7,71},{8,72},{9,... | collective-permute-start | bytes 4718600 | tf_op jit(solution)/shard_map/ppermute | solution.py:61
  67.3 7.2 %collective-permute-start.13 = (bf16[3,8,4096]{2,1,0:T(8,128)(2,1)S(1)}, bf16[3,8,4096]{2,1,0:T(8,128)(2,1)S(1)}, u32[]{:S(2)}, u32[]{:S(2)}) collective-permute-start(bf16[3,8,4096]{2,1,0:T(8,128)(2,1)S(1)} %get-tuple-element.26), channel_id=1, source_target_pairs={{0,24},{1,25},{2,26},{3,27},{4,28},{5,29},{6,30},{7,31},{8,0},{9,1... | collective-permute-start | bytes 589832 | tf_op jit(solution)/shard_map/ppermute | solution.py:61
  67.4 7.8 %collective-permute-start.14 = (bf16[3,8,4096]{2,1,0:T(8,128)(2,1)S(1)}, bf16[3,8,4096]{2,1,0:T(8,128)(2,1)S(1)}, u32[]{:S(2)}, u32[]{:S(2)}) collective-permute-start(bf16[3,8,4096]{2,1,0:T(8,128)(2,1)S(1)} %get-tuple-element.27), channel_id=1, source_target_pairs={{0,8},{1,9},{2,10},{3,11},{4,12},{5,13},{6,14},{7,15},{8,16},{9,17... | collective-permute-start | bytes 589832 | tf_op jit(solution)/shard_map/ppermute | solution.py:61
  68.9 5.7 %collective-permute-start.15 = (bf16[2,8,4096]{2,1,0:T(8,128)(2,1)S(1)}, bf16[2,8,4096]{2,1,0:T(8,128)(2,1)S(1)}, u32[]{:S(2)}, u32[]{:S(2)}) collective-permute-start(bf16[2,8,4096]{2,1,0:T(8,128)(2,1)S(1)} %get-tuple-element.28), channel_id=1, source_target_pairs={{0,160},{1,161},{2,162},{3,163},{4,164},{5,165},{6,166},{7,167},{8... | collective-permute-start | bytes 393224 | tf_op jit(solution)/shard_map/ppermute | solution.py:61
  75.3 2.4 %collective-permute-start.20 = (bf16[8,8,4096]{2,1,0:T(8,128)(2,1)S(1)}, bf16[8,8,4096]{2,1,0:T(8,128)(2,1)S(1)}, u32[]{:S(2)}, u32[]{:S(2)}) collective-permute-start(bf16[8,8,4096]{2,1,0:T(8,128)(2,1)S(1)} %last.1.refs_0_), channel_id=1, source_target_pairs={{0,64},{1,65},{2,66},{3,67},{4,68},{5,69},{6,70},{7,71},{8,72},{9,... | collective-permute-start | bytes 1572872 | tf_op jit(solution)/shard_map/ppermute | solution.py:61

commit v5 on v4

--- a/solution.py
+++ b/solution.py
@@ -17,7 +17,7 @@
 AXES = ("island", "fsdp")
 HALF = 4096
 ROWS = 8
-PARTS = ((0, 3), (3, 3), (6, 2))
+RING = 8
 
 
 def all_places():
@@ -43,18 +43,32 @@
 OTHER_BOTH = pairs(lambda x_lo, core, x_hi, y, z: (1 - x_lo, 1 - core, x_hi, y, z))
 
 
-def from_z(step):
-    return pairs(lambda x_lo, core, x_hi, y, z: (x_lo, core, x_hi, y, (z - step) % 8))
-
-
-FROM_PAIR = pairs(lambda x_lo, core, x_hi, y, z: (x_lo, core, x_hi, y, z ^ 1))
-
-
-def from_y(step):
-    return pairs(lambda x_lo, core, x_hi, y, z: (x_lo, core, x_hi, y - step, z))
-
-
-FROM_X = pairs(lambda x_lo, core, x_hi, y, z: (1 - x_lo, core, 1 - x_hi, y, z))
+def by_core(first, second):
+    return pairs(lambda *p: (first if p[1] == 0 else second)(*p))
+
+
+def across_x(x_lo, core, x_hi, y, z):
+    return 1 - x_lo, core, 1 - x_hi, y, z
+
+
+def along_y(step):
+    return lambda x_lo, core, x_hi, y, z: (x_lo, core, x_hi, y + step, z)
+
+
+def along_z(step):
+    return lambda x_lo, core, x_hi, y, z: (x_lo, core, x_hi, y, (z + step) % 8)
+
+
+def z_neighbour(x_lo, core, x_hi, y, z):
+    return x_lo, core, x_hi, y, z ^ 1
+
+
+def along_snake(step):
+    def target(x_lo, core, x_hi, y, z):
+        at = ((y if x_hi == 0 else 7 - y) + step) % RING
+        to_x, to_y = (0, at) if at < 4 else (1, 7 - at)
+        return (x_lo if to_x == x_hi else 1 - x_lo), core, to_x, to_y, z
+    return target
 
 
 def send(x, to):
@@ -71,6 +85,12 @@
 
 def my_y():
     return lax.rem(lax.div(lax.axis_index("fsdp"), 8), 4)
+
+
+def snake_block(step):
+    at = lax.div(lax.axis_index("fsdp"), 8)
+    at = lax.rem(jnp.where(at < 4, at, 11 - at) + step + RING, RING)
+    return jnp.where(at < 4, at, 11 - at)
 
 
 def my_x_hi():
@@ -117,16 +137,17 @@
         moment_out[:, pl.ds(start, HALF)] = fresh
 
 
-def pair_kernel(own, other, out):
-    out[0], out[1] = own[...], other[...]
+def couple_kernel(own, other, *refs):
+    refs[-1][0], refs[-1][1] = own[...], other[...]
 
 
 def bundle_kernel(*refs):
     *couples, out = refs
-    z = my_z()
-    for step, couple in zip((0, 2, 4, 6), couples):
+    core, x_hi, y, z = my_core(), my_x_hi(), my_y(), my_z()
+    for step, couple in enumerate(couples):
         for i in range(2):
-            out[pl.ds(lax.rem((z ^ i) + step, 8), 1)] = couple[i][None]
+            at = jnp.where(core == 0, (x_hi ^ i) * 4 + lax.rem(y + step, 4), lax.rem((z ^ i) + 2 * step, 8))
+            out[pl.ds(at, 1)] = couple[i][None]
 
 
 def pack_kernel(count, *refs):
@@ -134,29 +155,39 @@
         refs[-1][i] = refs[i][...]
 
 
-def cut_kernel(up, down, across, *outs):
-    for ref, (start, count), out in zip((up, down, across), PARTS, outs):
-        out[...] = ref[start:start + count]
-
-
-def last_kernel(*refs):
-    for ref, (start, count) in zip(refs, PARTS):
-        refs[-1][start:start + count] = ref[...]
-
-
-def assemble_kernel(where, *refs):
-    *refs, out, written, sems = refs
-    core, todo = my_core(), []
-    for i, (array, place, theirs, flip, up) in enumerate(where):
-        source = refs[array] if place is None else refs[array].at[place]
-        block = (my_x_hi() ^ flip) * 4 + lax.rem(my_y() + up, 4)
-        start = pl.multiple_of((1 - core if theirs else core) * HALF, HALF)
-        todo.append(pltpu.make_async_copy(source, out.at[block, :, :, pl.ds(start, HALF)], sems.at[i]))
-    for copy in todo:
-        copy.start()
-    for copy in todo:
-        copy.wait()
-    written[...] = jnp.zeros_like(written)
+def cut_kernel(ahead, behind, low, high):
+    low[...], high[...] = ahead[:4], behind[4:]
+
+
+def last_kernel(low, high, *refs):
+    refs[-1][:4], refs[-1][4:] = low[...], high[...]
+
+
+def assemble_kernel(own, other, ends, *refs):
+    *refs, sems = refs
+    written = None if ends else refs.pop()
+    *refs, out = refs
+
+    def copies(where, of_core):
+        for array, place, step in where:
+            source = refs[array] if place is None else refs[array].at[place]
+            if of_core == 0:
+                yield source, out.at[:, lax.rem(my_z() + step + RING, RING), :, pl.ds(0, HALF)]
+            else:
+                yield source, out.at[snake_block(step), :, :, pl.ds(HALF, HALF)]
+
+    for core in range(2):
+        @pl.when(my_core() == core)
+        def _():
+            found = [*copies(own, core), *copies(other, 1 - core)]
+            todo = [pltpu.make_async_copy(*ends, sems.at[i]) for i, ends in enumerate(found)]
+            for copy in todo:
+                copy.start()
+            for copy in todo:
+                copy.wait()
+
+    if written is not None:
+        written[...] = jnp.zeros_like(written)
 
 
 VMEM = pl.BlockSpec(memory_space=pltpu.VMEM)
@@ -186,27 +217,31 @@
     )(*given)
 
 
-def assemble(given, out=None):
-    where = []
-    for array, (_, theirs, places) in enumerate(given):
-        packed = isinstance(places, list)
-        where.extend((array, i if packed else None, theirs, *at) for i, at in enumerate(places if packed else [places]))
-    given = [array for array, _, _ in given] + ([] if out is None else [out])
+def assemble(own, other, out=None, ends=False):
+    arrays, placed = [], ([], [])
+    for found, given in zip(placed, (own, other)):
+        for array, steps in given:
+            packed = isinstance(steps, list)
+            found.extend((len(arrays), i if packed else None, step) for i, step in enumerate(steps if packed else [steps]))
+            arrays.append(array)
+    count = len(placed[0]) + len(placed[1])
+    given = arrays + ([] if out is None else [out])
     return pl.pallas_call(
-        functools.partial(assemble_kernel, where),
-        out_shape=(shape((8, 8, ROWS, 2 * HALF), jnp.bfloat16), shape((8, 128), jnp.float32)),
+        functools.partial(assemble_kernel, *placed, ends),
+        out_shape=(shape((8, 8, ROWS, 2 * HALF), jnp.bfloat16), shape((8, 128), jnp.float32))[:1 if ends else 2],
         in_specs=[ANY] * len(given),
-        out_specs=(ANY, VMEM),
-        scratch_shapes=[pltpu.SemaphoreType.DMA((len(where),))],
+        out_specs=(ANY, VMEM)[:1 if ends else 2],
+        scratch_shapes=[pltpu.SemaphoreType.DMA((count,))],
         input_output_aliases={} if out is None else {len(given) - 1: 0},
         name="assemble",
-        **hints(len(where) << 20, 1 << 20),
+        **hints(count << 20, 1 << 20),
     )(*given)
 
 
 def on_device(local_weights, base_in, moment_in):
     bf16, f32 = jnp.bfloat16, jnp.float32
     half, whole = (ROWS, HALF), (ROWS, 2 * HALF)
+    local_weights, base_in = (pltpu.with_memory_space_constraint(x, pltpu.HBM) for x in (local_weights, base_in))
     keep, give, base = local(
         encode_kernel, [(half, bf16), (half, bf16), (whole, f32)], (local_weights, base_in), name="encode",
     )
@@ -217,11 +252,6 @@
         (keep, from_core, from_chip, from_both, base, decayed), name="half_step",
     )
 
-    theirs_summed = send(summed, OTHER_CORE)
-    master, fresh_moment, stepped = local(
-        whole_step_kernel, [(whole, f32)] * 2 + [((8, 128), f32)], (summed, theirs_summed, base, decayed), name="whole_step",
-    )
-
     def swap(x):
         return send(x, OTHER_CORE)
 
@@ -231,30 +261,36 @@
             name="pack", grant=1 << 20, in_specs=[VMEM] * len(arrays) + [ANY] * len(after),
         )[0]
 
-    couple, = local(pair_kernel, [((2, *half), bf16)], (fresh, send(fresh, FROM_PAIR)), name="couple")
-    couples = [couple] + [send(couple, from_z(step)) for step in (2, 4, 6)]
+    other = send(fresh, by_core(across_x, z_neighbour))
+    theirs_summed = send(summed, OTHER_CORE)
+    master, fresh_moment, stepped = local(
+        whole_step_kernel, [(whole, f32)] * 2 + [((8, 128), f32)], (summed, theirs_summed, base, decayed), name="whole_step",
+    )
+    couple, = local(
+        couple_kernel, [((2, *half), bf16)], (fresh, other, stepped), name="couple", in_specs=[VMEM] * 2 + [ANY],
+    )
+    couples = [couple] + [send(couple, by_core(along_y(-step), along_z(-2 * step))) for step in (1, 2, 3)]
     bundle, = local(bundle_kernel, [((8, *half), bf16)], couples, name="bundle")
-    up, down, across = send(bundle, from_y(1)), send(bundle, from_y(-1)), send(bundle, FROM_X)
-    up_up, down_across, up_across = send(up, from_y(1)), send(across, from_y(-1)), send(up, FROM_X)
-    cuts = local(
-        cut_kernel, [((count, *half), bf16) for _, count in PARTS], (up_across, down_across, up_up), name="cut",
-    )
-    parts = [send(x, to) for x, to in zip(cuts, (from_y(1), from_y(-1), FROM_X))]
-
-    first_places, second_places = [(0, 1), (0, 3), (1, 0)], [(0, 2), (1, 3), (1, 1)]
-    their_bundle = swap(bundle)
-    first = pack((up, down, across), (stepped,))
-    their_first = swap(first)
-    out, written = assemble([(bundle, False, (0, 0)), (their_bundle, True, (0, 0)), (first, False, first_places)])
-    second = pack((up_up, down_across, up_across), (written,))
-    their_second = swap(second)
-    out, written = assemble(
-        [(their_first, True, first_places), (second, False, second_places), (their_second, True, second_places)], out,
-    )
+
+    ahead, behind = by_core(along_z(-1), along_snake(-1)), by_core(along_z(1), along_snake(1))
+    got = {0: bundle}
+    for step in (1, 2, 3):
+        got[step], got[-step] = send(got[step - 1], ahead), send(got[1 - step], behind)
+    low, high = local(cut_kernel, [((4, *half), bf16)] * 2, (got[3], got[-3]), name="cut")
+    low, high = send(low, ahead), send(high, behind)
+
+    out, theirs, after = None, [], ()
+    for steps in ([0, 1, -1], [2, -2], [3, -3]):
+        packed = pack([got[step] for step in steps], after)
+        out, written = assemble([(packed, steps)], theirs, out)
+        theirs, after = [(swap(packed), steps)], (written,)
+    out, written = assemble([], theirs, out)
     last, = local(
-        last_kernel, [((8, *half), bf16)], [*parts, written], name="last", grant=1 << 20, in_specs=[VMEM] * 3 + [ANY],
-    )
-    out, _ = assemble([(last, False, (1, 2)), (swap(last), True, (1, 2))], out)
+        last_kernel, [((8, *half), bf16)], (low, high, written), name="last", grant=1 << 20, in_specs=[VMEM] * 2 + [ANY],
+    )
+    their_last = swap(last)
+    out, = assemble([(last, 4)], [], out, ends=True)
+    out, = assemble([], [(their_last, 4)], out, ends=True)
     return master, fresh_moment, out.reshape(512, 2 * HALF)
 
 

time: 79.4 us -> 75.8 us (0.955)
  waiting for transfers between devices: 36.5 us -> 33.2 us
  Pallas kernels: 6.8 us -> 9.79 us
  local copies, waits for them, and re-layouts: 1.85 us -> 0 us
  starting transfers between devices: 32.4 us -> 30.9 us
    ppermute x21 -> x20, waiting for transfers between devices: 36.5 us -> 33.2 us  [send(): return lax.ppermute(x, AXES, to)]
    pallas_call x3 -> x6, Pallas kernels: 5.35 us -> 7.26 us  [assemble(): pl.pallas_call(functools.partial(assemble_kernel, *placed, ends), out_sha...]
    unnamed x4 -> x0, local copies, waits for them, and re-layouts: 1.85 us -> none
    ppermute x21 -> x20, starting transfers between devices: 32.4 us -> 30.9 us  [send(): return lax.ppermute(x, AXES, to)]
    pallas_call x9 -> x10, Pallas kernels: 1.45 us -> 2.53 us  [local(): pl.pallas_call(kernel, out_shape=tuple((shape(*out) for out in outs)), in...]
  transfers between devices with their start and end apart: 21 -> 20, of which waited for: 12 -> 12; matrix products, arithmetic and copies ran while one was open for 1% -> 1% of each run, Pallas kernels for 6% -> 10%
where the time goes in v5:
time: 75.8 us; the launch traced here: 75.6 us
  waiting for transfers between devices  33.2 us (44%)
  starting transfers between devices  30.9 us (41%)
  Pallas kernels  9.79 us (13%)
  other arithmetic  0.97 us (1%)
  between operations  0.76 us (1%)
    ppermute x20, waiting for transfers between devices, send(): return lax.ppermute(x, AXES, to)  33.2 us
    ppermute x20, starting transfers between devices, send(): return lax.ppermute(x, AXES, to)  30.9 us
    pallas_call x6, Pallas kernels, assemble(): pl.pallas_call(functools.partial(assemble_kernel, *placed, ends), out_sha...  7.26 us
    pallas_call x10, Pallas kernels, local(): pl.pallas_call(kernel, out_shape=tuple((shape(*out) for out in outs)), in...  2.53 us
  transfers between devices with their start and end apart: 20, of which 12 were waited for; matrix products, arithmetic and copies ran while one was open for 1% of the time, Pallas kernels for 10%

profile of v5, /device:TPU:1, one launch (start us, length us, event | category | flops | bytes accessed | tf_op | source)
XLA Modules:
  0.0 75.6 jit_solution(3866867024452305002)
XLA Ops:
  0.6 1.2 %encode.1 = (bf16[8,4096]{1,0:T(8,128)(2,1)S(1)}, bf16[8,4096]{1,0:T(8,128)(2,1)S(1)}, f32[8,8192]{1,0:T(8,128)S(1)}) custom-call(bf16[1,8,8192]{2,1,0:T(8,128)(2,1)} %weights.1, f32[8,8192]{1,0:T(8,128)} %base.1), custom_call_target="tpu_custom_call" | custom-call | flops 1048576 | bytes 1048576 | tf_op jit(solution)/shard_map/encode/pallas_call | solution.py:209
  1.9 3.3 %collective-permute-start = (bf16[8,4096]{1,0:T(8,128)(2,1)S(1)}, bf16[8,4096]{1,0:T(8,128)(2,1)S(1)}, u32[]{:S(2)}, u32[]{:S(2)}) collective-permute-start(bf16[8,4096]{1,0:T(8,128)(2,1)S(1)} %get-tuple-element.21), channel_id=1, source_target_pairs={{0,64},{1,65},{2,66},{3,67},{4,68},{5,69},{6,70},{7,71},{8,72},{9,... | collective-permute-start | bytes 196616 | tf_op jit(solution)/shard_map/ppermute | solution.py:75
  5.2 0.0 collective-permute-start.2
  5.2 1.4 %collective-permute-start.1 = (bf16[8,4096]{1,0:T(8,128)(2,1)S(1)}, bf16[8,4096]{1,0:T(8,128)(2,1)S(1)}, u32[]{:S(2)}, u32[]{:S(2)}) collective-permute-start(bf16[8,4096]{1,0:T(8,128)(2,1)S(1)} %get-tuple-element.20.keep), channel_id=1, source_target_pairs={{0,128},{1,129},{2,130},{3,131},{4,132},{5,133},{6,134},{7,135},{8... | collective-permute-start | bytes 196616 | tf_op jit(solution)/shard_map/ppermute | solution.py:75
  6.6 1.0 %broadcast_multiply_fusion.decayed = f32[8,8192]{1,0:T(8,128)S(1)} fusion(f32[8,8192]{1,0:T(8,128)} %param.5), kind=kLoop, calls=%fused_computation | loop fusion | flops 65536 | bytes 524288 | tf_op jit(solution)/shard_map/mul | solution.py:248
  7.6 0.0 collective-permute-done.from_core
  7.6 2.5 %collective-permute-done.1.from_chip = bf16[8,4096]{1,0:T(8,128)(2,1)S(1)} collective-permute-done((bf16[8,4096]{1,0:T(8,128)(2,1)S(1)}, bf16[8,4096]{1,0:T(8,128)(2,1)S(1)}, u32[]{:S(2)}, u32[]{:S(2)}) %collective-permute-start.1) | collective-permute-done | bytes 65568 | tf_op jit(solution)/shard_map/ppermute | solution.py:75
  10.1 0.0 collective-permute-done.2.from_both
  10.1 0.1 half_step.1
  10.2 1.0 %collective-permute-start.3 = (f32[8,4096]{1,0:T(8,128)S(1)}, f32[8,4096]{1,0:T(8,128)S(1)}, u32[]{:S(2)}, u32[]{:S(2)}) collective-permute-start(f32[8,4096]{1,0:T(8,128)S(1)} %get-tuple-element.23.mine), channel_id=1, source_target_pairs={{0,64},{1,65},{2,66},{3,67},{4,68},{5,69},{6,70},{7,71},{8,72},{9,... | collective-permute-start | bytes 393224 | tf_op jit(solution)/shard_map/ppermute | solution.py:75
  11.2 0.0 collective-permute-start.4
  11.2 1.0 %collective-permute-done.3.theirs = f32[8,4096]{1,0:T(8,128)S(1)} collective-permute-done((f32[8,4096]{1,0:T(8,128)S(1)}, f32[8,4096]{1,0:T(8,128)S(1)}, u32[]{:S(2)}, u32[]{:S(2)}) %collective-permute-start.3) | collective-permute-done | bytes 131104 | tf_op jit(solution)/shard_map/ppermute | solution.py:75
  12.2 0.9 %whole_step.1 = (f32[8,8192]{1,0:T(8,128)}, f32[8,8192]{1,0:T(8,128)}, f32[8,128]{1,0:T(8,128)S(1)}) custom-call(f32[8,4096]{1,0:T(8,128)S(1)} %get-tuple-element.23.mine, f32[8,4096]{1,0:T(8,128)S(1)} %collective-permute-done.3.theirs, f32[8,8192]{1,0:T(8,128)S(1)} %get-tuple-element.22.base, f32[8,8192]{1,0:T(8,128)S(1)} %broadcast_multiply_fusion.decayed), custom_call_target="tpu_custom_call" | custom-call | flops 1048576 | bytes 1048576 | tf_op jit(solution)/shard_map/whole_step/pallas_call | solution.py:209
  13.1 1.3 %collective-permute-done.4.other = bf16[8,4096]{1,0:T(8,128)(2,1)S(1)} collective-permute-done((bf16[8,4096]{1,0:T(8,128)(2,1)S(1)}, bf16[8,4096]{1,0:T(8,128)(2,1)S(1)}, u32[]{:S(2)}, u32[]{:S(2)}) %collective-permute-start.4) | collective-permute-done | bytes 65568 | tf_op jit(solution)/shard_map/ppermute | solution.py:75
  14.4 4.4 %collective-permute-start.5 = (bf16[2,8,4096]{2,1,0:T(8,128)(2,1)S(1)}, bf16[2,8,4096]{2,1,0:T(8,128)(2,1)S(1)}, u32[]{:S(2)}, u32[]{:S(2)}) collective-permute-start(bf16[2,8,4096]{2,1,0:T(8,128)(2,1)S(1)} %couple.1.refs_0_), channel_id=1, source_target_pairs={{0,24},{1,25},{2,26},{3,27},{4,28},{5,29},{6,30},{7,31},{8,0},{9,1... | collective-permute-start | bytes 393224 | tf_op jit(solution)/shard_map/ppermute | solution.py:75
  18.7 1.0 %collective-permute-start.6 = (bf16[2,8,4096]{2,1,0:T(8,128)(2,1)S(1)}, bf16[2,8,4096]{2,1,0:T(8,128)(2,1)S(1)}, u32[]{:S(2)}, u32[]{:S(2)}) collective-permute-start(bf16[2,8,4096]{2,1,0:T(8,128)(2,1)S(1)} %couple.1.refs_0_), channel_id=1, source_target_pairs={{0,16},{1,17},{2,18},{3,19},{4,20},{5,21},{6,22},{7,23},{8,24},{9,... | collective-permute-start | bytes 393224 | tf_op jit(solution)/shard_map/ppermute | solution.py:75
  19.7 2.3 %collective-permute-start.7 = (bf16[2,8,4096]{2,1,0:T(8,128)(2,1)S(1)}, bf16[2,8,4096]{2,1,0:T(8,128)(2,1)S(1)}, u32[]{:S(2)}, u32[]{:S(2)}) collective-permute-start(bf16[2,8,4096]{2,1,0:T(8,128)(2,1)S(1)} %couple.1.refs_0_), channel_id=1, source_target_pairs={{0,8},{1,9},{2,10},{3,11},{4,12},{5,13},{6,14},{7,15},{8,16},{9,17... | collective-permute-start | bytes 393224 | tf_op jit(solution)/shard_map/ppermute | solution.py:75
  22.0 2.9 %collective-permute-done.5.refs_1_ = bf16[2,8,4096]{2,1,0:T(8,128)(2,1)S(1)} collective-permute-done((bf16[2,8,4096]{2,1,0:T(8,128)(2,1)S(1)}, bf16[2,8,4096]{2,1,0:T(8,128)(2,1)S(1)}, u32[]{:S(2)}, u32[]{:S(2)}) %collective-permute-start.5) | collective-permute-done | bytes 131104 | tf_op jit(solution)/shard_map/ppermute | solution.py:75
  24.9 3.2 %collective-permute-done.6.refs_2_ = bf16[2,8,4096]{2,1,0:T(8,128)(2,1)S(1)} collective-permute-done((bf16[2,8,4096]{2,1,0:T(8,128)(2,1)S(1)}, bf16[2,8,4096]{2,1,0:T(8,128)(2,1)S(1)}, u32[]{:S(2)}, u32[]{:S(2)}) %collective-permute-start.6) | collective-permute-done | bytes 131104 | tf_op jit(solution)/shard_map/ppermute | solution.py:75
  28.0 0.0 collective-permute-done.7.refs_3_
  28.0 0.1 bundle.1.refs_0_
  28.1 1.2 %collective-permute-start.11 = (bf16[8,8,4096]{2,1,0:T(8,128)(2,1)S(1)}, bf16[8,8,4096]{2,1,0:T(8,128)(2,1)S(1)}, u32[]{:S(2)}, u32[]{:S(2)}) collective-permute-start(bf16[8,8,4096]{2,1,0:T(8,128)(2,1)S(1)} %bundle.1.refs_0_), channel_id=1, source_target_pairs={{0,1},{1,2},{2,3},{3,4},{4,5},{5,6},{6,7},{7,0},{8,9},{9,10},{10,1... | collective-permute-start | bytes 1572872 | tf_op jit(solution)/shard_map/ppermute | solution.py:75
  29.3 1.5 %collective-permute-start.8 = (bf16[8,8,4096]{2,1,0:T(8,128)(2,1)S(1)}, bf16[8,8,4096]{2,1,0:T(8,128)(2,1)S(1)}, u32[]{:S(2)}, u32[]{:S(2)}) collective-permute-start(bf16[8,8,4096]{2,1,0:T(8,128)(2,1)S(1)} %bundle.1.refs_0_), channel_id=1, source_target_pairs={{0,7},{1,0},{2,1},{3,2},{4,3},{5,4},{6,5},{7,6},{8,15},{9,8},{10,9... | collective-permute-start | bytes 1572872 | tf_op jit(solution)/shard_map/ppermute | solution.py:75
  30.8 6.9 %collective-permute-done.11.refs_2_ = bf16[8,8,4096]{2,1,0:T(8,128)(2,1)S(1)} collective-permute-done((bf16[8,8,4096]{2,1,0:T(8,128)(2,1)S(1)}, bf16[8,8,4096]{2,1,0:T(8,128)(2,1)S(1)}, u32[]{:S(2)}, u32[]{:S(2)}) %collective-permute-start.11) | collective-permute-done | bytes 524320 | tf_op jit(solution)/shard_map/ppermute | solution.py:75
  37.7 0.0 collective-permute-done.8.refs_1_
  37.7 0.1 pack.3.refs_0_
  37.8 1.6 %collective-permute-start.16 = (bf16[3,8,8,4096]{3,2,1,0:T(8,128)(2,1)S(1)}, bf16[3,8,8,4096]{3,2,1,0:T(8,128)(2,1)S(1)}, u32[]{:S(2)}, u32[]{:S(2)}) collective-permute-start(bf16[3,8,8,4096]{3,2,1,0:T(8,128)(2,1)S(1)} %pack.3.refs_0_), channel_id=1, source_target_pairs={{0,64},{1,65},{2,66},{3,67},{4,68},{5,69},{6,70},{7,71},{8,72},{9,... | collective-permute-start | bytes 4718600 | tf_op jit(solution)/shard_map/ppermute | solution.py:75
  39.4 2.5 %collective-permute-start.9 = (bf16[8,8,4096]{2,1,0:T(8,128)(2,1)S(1)}, bf16[8,8,4096]{2,1,0:T(8,128)(2,1)S(1)}, u32[]{:S(2)}, u32[]{:S(2)}) collective-permute-start(bf16[8,8,4096]{2,1,0:T(8,128)(2,1)S(1)} %collective-permute-done.8.refs_1_), channel_id=1, source_target_pairs={{0,7},{1,0},{2,1},{3,2},{4,3},{5,4},{6,5},{7,6},{8,15},{9,8},{10,9... | collective-permute-start | bytes 1572872 | tf_op jit(solution)/shard_map/ppermute | solution.py:75
  41.9 0.0 collective-permute-start.12
  41.9 6.1 %collective-permute-done.9.refs_0_ = bf16[8,8,4096]{2,1,0:T(8,128)(2,1)S(1)} collective-permute-done((bf16[8,8,4096]{2,1,0:T(8,128)(2,1)S(1)}, bf16[8,8,4096]{2,1,0:T(8,128)(2,1)S(1)}, u32[]{:S(2)}, u32[]{:S(2)}) %collective-permute-start.9) | collective-permute-done | bytes 524320 | tf_op jit(solution)/shard_map/ppermute | solution.py:75
  48.0 3.4 %collective-permute-start.10 = (bf16[8,8,4096]{2,1,0:T(8,128)(2,1)S(1)}, bf16[8,8,4096]{2,1,0:T(8,128)(2,1)S(1)}, u32[]{:S(2)}, u32[]{:S(2)}) collective-permute-start(bf16[8,8,4096]{2,1,0:T(8,128)(2,1)S(1)} %collective-permute-done.9.refs_0_), channel_id=1, source_target_pairs={{0,7},{1,0},{2,1},{3,2},{4,3},{5,4},{6,5},{7,6},{8,15},{9,8},{10,9... | collective-permute-start | bytes 1572872 | tf_op jit(solution)/shard_map/ppermute | solution.py:75
  51.4 0.0 collective-permute-done.12.refs_1_
  51.4 0.0 collective-permute-start.13
  51.4 1.2 %assemble.6 = (bf16[8,8,8,8192]{3,2,1,0:T(8,128)(2,1)}, f32[8,128]{1,0:T(8,128)S(1)}) custom-call(bf16[3,8,8,4096]{3,2,1,0:T(8,128)(2,1)S(1)} %pack.3.refs_0_), custom_call_target="tpu_custom_call" | custom-call | flops 3145728 | bytes 3145728 | tf_op jit(solution)/shard_map/assemble/pallas_call | solution.py:229
  52.6 0.1 pack.4.refs_0_
  52.7 1.9 %collective-permute-start.18 = (bf16[2,8,8,4096]{3,2,1,0:T(8,128)(2,1)S(1)}, bf16[2,8,8,4096]{3,2,1,0:T(8,128)(2,1)S(1)}, u32[]{:S(2)}, u32[]{:S(2)}) collective-permute-start(bf16[2,8,8,4096]{3,2,1,0:T(8,128)(2,1)S(1)} %pack.4.refs_0_), channel_id=1, source_target_pairs={{0,64},{1,65},{2,66},{3,67},{4,68},{5,69},{6,70},{7,71},{8,72},{9,... | collective-permute-start | bytes 3145736 | tf_op jit(solution)/shard_map/ppermute | solution.py:75
  54.6 0.0 collective-permute-done.16.refs_1_
  54.6 1.5 %assemble.7 = (bf16[8,8,8,8192]{3,2,1,0:T(8,128)(2,1)}, f32[8,128]{1,0:T(8,128)S(1)}) custom-call(bf16[2,8,8,4096]{3,2,1,0:T(8,128)(2,1)S(1)} %pack.4.refs_0_, bf16[3,8,8,4096]{3,2,1,0:T(8,128)(2,1)S(1)} %collective-permute-done.16.refs_1_, bf16[8,8,8,8192]{3,2,1,0:T(8,128)(2,1)} %get-tuple-element.31.refs_2_), custom_call_target="tpu_custom_call", output_to_operand_aliasing={{0}: (2, {})} | custom-call | flops 5242880 | bytes 5242880 | tf_op jit(solution)/shard_map/assemble/pallas_call | solution.py:229
  56.1 1.5 %collective-permute-done.10.ahead.refs_0_ = bf16[8,8,4096]{2,1,0:T(8,128)(2,1)S(1)} collective-permute-done((bf16[8,8,4096]{2,1,0:T(8,128)(2,1)S(1)}, bf16[8,8,4096]{2,1,0:T(8,128)(2,1)S(1)}, u32[]{:S(2)}, u32[]{:S(2)}) %collective-permute-start.10) | collective-permute-done | bytes 524320 | tf_op jit(solution)/shard_map/ppermute | solution.py:75
  57.6 3.4 %collective-permute-done.13.behind.refs_1_ = bf16[8,8,4096]{2,1,0:T(8,128)(2,1)S(1)} collective-permute-done((bf16[8,8,4096]{2,1,0:T(8,128)(2,1)S(1)}, bf16[8,8,4096]{2,1,0:T(8,128)(2,1)S(1)}, u32[]{:S(2)}, u32[]{:S(2)}) %collective-permute-start.13) | collective-permute-done | bytes 524320 | tf_op jit(solution)/shard_map/ppermute | solution.py:75
  61.0 0.1 pack.5.refs_0_
  61.0 2.7 %collective-permute-start.17 = (bf16[2,8,8,4096]{3,2,1,0:T(8,128)(2,1)S(1)}, bf16[2,8,8,4096]{3,2,1,0:T(8,128)(2,1)S(1)}, u32[]{:S(2)}, u32[]{:S(2)}) collective-permute-start(bf16[2,8,8,4096]{3,2,1,0:T(8,128)(2,1)S(1)} %pack.5.refs_0_), channel_id=1, source_target_pairs={{0,64},{1,65},{2,66},{3,67},{4,68},{5,69},{6,70},{7,71},{8,72},{9,... | collective-permute-start | bytes 3145736 | tf_op jit(solution)/shard_map/ppermute | solution.py:75
  63.8 2.6 %collective-permute-start.14 = (bf16[4,8,4096]{2,1,0:T(8,128)(2,1)S(1)}, bf16[4,8,4096]{2,1,0:T(8,128)(2,1)S(1)}, u32[]{:S(2)}, u32[]{:S(2)}) collective-permute-start(bf16[4,8,4096]{2,1,0:T(8,128)(2,1)S(1)} %get-tuple-element.28), channel_id=1, source_target_pairs={{0,7},{1,0},{2,1},{3,2},{4,3},{5,4},{6,5},{7,6},{8,15},{9,8},{10,9... | collective-permute-start | bytes 786440 | tf_op jit(solution)/shard_map/ppermute | solution.py:75
  66.4 0.0 collective-permute-start.15
  66.4 0.0 collective-permute-done.18.refs_1_
  66.4 1.9 %assemble.8 = (bf16[8,8,8,8192]{3,2,1,0:T(8,128)(2,1)}, f32[8,128]{1,0:T(8,128)}) custom-call(bf16[2,8,8,4096]{3,2,1,0:T(8,128)(2,1)S(1)} %pack.5.refs_0_, bf16[2,8,8,4096]{3,2,1,0:T(8,128)(2,1)S(1)} %collective-permute-done.18.refs_1_, bf16[8,8,8,8192]{3,2,1,0:T(8,128)(2,1)} %get-tuple-element.33.refs_2_), custom_call_target="tpu_custom_call", output_to_operand_aliasing={{0}: (2, {})} | custom-call | flops 4194304 | bytes 4194304 | tf_op jit(solution)/shard_map/assemble/pallas_call | solution.py:229
  68.3 0.0 collective-permute-done.17.refs_0_
  68.3 1.0 %assemble.9 = (bf16[8,8,8,8192]{3,2,1,0:T(8,128)(2,1)}, f32[8,128]{1,0:T(8,128)S(1)}) custom-call(bf16[2,8,8,4096]{3,2,1,0:T(8,128)(2,1)S(1)} %collective-permute-done.17.refs_0_, bf16[8,8,8,8192]{3,2,1,0:T(8,128)(2,1)} %get-tuple-element.34.refs_1_), custom_call_target="tpu_custom_call", output_to_operand_aliasing={{0}: (1, {})} | custom-call | flops 2097152 | bytes 2097152 | tf_op jit(solution)/shard_map/assemble/pallas_call | solution.py:229
  69.3 0.3 collective-permute-done.14.low
  69.7 3.1 %collective-permute-done.15.high = bf16[4,8,4096]{2,1,0:T(8,128)(2,1)S(1)} collective-permute-done((bf16[4,8,4096]{2,1,0:T(8,128)(2,1)S(1)}, bf16[4,8,4096]{2,1,0:T(8,128)(2,1)S(1)}, u32[]{:S(2)}, u32[]{:S(2)}) %collective-permute-start.15) | collective-permute-done | bytes 262176 | tf_op jit(solution)/shard_map/ppermute | solution.py:75
  72.8 0.1 collective-permute-start.19
  72.9 0.8 %assemble.10.refs_1_ = bf16[8,8,8,8192]{3,2,1,0:T(8,128)(2,1)} custom-call(bf16[8,8,4096]{2,1,0:T(8,128)(2,1)S(1)} %last.1.refs_0_, bf16[8,8,8,8192]{3,2,1,0:T(8,128)(2,1)} %get-tuple-element.36.refs_1_), custom_call_target="tpu_custom_call", output_to_operand_aliasing={{}: (1, {})} | custom-call | flops 1048576 | bytes 1048576 | tf_op jit(solution)/shard_map/assemble/pallas_call | solution.py:229
  73.8 1.1 %collective-permute-done.19.refs_0_ = bf16[8,8,4096]{2,1,0:T(8,128)(2,1)S(1)} collective-permute-done((bf16[8,8,4096]{2,1,0:T(8,128)(2,1)S(1)}, bf16[8,8,4096]{2,1,0:T(8,128)(2,1)S(1)}, u32[]{:S(2)}, u32[]{:S(2)}) %collective-permute-start.19) | collective-permute-done | bytes 524320 | tf_op jit(solution)/shard_map/ppermute | solution.py:75
  74.8 0.8 %assemble.11 = bf16[8,8,8,8192]{3,2,1,0:T(8,128)(2,1)} custom-call(bf16[8,8,4096]{2,1,0:T(8,128)(2,1)S(1)} %collective-permute-done.19.refs_0_, bf16[8,8,8,8192]{3,2,1,0:T(8,128)(2,1)} %assemble.10.refs_1_), custom_call_target="tpu_custom_call", output_to_operand_aliasing={{}: (1, {})} | custom-call | flops 1048576 | bytes 1048576 | tf_op jit(solution)/shard_map/assemble/pallas_call | solution.py:229
  (3 shorter events, 0.1 us)
Async XLA Ops:
  1.9 5.8 %collective-permute-start = (bf16[8,4096]{1,0:T(8,128)(2,1)S(1)}, bf16[8,4096]{1,0:T(8,128)(2,1)S(1)}, u32[]{:S(2)}, u32[]{:S(2)}) collective-permute-start(bf16[8,4096]{1,0:T(8,128)(2,1)S(1)} %get-tuple-element.21), channel_id=1, source_target_pairs={{0,64},{1,65},{2,66},{3,67},{4,68},{5,69},{6,70},{7,71},{8,72},{9,... | collective-permute-start | bytes 196616 | tf_op jit(solution)/shard_map/ppermute | solution.py:75
  5.2 5.0 %collective-permute-start.2 = (bf16[8,4096]{1,0:T(8,128)(2,1)S(1)}, bf16[8,4096]{1,0:T(8,128)(2,1)S(1)}, u32[]{:S(2)}, u32[]{:S(2)}) collective-permute-start(bf16[8,4096]{1,0:T(8,128)(2,1)S(1)} %get-tuple-element.21), channel_id=1, source_target_pairs={{0,192},{1,193},{2,194},{3,195},{4,196},{5,197},{6,198},{7,199},{8... | collective-permute-start | bytes 196616 | tf_op jit(solution)/shard_map/ppermute | solution.py:75
  5.2 4.9 %collective-permute-start.1 = (bf16[8,4096]{1,0:T(8,128)(2,1)S(1)}, bf16[8,4096]{1,0:T(8,128)(2,1)S(1)}, u32[]{:S(2)}, u32[]{:S(2)}) collective-permute-start(bf16[8,4096]{1,0:T(8,128)(2,1)S(1)} %get-tuple-element.20.keep), channel_id=1, source_target_pairs={{0,128},{1,129},{2,130},{3,131},{4,132},{5,133},{6,134},{7,135},{8... | collective-permute-start | bytes 196616 | tf_op jit(solution)/shard_map/ppermute | solution.py:75
  10.2 2.0 %collective-permute-start.3 = (f32[8,4096]{1,0:T(8,128)S(1)}, f32[8,4096]{1,0:T(8,128)S(1)}, u32[]{:S(2)}, u32[]{:S(2)}) collective-permute-start(f32[8,4096]{1,0:T(8,128)S(1)} %get-tuple-element.23.mine), channel_id=1, source_target_pairs={{0,64},{1,65},{2,66},{3,67},{4,68},{5,69},{6,70},{7,71},{8,72},{9,... | collective-permute-start | bytes 393224 | tf_op jit(solution)/shard_map/ppermute | solution.py:75
  11.2 3.1 %collective-permute-start.4 = (bf16[8,4096]{1,0:T(8,128)(2,1)S(1)}, bf16[8,4096]{1,0:T(8,128)(2,1)S(1)}, u32[]{:S(2)}, u32[]{:S(2)}) collective-permute-start(bf16[8,4096]{1,0:T(8,128)(2,1)S(1)} %get-tuple-element.26.own), channel_id=1, source_target_pairs={{0,160},{1,161},{2,162},{3,163},{4,164},{5,165},{6,166},{7,167},{8... | collective-permute-start | bytes 196616 | tf_op jit(solution)/shard_map/ppermute | solution.py:75
  14.4 10.5 %collective-permute-start.5 = (bf16[2,8,4096]{2,1,0:T(8,128)(2,1)S(1)}, bf16[2,8,4096]{2,1,0:T(8,128)(2,1)S(1)}, u32[]{:S(2)}, u32[]{:S(2)}) collective-permute-start(bf16[2,8,4096]{2,1,0:T(8,128)(2,1)S(1)} %couple.1.refs_0_), channel_id=1, source_target_pairs={{0,24},{1,25},{2,26},{3,27},{4,28},{5,29},{6,30},{7,31},{8,0},{9,1... | collective-permute-start | bytes 393224 | tf_op jit(solution)/shard_map/ppermute | solution.py:75
  18.7 9.3 %collective-permute-start.6 = (bf16[2,8,4096]{2,1,0:T(8,128)(2,1)S(1)}, bf16[2,8,4096]{2,1,0:T(8,128)(2,1)S(1)}, u32[]{:S(2)}, u32[]{:S(2)}) collective-permute-start(bf16[2,8,4096]{2,1,0:T(8,128)(2,1)S(1)} %couple.1.refs_0_), channel_id=1, source_target_pairs={{0,16},{1,17},{2,18},{3,19},{4,20},{5,21},{6,22},{7,23},{8,24},{9,... | collective-permute-start | bytes 393224 | tf_op jit(solution)/shard_map/ppermute | solution.py:75
  19.7 8.3 %collective-permute-start.7 = (bf16[2,8,4096]{2,1,0:T(8,128)(2,1)S(1)}, bf16[2,8,4096]{2,1,0:T(8,128)(2,1)S(1)}, u32[]{:S(2)}, u32[]{:S(2)}) collective-permute-start(bf16[2,8,4096]{2,1,0:T(8,128)(2,1)S(1)} %couple.1.refs_0_), channel_id=1, source_target_pairs={{0,8},{1,9},{2,10},{3,11},{4,12},{5,13},{6,14},{7,15},{8,16},{9,17... | collective-permute-start | bytes 393224 | tf_op jit(solution)/shard_map/ppermute | solution.py:75
  28.1 9.6 %collective-permute-start.11 = (bf16[8,8,4096]{2,1,0:T(8,128)(2,1)S(1)}, bf16[8,8,4096]{2,1,0:T(8,128)(2,1)S(1)}, u32[]{:S(2)}, u32[]{:S(2)}) collective-permute-start(bf16[8,8,4096]{2,1,0:T(8,128)(2,1)S(1)} %bundle.1.refs_0_), channel_id=1, source_target_pairs={{0,1},{1,2},{2,3},{3,4},{4,5},{5,6},{6,7},{7,0},{8,9},{9,10},{10,1... | collective-permute-start | bytes 1572872 | tf_op jit(solution)/shard_map/ppermute | solution.py:75
  29.3 8.4 %collective-permute-start.8 = (bf16[8,8,4096]{2,1,0:T(8,128)(2,1)S(1)}, bf16[8,8,4096]{2,1,0:T(8,128)(2,1)S(1)}, u32[]{:S(2)}, u32[]{:S(2)}) collective-permute-start(bf16[8,8,4096]{2,1,0:T(8,128)(2,1)S(1)} %bundle.1.refs_0_), channel_id=1, source_target_pairs={{0,7},{1,0},{2,1},{3,2},{4,3},{5,4},{6,5},{7,6},{8,15},{9,8},{10,9... | collective-permute-start | bytes 1572872 | tf_op jit(solution)/shard_map/ppermute | solution.py:75
  37.8 16.8 %collective-permute-start.16 = (bf16[3,8,8,4096]{3,2,1,0:T(8,128)(2,1)S(1)}, bf16[3,8,8,4096]{3,2,1,0:T(8,128)(2,1)S(1)}, u32[]{:S(2)}, u32[]{:S(2)}) collective-permute-start(bf16[3,8,8,4096]{3,2,1,0:T(8,128)(2,1)S(1)} %pack.3.refs_0_), channel_id=1, source_target_pairs={{0,64},{1,65},{2,66},{3,67},{4,68},{5,69},{6,70},{7,71},{8,72},{9,... | collective-permute-start | bytes 4718600 | tf_op jit(solution)/shard_map/ppermute | solution.py:75
  39.4 8.6 %collective-permute-start.9 = (bf16[8,8,4096]{2,1,0:T(8,128)(2,1)S(1)}, bf16[8,8,4096]{2,1,0:T(8,128)(2,1)S(1)}, u32[]{:S(2)}, u32[]{:S(2)}) collective-permute-start(bf16[8,8,4096]{2,1,0:T(8,128)(2,1)S(1)} %collective-permute-done.8.refs_1_), channel_id=1, source_target_pairs={{0,7},{1,0},{2,1},{3,2},{4,3},{5,4},{6,5},{7,6},{8,15},{9,8},{10,9... | collective-permute-start | bytes 1572872 | tf_op jit(solution)/shard_map/ppermute | solution.py:75
  41.9 9.5 %collective-permute-start.12 = (bf16[8,8,4096]{2,1,0:T(8,128)(2,1)S(1)}, bf16[8,8,4096]{2,1,0:T(8,128)(2,1)S(1)}, u32[]{:S(2)}, u32[]{:S(2)}) collective-permute-start(bf16[8,8,4096]{2,1,0:T(8,128)(2,1)S(1)} %collective-permute-done.11.refs_2_), channel_id=1, source_target_pairs={{0,1},{1,2},{2,3},{3,4},{4,5},{5,6},{6,7},{7,0},{8,9},{9,10},{10,1... | collective-permute-start | bytes 1572872 | tf_op jit(solution)/shard_map/ppermute | solution.py:75
  48.0 9.5 %collective-permute-start.10 = (bf16[8,8,4096]{2,1,0:T(8,128)(2,1)S(1)}, bf16[8,8,4096]{2,1,0:T(8,128)(2,1)S(1)}, u32[]{:S(2)}, u32[]{:S(2)}) collective-permute-start(bf16[8,8,4096]{2,1,0:T(8,128)(2,1)S(1)} %collective-permute-done.9.refs_0_), channel_id=1, source_target_pairs={{0,7},{1,0},{2,1},{3,2},{4,3},{5,4},{6,5},{7,6},{8,15},{9,8},{10,9... | collective-permute-start | bytes 1572872 | tf_op jit(solution)/shard_map/ppermute | solution.py:75
  51.4 9.5 %collective-permute-start.13 = (bf16[8,8,4096]{2,1,0:T(8,128)(2,1)S(1)}, bf16[8,8,4096]{2,1,0:T(8,128)(2,1)S(1)}, u32[]{:S(2)}, u32[]{:S(2)}) collective-permute-start(bf16[8,8,4096]{2,1,0:T(8,128)(2,1)S(1)} %collective-permute-done.12.refs_1_), channel_id=1, source_target_pairs={{0,1},{1,2},{2,3},{3,4},{4,5},{5,6},{6,7},{7,0},{8,9},{9,10},{10,1... | collective-permute-start | bytes 1572872 | tf_op jit(solution)/shard_map/ppermute | solution.py:75
  52.7 13.7 %collective-permute-start.18 = (bf16[2,8,8,4096]{3,2,1,0:T(8,128)(2,1)S(1)}, bf16[2,8,8,4096]{3,2,1,0:T(8,128)(2,1)S(1)}, u32[]{:S(2)}, u32[]{:S(2)}) collective-permute-start(bf16[2,8,8,4096]{3,2,1,0:T(8,128)(2,1)S(1)} %pack.4.refs_0_), channel_id=1, source_target_pairs={{0,64},{1,65},{2,66},{3,67},{4,68},{5,69},{6,70},{7,71},{8,72},{9,... | collective-permute-start | bytes 3145736 | tf_op jit(solution)/shard_map/ppermute | solution.py:75
  61.0 7.3 %collective-permute-start.17 = (bf16[2,8,8,4096]{3,2,1,0:T(8,128)(2,1)S(1)}, bf16[2,8,8,4096]{3,2,1,0:T(8,128)(2,1)S(1)}, u32[]{:S(2)}, u32[]{:S(2)}) collective-permute-start(bf16[2,8,8,4096]{3,2,1,0:T(8,128)(2,1)S(1)} %pack.5.refs_0_), channel_id=1, source_target_pairs={{0,64},{1,65},{2,66},{3,67},{4,68},{5,69},{6,70},{7,71},{8,72},{9,... | collective-permute-start | bytes 3145736 | tf_op jit(solution)/shard_map/ppermute | solution.py:75
  63.8 5.9 %collective-permute-start.14 = (bf16[4,8,4096]{2,1,0:T(8,128)(2,1)S(1)}, bf16[4,8,4096]{2,1,0:T(8,128)(2,1)S(1)}, u32[]{:S(2)}, u32[]{:S(2)}) collective-permute-start(bf16[4,8,4096]{2,1,0:T(8,128)(2,1)S(1)} %get-tuple-element.28), channel_id=1, source_target_pairs={{0,7},{1,0},{2,1},{3,2},{4,3},{5,4},{6,5},{7,6},{8,15},{9,8},{10,9... | collective-permute-start | bytes 786440 | tf_op jit(solution)/shard_map/ppermute | solution.py:75
  66.4 6.4 %collective-permute-start.15 = (bf16[4,8,4096]{2,1,0:T(8,128)(2,1)S(1)}, bf16[4,8,4096]{2,1,0:T(8,128)(2,1)S(1)}, u32[]{:S(2)}, u32[]{:S(2)}) collective-permute-start(bf16[4,8,4096]{2,1,0:T(8,128)(2,1)S(1)} %get-tuple-element.29), channel_id=1, source_target_pairs={{0,1},{1,2},{2,3},{3,4},{4,5},{5,6},{6,7},{7,0},{8,9},{9,10},{10,1... | collective-permute-start | bytes 786440 | tf_op jit(solution)/shard_map/ppermute | solution.py:75
  72.8 2.0 %collective-permute-start.19 = (bf16[8,8,4096]{2,1,0:T(8,128)(2,1)S(1)}, bf16[8,8,4096]{2,1,0:T(8,128)(2,1)S(1)}, u32[]{:S(2)}, u32[]{:S(2)}) collective-permute-start(bf16[8,8,4096]{2,1,0:T(8,128)(2,1)S(1)} %last.1.refs_0_), channel_id=1, source_target_pairs={{0,64},{1,65},{2,66},{3,67},{4,68},{5,69},{6,70},{7,71},{8,72},{9,... | collective-permute-start | bytes 1572872 | tf_op jit(solution)/shard_map/ppermute | solution.py:75

commit v6 on v5

--- a/solution.py
+++ b/solution.py
@@ -18,6 +18,7 @@
 HALF = 4096
 ROWS = 8
 RING = 8
+SPLIT = 5
 
 
 def all_places():
@@ -144,7 +145,7 @@
 def bundle_kernel(*refs):
     *couples, out = refs
     core, x_hi, y, z = my_core(), my_x_hi(), my_y(), my_z()
-    for step, couple in enumerate(couples):
+    for step, couple in zip((0, 2, 1, 3), couples):
         for i in range(2):
             at = jnp.where(core == 0, (x_hi ^ i) * 4 + lax.rem(y + step, 4), lax.rem((z ^ i) + 2 * step, 8))
             out[pl.ds(at, 1)] = couple[i][None]
@@ -155,12 +156,12 @@
         refs[-1][i] = refs[i][...]
 
 
-def cut_kernel(ahead, behind, low, high):
-    low[...], high[...] = ahead[:4], behind[4:]
+def cut_kernel(start, bundle, part):
+    part[...] = bundle[start:start + part.shape[0]]
 
 
 def last_kernel(low, high, *refs):
-    refs[-1][:4], refs[-1][4:] = low[...], high[...]
+    refs[-1][:SPLIT], refs[-1][SPLIT:] = low[...], high[...]
 
 
 def assemble_kernel(own, other, ends, *refs):
@@ -269,15 +270,17 @@
     couple, = local(
         couple_kernel, [((2, *half), bf16)], (fresh, other, stepped), name="couple", in_specs=[VMEM] * 2 + [ANY],
     )
-    couples = [couple] + [send(couple, by_core(along_y(-step), along_z(-2 * step))) for step in (1, 2, 3)]
+    couples = [couple] + [send(couple, by_core(along_y(-step), along_z(-2 * step))) for step in (2, 1, 3)]
     bundle, = local(bundle_kernel, [((8, *half), bf16)], couples, name="bundle")
 
     ahead, behind = by_core(along_z(-1), along_snake(-1)), by_core(along_z(1), along_snake(1))
     got = {0: bundle}
     for step in (1, 2, 3):
         got[step], got[-step] = send(got[step - 1], ahead), send(got[1 - step], behind)
-    low, high = local(cut_kernel, [((4, *half), bf16)] * 2, (got[3], got[-3]), name="cut")
-    low, high = send(low, ahead), send(high, behind)
+    def cut(bundle, start, count):
+        return local(functools.partial(cut_kernel, start), [((count, *half), bf16)], (bundle,), name="cut", grant=1 << 20)[0]
+
+    low, high = send(cut(got[3], 0, SPLIT), ahead), send(cut(got[-3], SPLIT, 8 - SPLIT), behind)
 
     out, theirs, after = None, [], ()
     for steps in ([0, 1, -1], [2, -2], [3, -3]):

time: 75.8 us -> 74.7 us (0.985)
  waiting for transfers between devices: 33.2 us -> 31.1 us
  starting transfers between devices: 30.9 us -> 31.8 us
    ppermute x20, waiting for transfers between devices: 33.2 us -> 31.1 us  [send(): return lax.ppermute(x, AXES, to)]
    ppermute x20, starting transfers between devices: 30.9 us -> 31.8 us  [send(): return lax.ppermute(x, AXES, to)]
    pallas_call x10 -> x11, Pallas kernels: 2.53 us -> 2.53 us  [local(): pl.pallas_call(kernel, out_shape=tuple((shape(*out) for out in outs)), in...]
where the time goes in v6:
time: 74.7 us; the launch traced here: 74.6 us
  starting transfers between devices  31.8 us (43%)
  waiting for transfers between devices  31.1 us (42%)
  Pallas kernels  9.85 us (13%)
  other arithmetic  0.97 us (1%)
  between operations  0.78 us (1%)
    ppermute x20, starting transfers between devices, send(): return lax.ppermute(x, AXES, to)  31.8 us
    ppermute x20, waiting for transfers between devices, send(): return lax.ppermute(x, AXES, to)  31.1 us
    pallas_call x6, Pallas kernels, assemble(): pl.pallas_call(functools.partial(assemble_kernel, *placed, ends), out_sha...  7.32 us
    pallas_call x11, Pallas kernels, local(): pl.pallas_call(kernel, out_shape=tuple((shape(*out) for out in outs)), in...  2.53 us
  transfers between devices with their start and end apart: 20, of which 12 were waited for; matrix products, arithmetic and copies ran while one was open for 1% of the time, Pallas kernels for 10%

profile of v6, /device:TPU:1, one launch (start us, length us, event | category | flops | bytes accessed | tf_op | source)
XLA Modules:
  0.0 74.6 jit_solution(1667587255748460653)
XLA Ops:
  0.6 1.2 %encode.1 = (bf16[8,4096]{1,0:T(8,128)(2,1)S(1)}, bf16[8,4096]{1,0:T(8,128)(2,1)S(1)}, f32[8,8192]{1,0:T(8,128)S(1)}) custom-call(bf16[1,8,8192]{2,1,0:T(8,128)(2,1)} %weights.1, f32[8,8192]{1,0:T(8,128)} %base.1), custom_call_target="tpu_custom_call" | custom-call | flops 1048576 | bytes 1048576 | tf_op jit(solution)/shard_map/encode/pallas_call | solution.py:210
  1.9 3.3 %collective-permute-start = (bf16[8,4096]{1,0:T(8,128)(2,1)S(1)}, bf16[8,4096]{1,0:T(8,128)(2,1)S(1)}, u32[]{:S(2)}, u32[]{:S(2)}) collective-permute-start(bf16[8,4096]{1,0:T(8,128)(2,1)S(1)} %get-tuple-element.19), channel_id=1, source_target_pairs={{0,64},{1,65},{2,66},{3,67},{4,68},{5,69},{6,70},{7,71},{8,72},{9,... | collective-permute-start | bytes 196616 | tf_op jit(solution)/shard_map/ppermute | solution.py:76
  5.2 0.0 collective-permute-start.2
  5.2 1.4 %collective-permute-start.1 = (bf16[8,4096]{1,0:T(8,128)(2,1)S(1)}, bf16[8,4096]{1,0:T(8,128)(2,1)S(1)}, u32[]{:S(2)}, u32[]{:S(2)}) collective-permute-start(bf16[8,4096]{1,0:T(8,128)(2,1)S(1)} %get-tuple-element.18.keep), channel_id=1, source_target_pairs={{0,128},{1,129},{2,130},{3,131},{4,132},{5,133},{6,134},{7,135},{8... | collective-permute-start | bytes 196616 | tf_op jit(solution)/shard_map/ppermute | solution.py:76
  6.6 1.0 %broadcast_multiply_fusion.decayed = f32[8,8192]{1,0:T(8,128)S(1)} fusion(f32[8,8192]{1,0:T(8,128)} %param.5), kind=kLoop, calls=%fused_computation | loop fusion | flops 65536 | bytes 524288 | tf_op jit(solution)/shard_map/mul | solution.py:249
  7.6 0.0 collective-permute-done.from_core
  7.6 2.5 %collective-permute-done.1.from_chip = bf16[8,4096]{1,0:T(8,128)(2,1)S(1)} collective-permute-done((bf16[8,4096]{1,0:T(8,128)(2,1)S(1)}, bf16[8,4096]{1,0:T(8,128)(2,1)S(1)}, u32[]{:S(2)}, u32[]{:S(2)}) %collective-permute-start.1) | collective-permute-done | bytes 65568 | tf_op jit(solution)/shard_map/ppermute | solution.py:76
  10.1 0.0 collective-permute-done.2.from_both
  10.1 0.1 half_step.1
  10.2 1.0 %collective-permute-start.3 = (f32[8,4096]{1,0:T(8,128)S(1)}, f32[8,4096]{1,0:T(8,128)S(1)}, u32[]{:S(2)}, u32[]{:S(2)}) collective-permute-start(f32[8,4096]{1,0:T(8,128)S(1)} %get-tuple-element.21.mine), channel_id=1, source_target_pairs={{0,64},{1,65},{2,66},{3,67},{4,68},{5,69},{6,70},{7,71},{8,72},{9,... | collective-permute-start | bytes 393224 | tf_op jit(solution)/shard_map/ppermute | solution.py:76
  11.2 0.0 collective-permute-start.4
  11.2 1.0 %collective-permute-done.3.theirs = f32[8,4096]{1,0:T(8,128)S(1)} collective-permute-done((f32[8,4096]{1,0:T(8,128)S(1)}, f32[8,4096]{1,0:T(8,128)S(1)}, u32[]{:S(2)}, u32[]{:S(2)}) %collective-permute-start.3) | collective-permute-done | bytes 131104 | tf_op jit(solution)/shard_map/ppermute | solution.py:76
  12.2 0.9 %whole_step.1 = (f32[8,8192]{1,0:T(8,128)}, f32[8,8192]{1,0:T(8,128)}, f32[8,128]{1,0:T(8,128)S(1)}) custom-call(f32[8,4096]{1,0:T(8,128)S(1)} %get-tuple-element.21.mine, f32[8,4096]{1,0:T(8,128)S(1)} %collective-permute-done.3.theirs, f32[8,8192]{1,0:T(8,128)S(1)} %get-tuple-element.20.base, f32[8,8192]{1,0:T(8,128)S(1)} %broadcast_multiply_fusion.decayed), custom_call_target="tpu_custom_call" | custom-call | flops 1048576 | bytes 1048576 | tf_op jit(solution)/shard_map/whole_step/pallas_call | solution.py:210
  13.1 1.3 %collective-permute-done.4.other = bf16[8,4096]{1,0:T(8,128)(2,1)S(1)} collective-permute-done((bf16[8,4096]{1,0:T(8,128)(2,1)S(1)}, bf16[8,4096]{1,0:T(8,128)(2,1)S(1)}, u32[]{:S(2)}, u32[]{:S(2)}) %collective-permute-start.4) | collective-permute-done | bytes 65568 | tf_op jit(solution)/shard_map/ppermute | solution.py:76
  14.4 5.3 %collective-permute-start.5 = (bf16[2,8,4096]{2,1,0:T(8,128)(2,1)S(1)}, bf16[2,8,4096]{2,1,0:T(8,128)(2,1)S(1)}, u32[]{:S(2)}, u32[]{:S(2)}) collective-permute-start(bf16[2,8,4096]{2,1,0:T(8,128)(2,1)S(1)} %couple.1.refs_0_), channel_id=1, source_target_pairs={{0,16},{1,17},{2,18},{3,19},{4,20},{5,21},{6,22},{7,23},{8,24},{9,... | collective-permute-start | bytes 393224 | tf_op jit(solution)/shard_map/ppermute | solution.py:76
  19.6 0.0 collective-permute-start.6
  19.6 2.4 %collective-permute-start.7 = (bf16[2,8,4096]{2,1,0:T(8,128)(2,1)S(1)}, bf16[2,8,4096]{2,1,0:T(8,128)(2,1)S(1)}, u32[]{:S(2)}, u32[]{:S(2)}) collective-permute-start(bf16[2,8,4096]{2,1,0:T(8,128)(2,1)S(1)} %couple.1.refs_0_), channel_id=1, source_target_pairs={{0,8},{1,9},{2,10},{3,11},{4,12},{5,13},{6,14},{7,15},{8,16},{9,17... | collective-permute-start | bytes 393224 | tf_op jit(solution)/shard_map/ppermute | solution.py:76
  22.0 0.3 collective-permute-done.5.refs_1_
  22.3 4.4 %collective-permute-done.6.refs_2_ = bf16[2,8,4096]{2,1,0:T(8,128)(2,1)S(1)} collective-permute-done((bf16[2,8,4096]{2,1,0:T(8,128)(2,1)S(1)}, bf16[2,8,4096]{2,1,0:T(8,128)(2,1)S(1)}, u32[]{:S(2)}, u32[]{:S(2)}) %collective-permute-start.6) | collective-permute-done | bytes 131104 | tf_op jit(solution)/shard_map/ppermute | solution.py:76
  26.7 0.0 collective-permute-done.7.refs_3_
  26.7 0.1 bundle.1.refs_0_
  26.7 1.4 %collective-permute-start.12 = (bf16[8,8,4096]{2,1,0:T(8,128)(2,1)S(1)}, bf16[8,8,4096]{2,1,0:T(8,128)(2,1)S(1)}, u32[]{:S(2)}, u32[]{:S(2)}) collective-permute-start(bf16[8,8,4096]{2,1,0:T(8,128)(2,1)S(1)} %bundle.1.refs_0_), channel_id=1, source_target_pairs={{0,1},{1,2},{2,3},{3,4},{4,5},{5,6},{6,7},{7,0},{8,9},{9,10},{10,1... | collective-permute-start | bytes 1572872 | tf_op jit(solution)/shard_map/ppermute | solution.py:76
  28.1 1.4 %collective-permute-start.8 = (bf16[8,8,4096]{2,1,0:T(8,128)(2,1)S(1)}, bf16[8,8,4096]{2,1,0:T(8,128)(2,1)S(1)}, u32[]{:S(2)}, u32[]{:S(2)}) collective-permute-start(bf16[8,8,4096]{2,1,0:T(8,128)(2,1)S(1)} %bundle.1.refs_0_), channel_id=1, source_target_pairs={{0,7},{1,0},{2,1},{3,2},{4,3},{5,4},{6,5},{7,6},{8,15},{9,8},{10,9... | collective-permute-start | bytes 1572872 | tf_op jit(solution)/shard_map/ppermute | solution.py:76
  29.5 6.9 %collective-permute-done.12.refs_2_ = bf16[8,8,4096]{2,1,0:T(8,128)(2,1)S(1)} collective-permute-done((bf16[8,8,4096]{2,1,0:T(8,128)(2,1)S(1)}, bf16[8,8,4096]{2,1,0:T(8,128)(2,1)S(1)}, u32[]{:S(2)}, u32[]{:S(2)}) %collective-permute-start.12) | collective-permute-done | bytes 524320 | tf_op jit(solution)/shard_map/ppermute | solution.py:76
  36.3 0.1 collective-permute-done.8.refs_1_
  36.4 0.1 pack.3.refs_0_
  36.5 2.4 %collective-permute-start.16 = (bf16[3,8,8,4096]{3,2,1,0:T(8,128)(2,1)S(1)}, bf16[3,8,8,4096]{3,2,1,0:T(8,128)(2,1)S(1)}, u32[]{:S(2)}, u32[]{:S(2)}) collective-permute-start(bf16[3,8,8,4096]{3,2,1,0:T(8,128)(2,1)S(1)} %pack.3.refs_0_), channel_id=1, source_target_pairs={{0,64},{1,65},{2,66},{3,67},{4,68},{5,69},{6,70},{7,71},{8,72},{9,... | collective-permute-start | bytes 4718600 | tf_op jit(solution)/shard_map/ppermute | solution.py:76
  39.0 2.5 %collective-permute-start.9 = (bf16[8,8,4096]{2,1,0:T(8,128)(2,1)S(1)}, bf16[8,8,4096]{2,1,0:T(8,128)(2,1)S(1)}, u32[]{:S(2)}, u32[]{:S(2)}) collective-permute-start(bf16[8,8,4096]{2,1,0:T(8,128)(2,1)S(1)} %collective-permute-done.8.refs_1_), channel_id=1, source_target_pairs={{0,7},{1,0},{2,1},{3,2},{4,3},{5,4},{6,5},{7,6},{8,15},{9,8},{10,9... | collective-permute-start | bytes 1572872 | tf_op jit(solution)/shard_map/ppermute | solution.py:76
  41.4 0.0 collective-permute-start.13
  41.4 6.1 %collective-permute-done.9.refs_0_ = bf16[8,8,4096]{2,1,0:T(8,128)(2,1)S(1)} collective-permute-done((bf16[8,8,4096]{2,1,0:T(8,128)(2,1)S(1)}, bf16[8,8,4096]{2,1,0:T(8,128)(2,1)S(1)}, u32[]{:S(2)}, u32[]{:S(2)}) %collective-permute-start.9) | collective-permute-done | bytes 524320 | tf_op jit(solution)/shard_map/ppermute | solution.py:76
  47.6 3.4 %collective-permute-start.10 = (bf16[8,8,4096]{2,1,0:T(8,128)(2,1)S(1)}, bf16[8,8,4096]{2,1,0:T(8,128)(2,1)S(1)}, u32[]{:S(2)}, u32[]{:S(2)}) collective-permute-start(bf16[8,8,4096]{2,1,0:T(8,128)(2,1)S(1)} %collective-permute-done.9.refs_0_), channel_id=1, source_target_pairs={{0,7},{1,0},{2,1},{3,2},{4,3},{5,4},{6,5},{7,6},{8,15},{9,8},{10,9... | collective-permute-start | bytes 1572872 | tf_op jit(solution)/shard_map/ppermute | solution.py:76
  51.0 0.0 collective-permute-done.13.refs_1_
  51.0 0.0 collective-permute-start.14
  51.0 1.2 %assemble.6 = (bf16[8,8,8,8192]{3,2,1,0:T(8,128)(2,1)}, f32[8,128]{1,0:T(8,128)S(1)}) custom-call(bf16[3,8,8,4096]{3,2,1,0:T(8,128)(2,1)S(1)} %pack.3.refs_0_), custom_call_target="tpu_custom_call" | custom-call | flops 3145728 | bytes 3145728 | tf_op jit(solution)/shard_map/assemble/pallas_call | solution.py:230
  52.2 0.1 pack.4.refs_0_
  52.2 1.9 %collective-permute-start.18 = (bf16[2,8,8,4096]{3,2,1,0:T(8,128)(2,1)S(1)}, bf16[2,8,8,4096]{3,2,1,0:T(8,128)(2,1)S(1)}, u32[]{:S(2)}, u32[]{:S(2)}) collective-permute-start(bf16[2,8,8,4096]{3,2,1,0:T(8,128)(2,1)S(1)} %pack.4.refs_0_), channel_id=1, source_target_pairs={{0,64},{1,65},{2,66},{3,67},{4,68},{5,69},{6,70},{7,71},{8,72},{9,... | collective-permute-start | bytes 3145736 | tf_op jit(solution)/shard_map/ppermute | solution.py:76
  54.1 0.0 collective-permute-done.16.refs_1_
  54.1 1.5 %assemble.7 = (bf16[8,8,8,8192]{3,2,1,0:T(8,128)(2,1)}, f32[8,128]{1,0:T(8,128)S(1)}) custom-call(bf16[2,8,8,4096]{3,2,1,0:T(8,128)(2,1)S(1)} %pack.4.refs_0_, bf16[3,8,8,4096]{3,2,1,0:T(8,128)(2,1)S(1)} %collective-permute-done.16.refs_1_, bf16[8,8,8,8192]{3,2,1,0:T(8,128)(2,1)} %get-tuple-element.27.refs_2_), custom_call_target="tpu_custom_call", output_to_operand_aliasing={{0}: (2, {})} | custom-call | flops 5242880 | bytes 5242880 | tf_op jit(solution)/shard_map/assemble/pallas_call | solution.py:230
  55.6 1.5 %collective-permute-done.10.bundle.refs_0_ = bf16[8,8,4096]{2,1,0:T(8,128)(2,1)S(1)} collective-permute-done((bf16[8,8,4096]{2,1,0:T(8,128)(2,1)S(1)}, bf16[8,8,4096]{2,1,0:T(8,128)(2,1)S(1)}, u32[]{:S(2)}, u32[]{:S(2)}) %collective-permute-start.10) | collective-permute-done | bytes 524320 | tf_op jit(solution)/shard_map/ppermute | solution.py:76
  57.1 3.4 %collective-permute-done.14.bundle.refs_1_ = bf16[8,8,4096]{2,1,0:T(8,128)(2,1)S(1)} collective-permute-done((bf16[8,8,4096]{2,1,0:T(8,128)(2,1)S(1)}, bf16[8,8,4096]{2,1,0:T(8,128)(2,1)S(1)}, u32[]{:S(2)}, u32[]{:S(2)}) %collective-permute-start.14) | collective-permute-done | bytes 524320 | tf_op jit(solution)/shard_map/ppermute | solution.py:76
  60.5 0.1 pack.5.refs_0_
  60.6 2.7 %collective-permute-start.17 = (bf16[2,8,8,4096]{3,2,1,0:T(8,128)(2,1)S(1)}, bf16[2,8,8,4096]{3,2,1,0:T(8,128)(2,1)S(1)}, u32[]{:S(2)}, u32[]{:S(2)}) collective-permute-start(bf16[2,8,8,4096]{3,2,1,0:T(8,128)(2,1)S(1)} %pack.5.refs_0_), channel_id=1, source_target_pairs={{0,64},{1,65},{2,66},{3,67},{4,68},{5,69},{6,70},{7,71},{8,72},{9,... | collective-permute-start | bytes 3145736 | tf_op jit(solution)/shard_map/ppermute | solution.py:76
  63.3 2.6 %collective-permute-start.11 = (bf16[5,8,4096]{2,1,0:T(8,128)(2,1)S(1)}, bf16[5,8,4096]{2,1,0:T(8,128)(2,1)S(1)}, u32[]{:S(2)}, u32[]{:S(2)}) collective-permute-start(bf16[5,8,4096]{2,1,0:T(8,128)(2,1)S(1)} %cut.2), channel_id=1, source_target_pairs={{0,7},{1,0},{2,1},{3,2},{4,3},{5,4},{6,5},{7,6},{8,15},{9,8},{10,9... | collective-permute-start | bytes 983048 | tf_op jit(solution)/shard_map/ppermute | solution.py:76
  65.9 0.1 collective-permute-start.15
  66.0 0.0 collective-permute-done.18.refs_1_
  66.0 2.0 %assemble.8 = (bf16[8,8,8,8192]{3,2,1,0:T(8,128)(2,1)}, f32[8,128]{1,0:T(8,128)}) custom-call(bf16[2,8,8,4096]{3,2,1,0:T(8,128)(2,1)S(1)} %pack.5.refs_0_, bf16[2,8,8,4096]{3,2,1,0:T(8,128)(2,1)S(1)} %collective-permute-done.18.refs_1_, bf16[8,8,8,8192]{3,2,1,0:T(8,128)(2,1)} %get-tuple-element.29.refs_2_), custom_call_target="tpu_custom_call", output_to_operand_aliasing={{0}: (2, {})} | custom-call | flops 4194304 | bytes 4194304 | tf_op jit(solution)/shard_map/assemble/pallas_call | solution.py:230
  68.0 0.0 collective-permute-done.17.refs_0_
  68.0 1.0 %assemble.9 = (bf16[8,8,8,8192]{3,2,1,0:T(8,128)(2,1)}, f32[8,128]{1,0:T(8,128)S(1)}) custom-call(bf16[2,8,8,4096]{3,2,1,0:T(8,128)(2,1)S(1)} %collective-permute-done.17.refs_0_, bf16[8,8,8,8192]{3,2,1,0:T(8,128)(2,1)} %get-tuple-element.30.refs_1_), custom_call_target="tpu_custom_call", output_to_operand_aliasing={{0}: (1, {})} | custom-call | flops 2097152 | bytes 2097152 | tf_op jit(solution)/shard_map/assemble/pallas_call | solution.py:230
  69.0 2.7 %collective-permute-done.15.high = bf16[3,8,4096]{2,1,0:T(8,128)(2,1)S(1)} collective-permute-done((bf16[3,8,4096]{2,1,0:T(8,128)(2,1)S(1)}, bf16[3,8,4096]{2,1,0:T(8,128)(2,1)S(1)}, u32[]{:S(2)}, u32[]{:S(2)}) %collective-permute-start.15) | collective-permute-done | bytes 196640 | tf_op jit(solution)/shard_map/ppermute | solution.py:76
  71.7 0.0 collective-permute-done.11.low
  71.8 0.1 collective-permute-start.19
  71.9 0.8 %assemble.10.refs_1_ = bf16[8,8,8,8192]{3,2,1,0:T(8,128)(2,1)} custom-call(bf16[8,8,4096]{2,1,0:T(8,128)(2,1)S(1)} %last.1.refs_0_, bf16[8,8,8,8192]{3,2,1,0:T(8,128)(2,1)} %get-tuple-element.32.refs_1_), custom_call_target="tpu_custom_call", output_to_operand_aliasing={{}: (1, {})} | custom-call | flops 1048576 | bytes 1048576 | tf_op jit(solution)/shard_map/assemble/pallas_call | solution.py:230
  72.7 1.1 %collective-permute-done.19.refs_0_ = bf16[8,8,4096]{2,1,0:T(8,128)(2,1)S(1)} collective-permute-done((bf16[8,8,4096]{2,1,0:T(8,128)(2,1)S(1)}, bf16[8,8,4096]{2,1,0:T(8,128)(2,1)S(1)}, u32[]{:S(2)}, u32[]{:S(2)}) %collective-permute-start.19) | collective-permute-done | bytes 524320 | tf_op jit(solution)/shard_map/ppermute | solution.py:76
  73.8 0.8 %assemble.11 = bf16[8,8,8,8192]{3,2,1,0:T(8,128)(2,1)} custom-call(bf16[8,8,4096]{2,1,0:T(8,128)(2,1)S(1)} %collective-permute-done.19.refs_0_, bf16[8,8,8,8192]{3,2,1,0:T(8,128)(2,1)} %assemble.10.refs_1_), custom_call_target="tpu_custom_call", output_to_operand_aliasing={{}: (1, {})} | custom-call | flops 1048576 | bytes 1048576 | tf_op jit(solution)/shard_map/assemble/pallas_call | solution.py:230
  (4 shorter events, 0.1 us)
Async XLA Ops:
  1.9 5.8 %collective-permute-start = (bf16[8,4096]{1,0:T(8,128)(2,1)S(1)}, bf16[8,4096]{1,0:T(8,128)(2,1)S(1)}, u32[]{:S(2)}, u32[]{:S(2)}) collective-permute-start(bf16[8,4096]{1,0:T(8,128)(2,1)S(1)} %get-tuple-element.19), channel_id=1, source_target_pairs={{0,64},{1,65},{2,66},{3,67},{4,68},{5,69},{6,70},{7,71},{8,72},{9,... | collective-permute-start | bytes 196616 | tf_op jit(solution)/shard_map/ppermute | solution.py:76
  5.2 5.0 %collective-permute-start.2 = (bf16[8,4096]{1,0:T(8,128)(2,1)S(1)}, bf16[8,4096]{1,0:T(8,128)(2,1)S(1)}, u32[]{:S(2)}, u32[]{:S(2)}) collective-permute-start(bf16[8,4096]{1,0:T(8,128)(2,1)S(1)} %get-tuple-element.19), channel_id=1, source_target_pairs={{0,192},{1,193},{2,194},{3,195},{4,196},{5,197},{6,198},{7,199},{8... | collective-permute-start | bytes 196616 | tf_op jit(solution)/shard_map/ppermute | solution.py:76
  5.2 4.9 %collective-permute-start.1 = (bf16[8,4096]{1,0:T(8,128)(2,1)S(1)}, bf16[8,4096]{1,0:T(8,128)(2,1)S(1)}, u32[]{:S(2)}, u32[]{:S(2)}) collective-permute-start(bf16[8,4096]{1,0:T(8,128)(2,1)S(1)} %get-tuple-element.18.keep), channel_id=1, source_target_pairs={{0,128},{1,129},{2,130},{3,131},{4,132},{5,133},{6,134},{7,135},{8... | collective-permute-start | bytes 196616 | tf_op jit(solution)/shard_map/ppermute | solution.py:76
  10.2 2.0 %collective-permute-start.3 = (f32[8,4096]{1,0:T(8,128)S(1)}, f32[8,4096]{1,0:T(8,128)S(1)}, u32[]{:S(2)}, u32[]{:S(2)}) collective-permute-start(f32[8,4096]{1,0:T(8,128)S(1)} %get-tuple-element.21.mine), channel_id=1, source_target_pairs={{0,64},{1,65},{2,66},{3,67},{4,68},{5,69},{6,70},{7,71},{8,72},{9,... | collective-permute-start | bytes 393224 | tf_op jit(solution)/shard_map/ppermute | solution.py:76
  11.2 3.1 %collective-permute-start.4 = (bf16[8,4096]{1,0:T(8,128)(2,1)S(1)}, bf16[8,4096]{1,0:T(8,128)(2,1)S(1)}, u32[]{:S(2)}, u32[]{:S(2)}) collective-permute-start(bf16[8,4096]{1,0:T(8,128)(2,1)S(1)} %get-tuple-element.24.own), channel_id=1, source_target_pairs={{0,160},{1,161},{2,162},{3,163},{4,164},{5,165},{6,166},{7,167},{8... | collective-permute-start | bytes 196616 | tf_op jit(solution)/shard_map/ppermute | solution.py:76
  14.4 7.9 %collective-permute-start.5 = (bf16[2,8,4096]{2,1,0:T(8,128)(2,1)S(1)}, bf16[2,8,4096]{2,1,0:T(8,128)(2,1)S(1)}, u32[]{:S(2)}, u32[]{:S(2)}) collective-permute-start(bf16[2,8,4096]{2,1,0:T(8,128)(2,1)S(1)} %couple.1.refs_0_), channel_id=1, source_target_pairs={{0,16},{1,17},{2,18},{3,19},{4,20},{5,21},{6,22},{7,23},{8,24},{9,... | collective-permute-start | bytes 393224 | tf_op jit(solution)/shard_map/ppermute | solution.py:76
  19.6 7.0 %collective-permute-start.6 = (bf16[2,8,4096]{2,1,0:T(8,128)(2,1)S(1)}, bf16[2,8,4096]{2,1,0:T(8,128)(2,1)S(1)}, u32[]{:S(2)}, u32[]{:S(2)}) collective-permute-start(bf16[2,8,4096]{2,1,0:T(8,128)(2,1)S(1)} %couple.1.refs_0_), channel_id=1, source_target_pairs={{0,24},{1,25},{2,26},{3,27},{4,28},{5,29},{6,30},{7,31},{8,0},{9,1... | collective-permute-start | bytes 393224 | tf_op jit(solution)/shard_map/ppermute | solution.py:76
  19.6 7.0 %collective-permute-start.7 = (bf16[2,8,4096]{2,1,0:T(8,128)(2,1)S(1)}, bf16[2,8,4096]{2,1,0:T(8,128)(2,1)S(1)}, u32[]{:S(2)}, u32[]{:S(2)}) collective-permute-start(bf16[2,8,4096]{2,1,0:T(8,128)(2,1)S(1)} %couple.1.refs_0_), channel_id=1, source_target_pairs={{0,8},{1,9},{2,10},{3,11},{4,12},{5,13},{6,14},{7,15},{8,16},{9,17... | collective-permute-start | bytes 393224 | tf_op jit(solution)/shard_map/ppermute | solution.py:76
  26.7 9.6 %collective-permute-start.12 = (bf16[8,8,4096]{2,1,0:T(8,128)(2,1)S(1)}, bf16[8,8,4096]{2,1,0:T(8,128)(2,1)S(1)}, u32[]{:S(2)}, u32[]{:S(2)}) collective-permute-start(bf16[8,8,4096]{2,1,0:T(8,128)(2,1)S(1)} %bundle.1.refs_0_), channel_id=1, source_target_pairs={{0,1},{1,2},{2,3},{3,4},{4,5},{5,6},{6,7},{7,0},{8,9},{9,10},{10,1... | collective-permute-start | bytes 1572872 | tf_op jit(solution)/shard_map/ppermute | solution.py:76
  28.1 8.3 %collective-permute-start.8 = (bf16[8,8,4096]{2,1,0:T(8,128)(2,1)S(1)}, bf16[8,8,4096]{2,1,0:T(8,128)(2,1)S(1)}, u32[]{:S(2)}, u32[]{:S(2)}) collective-permute-start(bf16[8,8,4096]{2,1,0:T(8,128)(2,1)S(1)} %bundle.1.refs_0_), channel_id=1, source_target_pairs={{0,7},{1,0},{2,1},{3,2},{4,3},{5,4},{6,5},{7,6},{8,15},{9,8},{10,9... | collective-permute-start | bytes 1572872 | tf_op jit(solution)/shard_map/ppermute | solution.py:76
  36.5 17.6 %collective-permute-start.16 = (bf16[3,8,8,4096]{3,2,1,0:T(8,128)(2,1)S(1)}, bf16[3,8,8,4096]{3,2,1,0:T(8,128)(2,1)S(1)}, u32[]{:S(2)}, u32[]{:S(2)}) collective-permute-start(bf16[3,8,8,4096]{3,2,1,0:T(8,128)(2,1)S(1)} %pack.3.refs_0_), channel_id=1, source_target_pairs={{0,64},{1,65},{2,66},{3,67},{4,68},{5,69},{6,70},{7,71},{8,72},{9,... | collective-permute-start | bytes 4718600 | tf_op jit(solution)/shard_map/ppermute | solution.py:76
  39.0 8.6 %collective-permute-start.9 = (bf16[8,8,4096]{2,1,0:T(8,128)(2,1)S(1)}, bf16[8,8,4096]{2,1,0:T(8,128)(2,1)S(1)}, u32[]{:S(2)}, u32[]{:S(2)}) collective-permute-start(bf16[8,8,4096]{2,1,0:T(8,128)(2,1)S(1)} %collective-permute-done.8.refs_1_), channel_id=1, source_target_pairs={{0,7},{1,0},{2,1},{3,2},{4,3},{5,4},{6,5},{7,6},{8,15},{9,8},{10,9... | collective-permute-start | bytes 1572872 | tf_op jit(solution)/shard_map/ppermute | solution.py:76
  41.4 9.5 %collective-permute-start.13 = (bf16[8,8,4096]{2,1,0:T(8,128)(2,1)S(1)}, bf16[8,8,4096]{2,1,0:T(8,128)(2,1)S(1)}, u32[]{:S(2)}, u32[]{:S(2)}) collective-permute-start(bf16[8,8,4096]{2,1,0:T(8,128)(2,1)S(1)} %collective-permute-done.12.refs_2_), channel_id=1, source_target_pairs={{0,1},{1,2},{2,3},{3,4},{4,5},{5,6},{6,7},{7,0},{8,9},{9,10},{10,1... | collective-permute-start | bytes 1572872 | tf_op jit(solution)/shard_map/ppermute | solution.py:76
  47.6 9.5 %collective-permute-start.10 = (bf16[8,8,4096]{2,1,0:T(8,128)(2,1)S(1)}, bf16[8,8,4096]{2,1,0:T(8,128)(2,1)S(1)}, u32[]{:S(2)}, u32[]{:S(2)}) collective-permute-start(bf16[8,8,4096]{2,1,0:T(8,128)(2,1)S(1)} %collective-permute-done.9.refs_0_), channel_id=1, source_target_pairs={{0,7},{1,0},{2,1},{3,2},{4,3},{5,4},{6,5},{7,6},{8,15},{9,8},{10,9... | collective-permute-start | bytes 1572872 | tf_op jit(solution)/shard_map/ppermute | solution.py:76
  51.0 9.5 %collective-permute-start.14 = (bf16[8,8,4096]{2,1,0:T(8,128)(2,1)S(1)}, bf16[8,8,4096]{2,1,0:T(8,128)(2,1)S(1)}, u32[]{:S(2)}, u32[]{:S(2)}) collective-permute-start(bf16[8,8,4096]{2,1,0:T(8,128)(2,1)S(1)} %collective-permute-done.13.refs_1_), channel_id=1, source_target_pairs={{0,1},{1,2},{2,3},{3,4},{4,5},{5,6},{6,7},{7,0},{8,9},{9,10},{10,1... | collective-permute-start | bytes 1572872 | tf_op jit(solution)/shard_map/ppermute | solution.py:76
  52.2 13.8 %collective-permute-start.18 = (bf16[2,8,8,4096]{3,2,1,0:T(8,128)(2,1)S(1)}, bf16[2,8,8,4096]{3,2,1,0:T(8,128)(2,1)S(1)}, u32[]{:S(2)}, u32[]{:S(2)}) collective-permute-start(bf16[2,8,8,4096]{3,2,1,0:T(8,128)(2,1)S(1)} %pack.4.refs_0_), channel_id=1, source_target_pairs={{0,64},{1,65},{2,66},{3,67},{4,68},{5,69},{6,70},{7,71},{8,72},{9,... | collective-permute-start | bytes 3145736 | tf_op jit(solution)/shard_map/ppermute | solution.py:76
  60.6 7.4 %collective-permute-start.17 = (bf16[2,8,8,4096]{3,2,1,0:T(8,128)(2,1)S(1)}, bf16[2,8,8,4096]{3,2,1,0:T(8,128)(2,1)S(1)}, u32[]{:S(2)}, u32[]{:S(2)}) collective-permute-start(bf16[2,8,8,4096]{3,2,1,0:T(8,128)(2,1)S(1)} %pack.5.refs_0_), channel_id=1, source_target_pairs={{0,64},{1,65},{2,66},{3,67},{4,68},{5,69},{6,70},{7,71},{8,72},{9,... | collective-permute-start | bytes 3145736 | tf_op jit(solution)/shard_map/ppermute | solution.py:76
  63.3 8.4 %collective-permute-start.11 = (bf16[5,8,4096]{2,1,0:T(8,128)(2,1)S(1)}, bf16[5,8,4096]{2,1,0:T(8,128)(2,1)S(1)}, u32[]{:S(2)}, u32[]{:S(2)}) collective-permute-start(bf16[5,8,4096]{2,1,0:T(8,128)(2,1)S(1)} %cut.2), channel_id=1, source_target_pairs={{0,7},{1,0},{2,1},{3,2},{4,3},{5,4},{6,5},{7,6},{8,15},{9,8},{10,9... | collective-permute-start | bytes 983048 | tf_op jit(solution)/shard_map/ppermute | solution.py:76
  65.9 5.8 %collective-permute-start.15 = (bf16[3,8,4096]{2,1,0:T(8,128)(2,1)S(1)}, bf16[3,8,4096]{2,1,0:T(8,128)(2,1)S(1)}, u32[]{:S(2)}, u32[]{:S(2)}) collective-permute-start(bf16[3,8,4096]{2,1,0:T(8,128)(2,1)S(1)} %cut.3), channel_id=1, source_target_pairs={{0,1},{1,2},{2,3},{3,4},{4,5},{5,6},{6,7},{7,0},{8,9},{9,10},{10,1... | collective-permute-start | bytes 589832 | tf_op jit(solution)/shard_map/ppermute | solution.py:76
  71.8 2.0 %collective-permute-start.19 = (bf16[8,8,4096]{2,1,0:T(8,128)(2,1)S(1)}, bf16[8,8,4096]{2,1,0:T(8,128)(2,1)S(1)}, u32[]{:S(2)}, u32[]{:S(2)}) collective-permute-start(bf16[8,8,4096]{2,1,0:T(8,128)(2,1)S(1)} %last.1.refs_0_), channel_id=1, source_target_pairs={{0,64},{1,65},{2,66},{3,67},{4,68},{5,69},{6,70},{7,71},{8,72},{9,... | collective-permute-start | bytes 1572872 | tf_op jit(solution)/shard_map/ppermute | solution.py:76

commit v7 on v6

--- a/solution.py
+++ b/solution.py
@@ -283,7 +283,7 @@
     low, high = send(cut(got[3], 0, SPLIT), ahead), send(cut(got[-3], SPLIT, 8 - SPLIT), behind)
 
     out, theirs, after = None, [], ()
-    for steps in ([0, 1, -1], [2, -2], [3, -3]):
+    for steps in ([0, 1, -1], [2, -2, 3, -3]):
         packed = pack([got[step] for step in steps], after)
         out, written = assemble([(packed, steps)], theirs, out)
         theirs, after = [(swap(packed), steps)], (written,)

time: 74.7 us -> 72.5 us (0.971)
  starting transfers between devices: 31.8 us -> 30.8 us
    ppermute x20 -> x19, starting transfers between devices: 31.8 us -> 30.8 us  [send(): return lax.ppermute(x, AXES, to)]
    pallas_call x6 -> x5, Pallas kernels: 7.32 us -> 6.66 us  [assemble(): pl.pallas_call(functools.partial(assemble_kernel, *placed, ends), out_sha...]
    ppermute x20 -> x19, waiting for transfers between devices: 31.1 us -> 30.7 us  [send(): return lax.ppermute(x, AXES, to)]
    pallas_call x11 -> x10, Pallas kernels: 2.53 us -> 2.53 us  [local(): pl.pallas_call(kernel, out_shape=tuple((shape(*out) for out in outs)), in...]
  transfers between devices with their start and end apart: 20 -> 19, of which waited for: 12 -> 10; matrix products, arithmetic and copies ran while one was open for 1% -> 1% of each run, Pallas kernels for 10% -> 9%
where the time goes in v7:
time: 72.5 us; the launch traced here: 72.4 us
  starting transfers between devices  30.8 us (42%)
  waiting for transfers between devices  30.7 us (42%)
  Pallas kernels  9.19 us (13%)
  other arithmetic  0.97 us (1%)
  between operations  0.76 us (1%)
    ppermute x19, starting transfers between devices, send(): return lax.ppermute(x, AXES, to)  30.8 us
    ppermute x19, waiting for transfers between devices, send(): return lax.ppermute(x, AXES, to)  30.7 us
    pallas_call x5, Pallas kernels, assemble(): pl.pallas_call(functools.partial(assemble_kernel, *placed, ends), out_sha...  6.66 us
    pallas_call x10, Pallas kernels, local(): pl.pallas_call(kernel, out_shape=tuple((shape(*out) for out in outs)), in...  2.53 us
  transfers between devices with their start and end apart: 19, of which 10 were waited for; matrix products, arithmetic and copies ran while one was open for 1% of the time, Pallas kernels for 9%

profile of v7, /device:TPU:1, one launch (start us, length us, event | category | flops | bytes accessed | tf_op | source)
XLA Modules:
  0.0 72.4 jit_solution(1256883204194732695)
XLA Ops:
  0.6 1.2 %encode.1 = (bf16[8,4096]{1,0:T(8,128)(2,1)S(1)}, bf16[8,4096]{1,0:T(8,128)(2,1)S(1)}, f32[8,8192]{1,0:T(8,128)S(1)}) custom-call(bf16[1,8,8192]{2,1,0:T(8,128)(2,1)} %weights.1, f32[8,8192]{1,0:T(8,128)} %base.1), custom_call_target="tpu_custom_call" | custom-call | flops 1048576 | bytes 1048576 | tf_op jit(solution)/shard_map/encode/pallas_call | solution.py:210
  1.9 2.7 %collective-permute-start.2 = (bf16[8,4096]{1,0:T(8,128)(2,1)S(1)}, bf16[8,4096]{1,0:T(8,128)(2,1)S(1)}, u32[]{:S(2)}, u32[]{:S(2)}) collective-permute-start(bf16[8,4096]{1,0:T(8,128)(2,1)S(1)} %get-tuple-element.17), channel_id=1, source_target_pairs={{0,192},{1,193},{2,194},{3,195},{4,196},{5,197},{6,198},{7,199},{8... | collective-permute-start | bytes 196616 | tf_op jit(solution)/shard_map/ppermute | solution.py:76
  4.6 0.7 %collective-permute-start = (bf16[8,4096]{1,0:T(8,128)(2,1)S(1)}, bf16[8,4096]{1,0:T(8,128)(2,1)S(1)}, u32[]{:S(2)}, u32[]{:S(2)}) collective-permute-start(bf16[8,4096]{1,0:T(8,128)(2,1)S(1)} %get-tuple-element.17), channel_id=1, source_target_pairs={{0,64},{1,65},{2,66},{3,67},{4,68},{5,69},{6,70},{7,71},{8,72},{9,... | collective-permute-start | bytes 196616 | tf_op jit(solution)/shard_map/ppermute | solution.py:76
  5.3 1.3 %collective-permute-start.1 = (bf16[8,4096]{1,0:T(8,128)(2,1)S(1)}, bf16[8,4096]{1,0:T(8,128)(2,1)S(1)}, u32[]{:S(2)}, u32[]{:S(2)}) collective-permute-start(bf16[8,4096]{1,0:T(8,128)(2,1)S(1)} %get-tuple-element.16.keep), channel_id=1, source_target_pairs={{0,128},{1,129},{2,130},{3,131},{4,132},{5,133},{6,134},{7,135},{8... | collective-permute-start | bytes 196616 | tf_op jit(solution)/shard_map/ppermute | solution.py:76
  6.5 1.0 %broadcast_multiply_fusion.decayed = f32[8,8192]{1,0:T(8,128)S(1)} fusion(f32[8,8192]{1,0:T(8,128)} %param.5), kind=kLoop, calls=%fused_computation | loop fusion | flops 65536 | bytes 524288 | tf_op jit(solution)/shard_map/mul | solution.py:249
  7.5 2.3 %collective-permute-done.1.from_chip = bf16[8,4096]{1,0:T(8,128)(2,1)S(1)} collective-permute-done((bf16[8,4096]{1,0:T(8,128)(2,1)S(1)}, bf16[8,4096]{1,0:T(8,128)(2,1)S(1)}, u32[]{:S(2)}, u32[]{:S(2)}) %collective-permute-start.1) | collective-permute-done | bytes 65568 | tf_op jit(solution)/shard_map/ppermute | solution.py:76
  9.8 0.0 collective-permute-done.2.from_both
  9.9 0.0 collective-permute-done.from_core
  9.9 0.1 half_step.1
  9.9 0.5 collective-permute-start.3
  10.4 0.7 collective-permute-start.4
  11.1 0.3 collective-permute-done.3.theirs
  11.4 0.9 %whole_step.1 = (f32[8,8192]{1,0:T(8,128)}, f32[8,8192]{1,0:T(8,128)}, f32[8,128]{1,0:T(8,128)S(1)}) custom-call(f32[8,4096]{1,0:T(8,128)S(1)} %get-tuple-element.19.mine, f32[8,4096]{1,0:T(8,128)S(1)} %collective-permute-done.3.theirs, f32[8,8192]{1,0:T(8,128)S(1)} %get-tuple-element.18.base, f32[8,8192]{1,0:T(8,128)S(1)} %broadcast_multiply_fusion.decayed), custom_call_target="tpu_custom_call" | custom-call | flops 1048576 | bytes 1048576 | tf_op jit(solution)/shard_map/whole_step/pallas_call | solution.py:210
  12.3 1.3 %collective-permute-done.4.other = bf16[8,4096]{1,0:T(8,128)(2,1)S(1)} collective-permute-done((bf16[8,4096]{1,0:T(8,128)(2,1)S(1)}, bf16[8,4096]{1,0:T(8,128)(2,1)S(1)}, u32[]{:S(2)}, u32[]{:S(2)}) %collective-permute-start.4) | collective-permute-done | bytes 65568 | tf_op jit(solution)/shard_map/ppermute | solution.py:76
  13.6 2.3 %collective-permute-start.7 = (bf16[2,8,4096]{2,1,0:T(8,128)(2,1)S(1)}, bf16[2,8,4096]{2,1,0:T(8,128)(2,1)S(1)}, u32[]{:S(2)}, u32[]{:S(2)}) collective-permute-start(bf16[2,8,4096]{2,1,0:T(8,128)(2,1)S(1)} %couple.1.refs_0_), channel_id=1, source_target_pairs={{0,8},{1,9},{2,10},{3,11},{4,12},{5,13},{6,14},{7,15},{8,16},{9,17... | collective-permute-start | bytes 393224 | tf_op jit(solution)/shard_map/ppermute | solution.py:76
  15.9 2.9 %collective-permute-start.6 = (bf16[2,8,4096]{2,1,0:T(8,128)(2,1)S(1)}, bf16[2,8,4096]{2,1,0:T(8,128)(2,1)S(1)}, u32[]{:S(2)}, u32[]{:S(2)}) collective-permute-start(bf16[2,8,4096]{2,1,0:T(8,128)(2,1)S(1)} %couple.1.refs_0_), channel_id=1, source_target_pairs={{0,24},{1,25},{2,26},{3,27},{4,28},{5,29},{6,30},{7,31},{8,0},{9,1... | collective-permute-start | bytes 393224 | tf_op jit(solution)/shard_map/ppermute | solution.py:76
  18.8 4.4 %collective-permute-start.5 = (bf16[2,8,4096]{2,1,0:T(8,128)(2,1)S(1)}, bf16[2,8,4096]{2,1,0:T(8,128)(2,1)S(1)}, u32[]{:S(2)}, u32[]{:S(2)}) collective-permute-start(bf16[2,8,4096]{2,1,0:T(8,128)(2,1)S(1)} %couple.1.refs_0_), channel_id=1, source_target_pairs={{0,16},{1,17},{2,18},{3,19},{4,20},{5,21},{6,22},{7,23},{8,24},{9,... | collective-permute-start | bytes 393224 | tf_op jit(solution)/shard_map/ppermute | solution.py:76
  23.2 0.0 collective-permute-done.7.refs_3_
  23.2 0.5 collective-permute-done.6.refs_2_
  23.6 3.0 %collective-permute-done.5.refs_1_ = bf16[2,8,4096]{2,1,0:T(8,128)(2,1)S(1)} collective-permute-done((bf16[2,8,4096]{2,1,0:T(8,128)(2,1)S(1)}, bf16[2,8,4096]{2,1,0:T(8,128)(2,1)S(1)}, u32[]{:S(2)}, u32[]{:S(2)}) %collective-permute-start.5) | collective-permute-done | bytes 131104 | tf_op jit(solution)/shard_map/ppermute | solution.py:76
  26.6 0.1 bundle.1.refs_0_
  26.7 1.4 %collective-permute-start.12 = (bf16[8,8,4096]{2,1,0:T(8,128)(2,1)S(1)}, bf16[8,8,4096]{2,1,0:T(8,128)(2,1)S(1)}, u32[]{:S(2)}, u32[]{:S(2)}) collective-permute-start(bf16[8,8,4096]{2,1,0:T(8,128)(2,1)S(1)} %bundle.1.refs_0_), channel_id=1, source_target_pairs={{0,1},{1,2},{2,3},{3,4},{4,5},{5,6},{6,7},{7,0},{8,9},{9,10},{10,1... | collective-permute-start | bytes 1572872 | tf_op jit(solution)/shard_map/ppermute | solution.py:76
  28.1 1.4 %collective-permute-start.8 = (bf16[8,8,4096]{2,1,0:T(8,128)(2,1)S(1)}, bf16[8,8,4096]{2,1,0:T(8,128)(2,1)S(1)}, u32[]{:S(2)}, u32[]{:S(2)}) collective-permute-start(bf16[8,8,4096]{2,1,0:T(8,128)(2,1)S(1)} %bundle.1.refs_0_), channel_id=1, source_target_pairs={{0,7},{1,0},{2,1},{3,2},{4,3},{5,4},{6,5},{7,6},{8,15},{9,8},{10,9... | collective-permute-start | bytes 1572872 | tf_op jit(solution)/shard_map/ppermute | solution.py:76
  29.4 6.9 %collective-permute-done.12.refs_2_ = bf16[8,8,4096]{2,1,0:T(8,128)(2,1)S(1)} collective-permute-done((bf16[8,8,4096]{2,1,0:T(8,128)(2,1)S(1)}, bf16[8,8,4096]{2,1,0:T(8,128)(2,1)S(1)}, u32[]{:S(2)}, u32[]{:S(2)}) %collective-permute-start.12) | collective-permute-done | bytes 524320 | tf_op jit(solution)/shard_map/ppermute | solution.py:76
  36.3 0.1 collective-permute-start.13
  36.4 0.0 collective-permute-done.8.refs_1_
  36.4 2.6 %collective-permute-start.9 = (bf16[8,8,4096]{2,1,0:T(8,128)(2,1)S(1)}, bf16[8,8,4096]{2,1,0:T(8,128)(2,1)S(1)}, u32[]{:S(2)}, u32[]{:S(2)}) collective-permute-start(bf16[8,8,4096]{2,1,0:T(8,128)(2,1)S(1)} %collective-permute-done.8.refs_1_), channel_id=1, source_target_pairs={{0,7},{1,0},{2,1},{3,2},{4,3},{5,4},{6,5},{7,6},{8,15},{9,8},{10,9... | collective-permute-start | bytes 1572872 | tf_op jit(solution)/shard_map/ppermute | solution.py:76
  39.0 6.9 %collective-permute-done.13.refs_1_ = bf16[8,8,4096]{2,1,0:T(8,128)(2,1)S(1)} collective-permute-done((bf16[8,8,4096]{2,1,0:T(8,128)(2,1)S(1)}, bf16[8,8,4096]{2,1,0:T(8,128)(2,1)S(1)}, u32[]{:S(2)}, u32[]{:S(2)}) %collective-permute-start.13) | collective-permute-done | bytes 524320 | tf_op jit(solution)/shard_map/ppermute | solution.py:76
  45.8 0.0 collective-permute-start.14
  45.9 0.0 collective-permute-done.9.refs_0_
  45.9 2.7 %collective-permute-start.10 = (bf16[8,8,4096]{2,1,0:T(8,128)(2,1)S(1)}, bf16[8,8,4096]{2,1,0:T(8,128)(2,1)S(1)}, u32[]{:S(2)}, u32[]{:S(2)}) collective-permute-start(bf16[8,8,4096]{2,1,0:T(8,128)(2,1)S(1)} %collective-permute-done.9.refs_0_), channel_id=1, source_target_pairs={{0,7},{1,0},{2,1},{3,2},{4,3},{5,4},{6,5},{7,6},{8,15},{9,8},{10,9... | collective-permute-start | bytes 1572872 | tf_op jit(solution)/shard_map/ppermute | solution.py:76
  48.5 0.1 pack.2.refs_0_
  48.6 1.2 %assemble.5 = (bf16[8,8,8,8192]{3,2,1,0:T(8,128)(2,1)}, f32[8,128]{1,0:T(8,128)S(1)}) custom-call(bf16[3,8,8,4096]{3,2,1,0:T(8,128)(2,1)S(1)} %pack.2.refs_0_), custom_call_target="tpu_custom_call" | custom-call | flops 3145728 | bytes 3145728 | tf_op jit(solution)/shard_map/assemble/pallas_call | solution.py:230
  49.8 5.5 %collective-permute-done.14.bundle.refs_3_ = bf16[8,8,4096]{2,1,0:T(8,128)(2,1)S(1)} collective-permute-done((bf16[8,8,4096]{2,1,0:T(8,128)(2,1)S(1)}, bf16[8,8,4096]{2,1,0:T(8,128)(2,1)S(1)}, u32[]{:S(2)}, u32[]{:S(2)}) %collective-permute-start.14) | collective-permute-done | bytes 524320 | tf_op jit(solution)/shard_map/ppermute | solution.py:76
  55.4 0.0 collective-permute-done.10.bundle.refs_2_
  55.4 0.1 pack.3.refs_0_
  55.5 3.5 %collective-permute-start.16 = (bf16[4,8,8,4096]{3,2,1,0:T(8,128)(2,1)S(1)}, bf16[4,8,8,4096]{3,2,1,0:T(8,128)(2,1)S(1)}, u32[]{:S(2)}, u32[]{:S(2)}) collective-permute-start(bf16[4,8,8,4096]{3,2,1,0:T(8,128)(2,1)S(1)} %pack.3.refs_0_), channel_id=1, source_target_pairs={{0,64},{1,65},{2,66},{3,67},{4,68},{5,69},{6,70},{7,71},{8,72},{9,... | collective-permute-start | bytes 6291464 | tf_op jit(solution)/shard_map/ppermute | solution.py:76
  59.0 0.1 collective-permute-start.17
  59.2 2.5 %collective-permute-start.11 = (bf16[5,8,4096]{2,1,0:T(8,128)(2,1)S(1)}, bf16[5,8,4096]{2,1,0:T(8,128)(2,1)S(1)}, u32[]{:S(2)}, u32[]{:S(2)}) collective-permute-start(bf16[5,8,4096]{2,1,0:T(8,128)(2,1)S(1)} %cut.2), channel_id=1, source_target_pairs={{0,7},{1,0},{2,1},{3,2},{4,3},{5,4},{6,5},{7,6},{8,15},{9,8},{10,9... | collective-permute-start | bytes 983048 | tf_op jit(solution)/shard_map/ppermute | solution.py:76
  61.7 0.1 collective-permute-start.15
  61.7 3.3 %collective-permute-done.17.refs_1_ = bf16[3,8,8,4096]{3,2,1,0:T(8,128)(2,1)S(1)} collective-permute-done((bf16[3,8,8,4096]{3,2,1,0:T(8,128)(2,1)S(1)}, bf16[3,8,8,4096]{3,2,1,0:T(8,128)(2,1)S(1)}, u32[]{:S(2)}, u32[]{:S(2)}) %collective-permute-start.17) | collective-permute-done | bytes 1572896 | tf_op jit(solution)/shard_map/ppermute | solution.py:76
  65.1 2.5 %assemble.6 = (bf16[8,8,8,8192]{3,2,1,0:T(8,128)(2,1)}, f32[8,128]{1,0:T(8,128)}) custom-call(bf16[4,8,8,4096]{3,2,1,0:T(8,128)(2,1)S(1)} %pack.3.refs_0_, bf16[3,8,8,4096]{3,2,1,0:T(8,128)(2,1)S(1)} %collective-permute-done.17.refs_1_, bf16[8,8,8,8192]{3,2,1,0:T(8,128)(2,1)} %get-tuple-element.25.refs_2_), custom_call_target="tpu_custom_call", output_to_operand_aliasing={{0}: (2, {})} | custom-call | flops 7340032 | bytes 7340032 | tf_op jit(solution)/shard_map/assemble/pallas_call | solution.py:230
  67.5 0.0 collective-permute-done.16.refs_0_
  67.6 1.4 %assemble.7 = (bf16[8,8,8,8192]{3,2,1,0:T(8,128)(2,1)}, f32[8,128]{1,0:T(8,128)S(1)}) custom-call(bf16[4,8,8,4096]{3,2,1,0:T(8,128)(2,1)S(1)} %collective-permute-done.16.refs_0_, bf16[8,8,8,8192]{3,2,1,0:T(8,128)(2,1)} %get-tuple-element.26.refs_1_), custom_call_target="tpu_custom_call", output_to_operand_aliasing={{0}: (1, {})} | custom-call | flops 4194304 | bytes 4194304 | tf_op jit(solution)/shard_map/assemble/pallas_call | solution.py:230
  69.0 0.0 collective-permute-done.15.high
  69.0 0.0 collective-permute-done.11.low
  69.0 1.0 %collective-permute-start.18 = (bf16[8,8,4096]{2,1,0:T(8,128)(2,1)S(1)}, bf16[8,8,4096]{2,1,0:T(8,128)(2,1)S(1)}, u32[]{:S(2)}, u32[]{:S(2)}) collective-permute-start(bf16[8,8,4096]{2,1,0:T(8,128)(2,1)S(1)} %last.1.refs_0_), channel_id=1, source_target_pairs={{0,64},{1,65},{2,66},{3,67},{4,68},{5,69},{6,70},{7,71},{8,72},{9,... | collective-permute-start | bytes 1572872 | tf_op jit(solution)/shard_map/ppermute | solution.py:76
  70.1 0.8 %assemble.8.refs_1_ = bf16[8,8,8,8192]{3,2,1,0:T(8,128)(2,1)} custom-call(bf16[8,8,4096]{2,1,0:T(8,128)(2,1)S(1)} %last.1.refs_0_, bf16[8,8,8,8192]{3,2,1,0:T(8,128)(2,1)} %get-tuple-element.28.refs_1_), custom_call_target="tpu_custom_call", output_to_operand_aliasing={{}: (1, {})} | custom-call | flops 1048576 | bytes 1048576 | tf_op jit(solution)/shard_map/assemble/pallas_call | solution.py:230
  70.9 0.7 %collective-permute-done.18.refs_0_ = bf16[8,8,4096]{2,1,0:T(8,128)(2,1)S(1)} collective-permute-done((bf16[8,8,4096]{2,1,0:T(8,128)(2,1)S(1)}, bf16[8,8,4096]{2,1,0:T(8,128)(2,1)S(1)}, u32[]{:S(2)}, u32[]{:S(2)}) %collective-permute-start.18) | collective-permute-done | bytes 524320 | tf_op jit(solution)/shard_map/ppermute | solution.py:76
  71.6 0.8 %assemble.9 = bf16[8,8,8,8192]{3,2,1,0:T(8,128)(2,1)} custom-call(bf16[8,8,4096]{2,1,0:T(8,128)(2,1)S(1)} %collective-permute-done.18.refs_0_, bf16[8,8,8,8192]{3,2,1,0:T(8,128)(2,1)} %assemble.8.refs_1_), custom_call_target="tpu_custom_call", output_to_operand_aliasing={{}: (1, {})} | custom-call | flops 1048576 | bytes 1048576 | tf_op jit(solution)/shard_map/assemble/pallas_call | solution.py:230
  (4 shorter events, 0.1 us)
Async XLA Ops:
  1.9 8.0 %collective-permute-start.2 = (bf16[8,4096]{1,0:T(8,128)(2,1)S(1)}, bf16[8,4096]{1,0:T(8,128)(2,1)S(1)}, u32[]{:S(2)}, u32[]{:S(2)}) collective-permute-start(bf16[8,4096]{1,0:T(8,128)(2,1)S(1)} %get-tuple-element.17), channel_id=1, source_target_pairs={{0,192},{1,193},{2,194},{3,195},{4,196},{5,197},{6,198},{7,199},{8... | collective-permute-start | bytes 196616 | tf_op jit(solution)/shard_map/ppermute | solution.py:76
  4.6 5.3 %collective-permute-start = (bf16[8,4096]{1,0:T(8,128)(2,1)S(1)}, bf16[8,4096]{1,0:T(8,128)(2,1)S(1)}, u32[]{:S(2)}, u32[]{:S(2)}) collective-permute-start(bf16[8,4096]{1,0:T(8,128)(2,1)S(1)} %get-tuple-element.17), channel_id=1, source_target_pairs={{0,64},{1,65},{2,66},{3,67},{4,68},{5,69},{6,70},{7,71},{8,72},{9,... | collective-permute-start | bytes 196616 | tf_op jit(solution)/shard_map/ppermute | solution.py:76
  5.3 4.6 %collective-permute-start.1 = (bf16[8,4096]{1,0:T(8,128)(2,1)S(1)}, bf16[8,4096]{1,0:T(8,128)(2,1)S(1)}, u32[]{:S(2)}, u32[]{:S(2)}) collective-permute-start(bf16[8,4096]{1,0:T(8,128)(2,1)S(1)} %get-tuple-element.16.keep), channel_id=1, source_target_pairs={{0,128},{1,129},{2,130},{3,131},{4,132},{5,133},{6,134},{7,135},{8... | collective-permute-start | bytes 196616 | tf_op jit(solution)/shard_map/ppermute | solution.py:76
  9.9 1.5 %collective-permute-start.3 = (f32[8,4096]{1,0:T(8,128)S(1)}, f32[8,4096]{1,0:T(8,128)S(1)}, u32[]{:S(2)}, u32[]{:S(2)}) collective-permute-start(f32[8,4096]{1,0:T(8,128)S(1)} %get-tuple-element.19.mine), channel_id=1, source_target_pairs={{0,64},{1,65},{2,66},{3,67},{4,68},{5,69},{6,70},{7,71},{8,72},{9,... | collective-permute-start | bytes 393224 | tf_op jit(solution)/shard_map/ppermute | solution.py:76
  10.4 3.1 %collective-permute-start.4 = (bf16[8,4096]{1,0:T(8,128)(2,1)S(1)}, bf16[8,4096]{1,0:T(8,128)(2,1)S(1)}, u32[]{:S(2)}, u32[]{:S(2)}) collective-permute-start(bf16[8,4096]{1,0:T(8,128)(2,1)S(1)} %get-tuple-element.22.own), channel_id=1, source_target_pairs={{0,160},{1,161},{2,162},{3,163},{4,164},{5,165},{6,166},{7,167},{8... | collective-permute-start | bytes 196616 | tf_op jit(solution)/shard_map/ppermute | solution.py:76
  13.6 9.6 %collective-permute-start.7 = (bf16[2,8,4096]{2,1,0:T(8,128)(2,1)S(1)}, bf16[2,8,4096]{2,1,0:T(8,128)(2,1)S(1)}, u32[]{:S(2)}, u32[]{:S(2)}) collective-permute-start(bf16[2,8,4096]{2,1,0:T(8,128)(2,1)S(1)} %couple.1.refs_0_), channel_id=1, source_target_pairs={{0,8},{1,9},{2,10},{3,11},{4,12},{5,13},{6,14},{7,15},{8,16},{9,17... | collective-permute-start | bytes 393224 | tf_op jit(solution)/shard_map/ppermute | solution.py:76
  15.9 7.8 %collective-permute-start.6 = (bf16[2,8,4096]{2,1,0:T(8,128)(2,1)S(1)}, bf16[2,8,4096]{2,1,0:T(8,128)(2,1)S(1)}, u32[]{:S(2)}, u32[]{:S(2)}) collective-permute-start(bf16[2,8,4096]{2,1,0:T(8,128)(2,1)S(1)} %couple.1.refs_0_), channel_id=1, source_target_pairs={{0,24},{1,25},{2,26},{3,27},{4,28},{5,29},{6,30},{7,31},{8,0},{9,1... | collective-permute-start | bytes 393224 | tf_op jit(solution)/shard_map/ppermute | solution.py:76
  18.8 7.8 %collective-permute-start.5 = (bf16[2,8,4096]{2,1,0:T(8,128)(2,1)S(1)}, bf16[2,8,4096]{2,1,0:T(8,128)(2,1)S(1)}, u32[]{:S(2)}, u32[]{:S(2)}) collective-permute-start(bf16[2,8,4096]{2,1,0:T(8,128)(2,1)S(1)} %couple.1.refs_0_), channel_id=1, source_target_pairs={{0,16},{1,17},{2,18},{3,19},{4,20},{5,21},{6,22},{7,23},{8,24},{9,... | collective-permute-start | bytes 393224 | tf_op jit(solution)/shard_map/ppermute | solution.py:76
  26.7 9.6 %collective-permute-start.12 = (bf16[8,8,4096]{2,1,0:T(8,128)(2,1)S(1)}, bf16[8,8,4096]{2,1,0:T(8,128)(2,1)S(1)}, u32[]{:S(2)}, u32[]{:S(2)}) collective-permute-start(bf16[8,8,4096]{2,1,0:T(8,128)(2,1)S(1)} %bundle.1.refs_0_), channel_id=1, source_target_pairs={{0,1},{1,2},{2,3},{3,4},{4,5},{5,6},{6,7},{7,0},{8,9},{9,10},{10,1... | collective-permute-start | bytes 1572872 | tf_op jit(solution)/shard_map/ppermute | solution.py:76
  28.1 8.3 %collective-permute-start.8 = (bf16[8,8,4096]{2,1,0:T(8,128)(2,1)S(1)}, bf16[8,8,4096]{2,1,0:T(8,128)(2,1)S(1)}, u32[]{:S(2)}, u32[]{:S(2)}) collective-permute-start(bf16[8,8,4096]{2,1,0:T(8,128)(2,1)S(1)} %bundle.1.refs_0_), channel_id=1, source_target_pairs={{0,7},{1,0},{2,1},{3,2},{4,3},{5,4},{6,5},{7,6},{8,15},{9,8},{10,9... | collective-permute-start | bytes 1572872 | tf_op jit(solution)/shard_map/ppermute | solution.py:76
  36.3 9.5 %collective-permute-start.13 = (bf16[8,8,4096]{2,1,0:T(8,128)(2,1)S(1)}, bf16[8,8,4096]{2,1,0:T(8,128)(2,1)S(1)}, u32[]{:S(2)}, u32[]{:S(2)}) collective-permute-start(bf16[8,8,4096]{2,1,0:T(8,128)(2,1)S(1)} %collective-permute-done.12.refs_2_), channel_id=1, source_target_pairs={{0,1},{1,2},{2,3},{3,4},{4,5},{5,6},{6,7},{7,0},{8,9},{9,10},{10,1... | collective-permute-start | bytes 1572872 | tf_op jit(solution)/shard_map/ppermute | solution.py:76
  36.4 9.5 %collective-permute-start.9 = (bf16[8,8,4096]{2,1,0:T(8,128)(2,1)S(1)}, bf16[8,8,4096]{2,1,0:T(8,128)(2,1)S(1)}, u32[]{:S(2)}, u32[]{:S(2)}) collective-permute-start(bf16[8,8,4096]{2,1,0:T(8,128)(2,1)S(1)} %collective-permute-done.8.refs_1_), channel_id=1, source_target_pairs={{0,7},{1,0},{2,1},{3,2},{4,3},{5,4},{6,5},{7,6},{8,15},{9,8},{10,9... | collective-permute-start | bytes 1572872 | tf_op jit(solution)/shard_map/ppermute | solution.py:76
  45.8 9.5 %collective-permute-start.14 = (bf16[8,8,4096]{2,1,0:T(8,128)(2,1)S(1)}, bf16[8,8,4096]{2,1,0:T(8,128)(2,1)S(1)}, u32[]{:S(2)}, u32[]{:S(2)}) collective-permute-start(bf16[8,8,4096]{2,1,0:T(8,128)(2,1)S(1)} %collective-permute-done.13.refs_1_), channel_id=1, source_target_pairs={{0,1},{1,2},{2,3},{3,4},{4,5},{5,6},{6,7},{7,0},{8,9},{9,10},{10,1... | collective-permute-start | bytes 1572872 | tf_op jit(solution)/shard_map/ppermute | solution.py:76
  45.9 9.5 %collective-permute-start.10 = (bf16[8,8,4096]{2,1,0:T(8,128)(2,1)S(1)}, bf16[8,8,4096]{2,1,0:T(8,128)(2,1)S(1)}, u32[]{:S(2)}, u32[]{:S(2)}) collective-permute-start(bf16[8,8,4096]{2,1,0:T(8,128)(2,1)S(1)} %collective-permute-done.9.refs_0_), channel_id=1, source_target_pairs={{0,7},{1,0},{2,1},{3,2},{4,3},{5,4},{6,5},{7,6},{8,15},{9,8},{10,9... | collective-permute-start | bytes 1572872 | tf_op jit(solution)/shard_map/ppermute | solution.py:76
  55.5 12.0 %collective-permute-start.16 = (bf16[4,8,8,4096]{3,2,1,0:T(8,128)(2,1)S(1)}, bf16[4,8,8,4096]{3,2,1,0:T(8,128)(2,1)S(1)}, u32[]{:S(2)}, u32[]{:S(2)}) collective-permute-start(bf16[4,8,8,4096]{3,2,1,0:T(8,128)(2,1)S(1)} %pack.3.refs_0_), channel_id=1, source_target_pairs={{0,64},{1,65},{2,66},{3,67},{4,68},{5,69},{6,70},{7,71},{8,72},{9,... | collective-permute-start | bytes 6291464 | tf_op jit(solution)/shard_map/ppermute | solution.py:76
  59.0 6.0 %collective-permute-start.17 = (bf16[3,8,8,4096]{3,2,1,0:T(8,128)(2,1)S(1)}, bf16[3,8,8,4096]{3,2,1,0:T(8,128)(2,1)S(1)}, u32[]{:S(2)}, u32[]{:S(2)}) collective-permute-start(bf16[3,8,8,4096]{3,2,1,0:T(8,128)(2,1)S(1)} %pack.2.refs_0_), channel_id=1, source_target_pairs={{0,64},{1,65},{2,66},{3,67},{4,68},{5,69},{6,70},{7,71},{8,72},{9,... | collective-permute-start | bytes 4718600 | tf_op jit(solution)/shard_map/ppermute | solution.py:76
  59.2 9.8 %collective-permute-start.11 = (bf16[5,8,4096]{2,1,0:T(8,128)(2,1)S(1)}, bf16[5,8,4096]{2,1,0:T(8,128)(2,1)S(1)}, u32[]{:S(2)}, u32[]{:S(2)}) collective-permute-start(bf16[5,8,4096]{2,1,0:T(8,128)(2,1)S(1)} %cut.2), channel_id=1, source_target_pairs={{0,7},{1,0},{2,1},{3,2},{4,3},{5,4},{6,5},{7,6},{8,15},{9,8},{10,9... | collective-permute-start | bytes 983048 | tf_op jit(solution)/shard_map/ppermute | solution.py:76
  61.7 7.3 %collective-permute-start.15 = (bf16[3,8,4096]{2,1,0:T(8,128)(2,1)S(1)}, bf16[3,8,4096]{2,1,0:T(8,128)(2,1)S(1)}, u32[]{:S(2)}, u32[]{:S(2)}) collective-permute-start(bf16[3,8,4096]{2,1,0:T(8,128)(2,1)S(1)} %cut.3), channel_id=1, source_target_pairs={{0,1},{1,2},{2,3},{3,4},{4,5},{5,6},{6,7},{7,0},{8,9},{9,10},{10,1... | collective-permute-start | bytes 589832 | tf_op jit(solution)/shard_map/ppermute | solution.py:76
  69.0 2.6 %collective-permute-start.18 = (bf16[8,8,4096]{2,1,0:T(8,128)(2,1)S(1)}, bf16[8,8,4096]{2,1,0:T(8,128)(2,1)S(1)}, u32[]{:S(2)}, u32[]{:S(2)}) collective-permute-start(bf16[8,8,4096]{2,1,0:T(8,128)(2,1)S(1)} %last.1.refs_0_), channel_id=1, source_target_pairs={{0,64},{1,65},{2,66},{3,67},{4,68},{5,69},{6,70},{7,71},{8,72},{9,... | collective-permute-start | bytes 1572872 | tf_op jit(solution)/shard_map/ppermute | solution.py:76
